TPU v7x, 32 devices: a whole 2x2x4 slice. The times are simulated.
32 devices in a mesh: dp: 4 (over y, x), blk: 8 (over z, core).
Axes of the slice: x: 2, y: 2, z: 4, core: 2. Of those that a mesh axis runs over, the one named last changes fastest.
Arguments:
- tokens: bfloat16 [16, 512, 1024], P('dp', 'blk'), may hold values from -6 to 6
- first_values: bfloat16 [16, 512, 1024], P('dp', 'blk'), may hold values from -6 to 6
- docs: int32 [16, 512], P('dp', 'blk'), may hold values from 0 to 3, never falling along the last dimension, each value on 1 to 384 neighbouring positions
- cotangent: bfloat16 [16, 512, 1024], P('dp', 'blk'), may hold values from -6 to 6
- w_qkv: bfloat16 [1024, 3072], replicated, may hold values from -0.1875 to 0.1875
- w_out: bfloat16 [1024, 1024], replicated, may hold values from -3 to 3
- w_gate: bfloat16 [1024, 2816], replicated, may hold values from -0.1875 to 0.1875
- w_up: bfloat16 [1024, 2816], replicated, may hold values from -0.1875 to 0.1875
- w_down: bfloat16 [2816, 1024], replicated, may hold values from -0.109375 to 0.109375
- gain_attn: float32 [1024], replicated, may hold values from 0.5 to 1.5
- gain_ffn: float32 [1024], replicated, may hold values from 0.5 to 1.5
Outputs:
- output: bfloat16 [16, 512, 1024], P('dp', 'blk')
- grad_tokens: bfloat16 [16, 512, 1024], P('dp', 'blk')
- grad_first_values: bfloat16 [16, 512, 1024], P('dp', 'blk')
- grad_qkv: float32 [1024, 3072], P(('dp', 'blk'))
- grad_out: float32 [1024, 1024], P(('dp', 'blk'))
- grad_gate: float32 [1024, 2816], P(('dp', 'blk'))
- grad_up: float32 [1024, 2816], P(('dp', 'blk'))
- grad_down: float32 [2816, 1024], P(('dp', 'blk'))
- grad_gain_attn: float32 [1024], P(('dp', 'blk'))
- grad_gain_ffn: float32 [1024], P(('dp', 'blk'))
Inputs may be any that keep to these rules, and one draw needn't show every extreme that they name: `docs`: along each sequence the document ids never fall, begin at 0 and take every value up to 3; each document has 1 to 384 positions.
All inputs are finite; a program needn't handle non-finite values.
Results may differ from a plain program's by a relative error of at most 0.023.
Values may be sent and summed in bfloat16 or wider, within the bound.
No kernel may reach another device: no remote copies, remote signals or barrier semaphores. Data moves between devices by JAX's collectives and lax.ppermute only.
A program may use at most 320 MiB of HBM per device.

v0:
```python
import math

import jax
import jax.numpy as jnp
from jax import lax
from jax.sharding import PartitionSpec as P

HEADS = 16
HEAD_DIM = 64


epsilon = 1e-06
score_scale = 0.125


def norm_scale(values):
    return lax.rsqrt(jnp.mean(values * values, axis=-1, keepdims=True) + epsilon)


def norm_back(grad_normed, values, factor, gain_vector):
    scaled = grad_normed * gain_vector
    grad_gain = jnp.sum(grad_normed * values * factor, axis=0)
    grad_values = factor * (
        scaled - values * factor * factor * jnp.mean(scaled * values, axis=-1, keepdims=True)
    )
    return (grad_values, grad_gain)


def rope_tables(positions, half_dim):
    inverse = 10000.0 ** (-jnp.arange(half_dim, dtype=jnp.float32) / half_dim)
    angles = positions.astype(jnp.float32)[:, None] * inverse[None, :]
    angles = jnp.concatenate([angles, angles], axis=-1)
    return (jnp.cos(angles), jnp.sin(angles))


def rotate(values, cosine, sines):
    half_dim = values.shape[-1] // 2
    turned = jnp.concatenate([-values[..., half_dim:], values[..., :half_dim]], axis=-1)
    return values * cosine + turned * sines


def unrotate(grad_values, cosine, sines):
    half_dim = grad_values.shape[-1] // 2
    turned = grad_values * sines
    return grad_values * cosine + jnp.concatenate(
        [turned[..., half_dim:], -turned[..., :half_dim]], axis=-1
    )


def by_rows(left_side, right_side):
    return lax.dot_general(
        left_side, right_side, (((0,), (0,)), ((), ())), preferred_element_type=jnp.float32
    )


def by_transpose(left_side, right_side):
    return lax.dot_general(
        left_side, right_side, (((1,), (1,)), ((), ())), preferred_element_type=jnp.float32
    )


def block_split(length):
    block_size = math.gcd(length, 512)
    return (block_size, length // block_size)


def masked_scores(queries, key_block, doc_query, doc_block, query_pos, key_pos):
    raw_scores = (
        jnp.einsum("rshd,rnhd->rhsn", queries, key_block, preferred_element_type=jnp.float32)
        * score_scale
    )
    allowed = (key_pos[None, None, None, :] <= query_pos[None, None, :, None]) & (
        doc_block[:, None, None, :] == doc_query[:, None, :, None]
    )
    return (jnp.where(allowed, raw_scores, -1e30), allowed)


def key_slices(keys_rot, mixed_values, doc_keys, offset, block_size):
    seq_rows = doc_keys.shape[0]
    key_block = lax.dynamic_slice_in_dim(keys_rot, offset, block_size, 1).reshape(
        seq_rows, block_size, HEADS, HEAD_DIM
    )
    value_block = lax.dynamic_slice_in_dim(mixed_values, offset, block_size, 1).reshape(
        seq_rows, block_size, HEADS, HEAD_DIM
    )
    doc_block = lax.dynamic_slice_in_dim(doc_keys, offset, block_size, 1)
    return (key_block, value_block, doc_block)


def fold_keys(carried, received, queries, doc_query, query_pos):
    keys_rot, mixed_values, doc_keys = received
    block_size, block_total = block_split(doc_keys.shape[1])

    def fold_one_step(block_index, loop_state):
        summed, running_top, running_sum = loop_state
        offset = block_index * block_size
        key_block, value_block, doc_block = key_slices(
            keys_rot, mixed_values, doc_keys, offset, block_size
        )
        key_pos = offset + jnp.arange(block_size, dtype=jnp.int32)
        scores, allowed = masked_scores(
            queries, key_block, doc_query, doc_block, query_pos, key_pos
        )
        new_top = jnp.maximum(running_top, jnp.max(scores, axis=-1))
        weights = jnp.where(allowed, jnp.exp(scores - new_top[..., None]), 0.0)
        factor = jnp.exp(running_top - new_top)
        running_sum = running_sum * factor + jnp.sum(weights, axis=-1)
        summed = summed * factor[..., None] + jnp.einsum(
            "rhsn,rnhd->rhsd",
            weights.astype(jnp.bfloat16),
            value_block,
            preferred_element_type=jnp.float32,
        )
        return (summed, new_top, running_sum)

    return lax.fori_loop(0, block_total, fold_one_step, carried)


def attend_back(
    queries,
    grad_attended,
    row_delta,
    log_total,
    keys_all,
    mixed_all,
    docs_all,
    doc_query,
    query_pos,
):
    seq_rows, length, model_width = keys_all.shape
    block_size, block_total = block_split(length)

    def attend_one_step(block_index, loop_state):
        offset = block_index * block_size
        key_block, value_block, doc_block = key_slices(
            keys_all, mixed_all, docs_all, offset, block_size
        )
        key_pos = offset + jnp.arange(block_size, dtype=jnp.int32)
        scores, allowed = masked_scores(
            queries, key_block, doc_query, doc_block, query_pos, key_pos
        )
        probs = jnp.exp(scores - log_total[..., None])
        grad_probs = jnp.einsum(
            "rshd,rnhd->rhsn", grad_attended, value_block, preferred_element_type=jnp.float32
        )
        grad_scores = (probs * (grad_probs - row_delta[..., None])).astype(jnp.bfloat16)
        grad_query = (
            loop_state[0]
            + jnp.einsum(
                "rhsn,rnhd->rshd", grad_scores, key_block, preferred_element_type=jnp.float32
            )
            * score_scale
        )
        grad_value_block = jnp.einsum(
            "rhsn,rshd->rnhd",
            probs.astype(jnp.bfloat16),
            grad_attended,
            preferred_element_type=jnp.float32,
        )
        grad_key_block = (
            jnp.einsum("rhsn,rshd->rnhd", grad_scores, queries, preferred_element_type=jnp.float32)
            * score_scale
        )
        grad_keys_all = lax.dynamic_update_slice_in_dim(
            loop_state[1], grad_key_block.reshape(seq_rows, block_size, model_width), offset, 1
        )
        grad_mixed_all = lax.dynamic_update_slice_in_dim(
            loop_state[2], grad_value_block.reshape(seq_rows, block_size, model_width), offset, 1
        )
        return (grad_query, grad_keys_all, grad_mixed_all)

    start_state = (
        jnp.zeros(queries.shape, jnp.float32),
        jnp.zeros((seq_rows, length, model_width), jnp.float32),
        jnp.zeros((seq_rows, length, model_width), jnp.float32),
    )
    return lax.fori_loop(0, block_total, attend_one_step, start_state)


def shards(
    tokens, first_values, docs, cotangent, w_qkv, w_out, w_gate, w_up, w_down, gain_attn, gain_ffn
):
    seq_rows, shard_length, model_width = tokens.shape
    count_tokens = seq_rows * shard_length
    head_shape = (seq_rows, shard_length, HEADS, HEAD_DIM)
    inputs = tokens.astype(jnp.float32).reshape(count_tokens, model_width)
    factor_attn = norm_scale(inputs)
    normed = (inputs * factor_attn * gain_attn).astype(jnp.bfloat16)
    projected = jnp.dot(normed, w_qkv, preferred_element_type=jnp.float32)
    query_pos = lax.axis_index("blk") * shard_length + jnp.arange(shard_length, dtype=jnp.int32)
    cosine, sines = rope_tables(query_pos, HEAD_DIM // 2)
    cosine = cosine[None, :, None, :]
    sines = sines[None, :, None, :]
    queries = rotate(projected[:, :model_width].reshape(head_shape), cosine, sines).astype(
        jnp.bfloat16
    )
    keys_rot = (
        rotate(projected[:, model_width : 2 * model_width].reshape(head_shape), cosine, sines)
        .astype(jnp.bfloat16)
        .reshape(seq_rows, shard_length, model_width)
    )
    first_rows = first_values.astype(jnp.float32).reshape(count_tokens, model_width)
    mixed_values = (
        (0.5 * projected[:, 2 * model_width :] + 0.5 * first_rows)
        .astype(jnp.bfloat16)
        .reshape(seq_rows, shard_length, model_width)
    )
    start_state = (
        jnp.zeros((seq_rows, HEADS, shard_length, HEAD_DIM), jnp.float32),
        jnp.full((seq_rows, HEADS, shard_length), -1e30, jnp.float32),
        jnp.zeros((seq_rows, HEADS, shard_length), jnp.float32),
    )
    summed, running_top, running_sum = fold_keys(
        start_state,
        (
            lax.all_gather(keys_rot, "blk", axis=1, tiled=True),
            lax.all_gather(mixed_values, "blk", axis=1, tiled=True),
            lax.all_gather(docs, "blk", axis=1, tiled=True),
        ),
        queries,
        docs,
        query_pos,
    )
    log_total = running_top + jnp.log(running_sum)
    attended = jnp.transpose(summed / running_sum[..., None], (0, 2, 1, 3))
    attended_low = attended.astype(jnp.bfloat16).reshape(count_tokens, model_width)
    middle = inputs + jnp.dot(attended_low, w_out, preferred_element_type=jnp.float32)
    factor_ffn = norm_scale(middle)
    normed_ffn = (middle * factor_ffn * gain_ffn).astype(jnp.bfloat16)
    gate = jnp.dot(normed_ffn, w_gate, preferred_element_type=jnp.float32)
    upward = jnp.dot(normed_ffn, w_up, preferred_element_type=jnp.float32)
    sigmoid_gate = jax.nn.sigmoid(gate)
    hidden = (gate * sigmoid_gate * upward).astype(jnp.bfloat16)
    output = (
        (middle + jnp.dot(hidden, w_down, preferred_element_type=jnp.float32))
        .astype(jnp.bfloat16)
        .reshape(tokens.shape)
    )
    grad_rows = cotangent.reshape(count_tokens, model_width)
    grad_down = by_rows(hidden, grad_rows)
    grad_hidden = by_transpose(grad_rows, w_down)
    grad_gate_act = (
        grad_hidden * upward * sigmoid_gate * (1.0 + gate * (1.0 - sigmoid_gate))
    ).astype(jnp.bfloat16)
    grad_up_act = (grad_hidden * gate * sigmoid_gate).astype(jnp.bfloat16)
    grad_gate = by_rows(normed_ffn, grad_gate_act)
    grad_up = by_rows(normed_ffn, grad_up_act)
    grad_normed_ffn = by_transpose(grad_gate_act, w_gate) + by_transpose(grad_up_act, w_up)
    grad_middle, grad_gain_ffn = norm_back(grad_normed_ffn, middle, factor_ffn, gain_ffn)
    grad_middle = grad_middle + grad_rows.astype(jnp.float32)
    grad_branch = grad_middle.astype(jnp.bfloat16)
    grad_out = by_rows(attended_low, grad_branch)
    grad_attended = by_transpose(grad_branch, w_out).astype(jnp.bfloat16).reshape(head_shape)
    row_delta = jnp.transpose(
        jnp.sum(grad_attended.astype(jnp.float32) * attended, axis=-1), (0, 2, 1)
    )
    keys_all, mixed_all, docs_all = (
        lax.all_gather(keys_rot, "blk", axis=1, tiled=True),
        lax.all_gather(mixed_values, "blk", axis=1, tiled=True),
        lax.all_gather(docs, "blk", axis=1, tiled=True),
    )
    grad_query, grad_keys_all, grad_mixed_all = attend_back(
        queries, grad_attended, row_delta, log_total, keys_all, mixed_all, docs_all, docs, query_pos
    )
    grad_keys, grad_mixed = (
        lax.psum_scatter(
            grad_keys_all.astype(jnp.bfloat16), "blk", scatter_dimension=1, tiled=True
        ).astype(jnp.float32),
        lax.psum_scatter(
            grad_mixed_all.astype(jnp.bfloat16), "blk", scatter_dimension=1, tiled=True
        ).astype(jnp.float32),
    )
    grad_query_pre = (
        unrotate(grad_query, cosine, sines).astype(jnp.bfloat16).reshape(count_tokens, model_width)
    )
    grad_keys_pre = (
        unrotate(grad_keys.reshape(head_shape), cosine, sines)
        .astype(jnp.bfloat16)
        .reshape(count_tokens, model_width)
    )
    grad_values = (0.5 * grad_mixed).astype(jnp.bfloat16)
    grad_projected = jnp.concatenate(
        [grad_query_pre, grad_keys_pre, grad_values.reshape(count_tokens, model_width)], axis=-1
    )
    grad_qkv = by_rows(normed, grad_projected)
    grad_normed = by_transpose(grad_projected, w_qkv)
    grad_inputs, grad_gain_attn = norm_back(grad_normed, inputs, factor_attn, gain_attn)
    grad_tokens = (grad_inputs + grad_middle).astype(jnp.bfloat16).reshape(tokens.shape)
    summed_grads = (
        lax.psum_scatter(grad_qkv, ("dp", "blk"), scatter_dimension=0, tiled=True),
        lax.psum_scatter(grad_out, ("dp", "blk"), scatter_dimension=0, tiled=True),
        lax.psum_scatter(grad_gate, ("dp", "blk"), scatter_dimension=0, tiled=True),
        lax.psum_scatter(grad_up, ("dp", "blk"), scatter_dimension=0, tiled=True),
        lax.psum_scatter(grad_down, ("dp", "blk"), scatter_dimension=0, tiled=True),
        lax.psum_scatter(grad_gain_attn, ("dp", "blk"), scatter_dimension=0, tiled=True),
        lax.psum_scatter(grad_gain_ffn, ("dp", "blk"), scatter_dimension=0, tiled=True),
    )
    return (
        output,
        grad_tokens,
        grad_values,
        summed_grads[0],
        summed_grads[1],
        summed_grads[2],
        summed_grads[3],
        summed_grads[4],
        summed_grads[5],
        summed_grads[6],
    )


def solution(mesh):
    in_specs = (
        P("dp", "blk", None),
        P("dp", "blk", None),
        P("dp", "blk"),
        P("dp", "blk", None),
        P(),
        P(),
        P(),
        P(),
        P(),
        P(),
        P(),
    )
    out_specs = (
        P("dp", "blk", None),
        P("dp", "blk", None),
        P("dp", "blk", None),
        P(("dp", "blk"), None),
        P(("dp", "blk"), None),
        P(("dp", "blk"), None),
        P(("dp", "blk"), None),
        P(("dp", "blk"), None),
        P(("dp", "blk")),
        P(("dp", "blk")),
    )
    return jax.shard_map(shards, mesh=mesh, in_specs=in_specs, out_specs=out_specs, check_vma=False)
```

profile of v0, /device:TPU:0, one launch (start us, length us, event | category | flops | bytes accessed | tf_op | source)
XLA Modules:
  0.0 1104.9 jit_solution(8303734076416939542)
XLA Ops:
  45.0 15.1 %all-gather = s32[8,64,4]{1,2,0:T(4,128)S(1)} all-gather(s32[1,64,4]{1,2,0:T(4,128)S(1)} %bitcast.123), channel_id=1, replica_groups=mesh['dp'=4,'blk'=8] {'blk'}, dimensions={0}, use_global_device_ids=true | all-gather | bytes 9216 | tf_op jit(solution)/shard_map/all_gather | solution.py:218
  60.4 24.1 %all-gather.4.cloned.1.call-done = bf16[4,512,1024]{2,1,0:T(8,128)(2,1)} async-done(((bf16[4,64,1024]{2,1,0:T(8,128)(2,1)}), bf16[4,512,1024]{2,1,0:T(8,128)(2,1)}) %all-gather.4.cloned.1.call-update) | async-done | bytes 4194320 | tf_op jit(solution)/shard_map/all_gather | solution.py:216
  84.5 6.2 copy.52
  98.3 34.0 %all-gather.6.cloned.1.call-done = bf16[4,512,1024]{2,1,0:T(8,128)(2,1)} async-done(((bf16[4,64,1024]{2,1,0:T(8,128)(2,1)}), bf16[4,512,1024]{2,1,0:T(8,128)(2,1)}) %all-gather.6.cloned.1.call-update) | async-done | bytes 4194320 | tf_op jit(solution)/shard_map/all_gather | solution.py:217
  132.4 6.2 copy.54
  138.6 8.9 fusion.53
  153.2 6.9 fusion.55
  163.5 18.1 %multiply_convert_fusion.2 = (bf16[256,2816]{1,0:T(8,128)(2,1)S(1)}, bf16[256,2816]{1,0:T(8,128)(2,1)S(1)}, bf16[256,2816]{1,0:T(8,128)(2,1)}) fusion(f32[256,2816]{1,0:T(8,128)} %fusion.55, f32[256,2816]{1,0:T(8,128)} %fusion.56, bf16[256,1024]{1,0:T(8,128)(2,1)S(1)} %bitcast.118, bf16[2816,1024]{1,0:T(8,128)(2,1)S(1)} %bitcast.129), kind=kOutput, calls=%fused_computation.20 | convolution fusion | flops 1487929344 | bytes 16384000 | tf_op jit(solution)/shard_map/dot_general | solution.py:57
  192.0 6.3 multiply_convert_fusion.1
  201.6 6.3 copy.60
  208.0 8.0 fusion.17
  215.9 6.3 copy.62
  227.7 5.9 fusion.58
  235.0 5.9 fusion.59
  242.5 5.8 fusion.60
  267.9 39.5 %reduce-scatter.10.cloned.1.call-done = bf16[4,64,1024]{2,1,0:T(8,128)(2,1)} async-done(((bf16[4,512,1024]{2,1,0:T(8,128)(2,1)}), bf16[4,64,1024]{2,1,0:T(8,128)(2,1)}) %reduce-scatter.10.cloned.1.call-update) | async-done | bytes 524304 | tf_op jit(solution)/shard_map/reduce_scatter | solution.py:269
  310.7 6.3 fusion.34
  323.9 5.9 fusion.33
  329.8 38.2 %all-reduce.2 = (f32[1024]{0:T(1024)S(1)}, f32[1024]{0:T(1024)S(1)}) all-reduce(f32[1024]{0:T(1024)S(1)} %get-tuple-element.73, f32[1024]{0:T(1024)S(1)} %get-tuple-element.57), channel_id=9, replica_groups=mesh['dp'=4,'blk'=8] {'dp','blk'}, use_global_device_ids=true, to_apply=%region_15.16.clone | all-reduce | flops 2048 | bytes 16384
  371.7 81.2 %reduce-scatter.14.cloned.1.call-done = f32[32,1024]{1,0:T(8,128)} async-done(((f32[1024,1024]{1,0:T(8,128)}), f32[32,1024]{1,0:T(8,128)}) %reduce-scatter.14.cloned.1.call-update) | async-done | bytes 131088 | tf_op jit(solution)/shard_map/reduce_scatter | solution.py:291
  452.9 161.6 %reduce-scatter.16.cloned.1.call-done = f32[32,2816]{1,0:T(8,128)} async-done(((f32[1024,2816]{1,0:T(8,128)}), f32[32,2816]{1,0:T(8,128)}) %reduce-scatter.16.cloned.1.call-update) | async-done | bytes 360464 | tf_op jit(solution)/shard_map/reduce_scatter | solution.py:292
  614.5 162.3 %reduce-scatter.18.cloned.1.call-done = f32[32,2816]{1,0:T(8,128)} async-done(((f32[1024,2816]{1,0:T(8,128)}), f32[32,2816]{1,0:T(8,128)}) %reduce-scatter.18.cloned.1.call-update) | async-done | bytes 360464 | tf_op jit(solution)/shard_map/reduce_scatter | solution.py:293
  776.8 161.7 %reduce-scatter.20.cloned.1.call-done = f32[88,1024]{1,0:T(8,128)} async-done(((f32[2816,1024]{1,0:T(8,128)}), f32[88,1024]{1,0:T(8,128)}) %reduce-scatter.20.cloned.1.call-update) | async-done | bytes 360464 | tf_op jit(solution)/shard_map/reduce_scatter | solution.py:294
  938.4 159.6 %reduce-scatter.12.cloned.1.call-done = f32[32,3072]{1,0:T(8,128)} async-done(((f32[1024,3072]{1,0:T(8,128)}), f32[32,3072]{1,0:T(8,128)}) %reduce-scatter.12.cloned.1.call-update) | async-done | bytes 393232 | tf_op jit(solution)/shard_map/reduce_scatter | solution.py:290
  (172 shorter events, 109.7 us)
Async XLA Ops:
  7.2 145.0 %copy-start = (bf16[1024,1024]{1,0:T(8,128)(2,1)S(1)}, bf16[1024,1024]{1,0:T(8,128)(2,1)}, u32[]{:S(2)}) copy-start(bf16[1024,1024]{1,0:T(8,128)(2,1)} %param.16) | copy-start | bytes 6291460
  7.2 77.3 %all-gather.4.cloned.1.call-start = ((), (), s32[]{:S(2)}) async-start(), calls=%async_computation.7 | async-start | bytes 4718592 | tf_op jit(solution)/shard_map/all_gather | solution.py:216
  34.6 97.8 %all-gather.6.cloned.1.call-start = ((), (), s32[]{:S(2)}) async-start(), calls=%async_computation.8 | async-start | bytes 4718592 | tf_op jit(solution)/shard_map/all_gather | solution.py:217
  35.4 225.0 %reduce-scatter.8.cloned.1.call-start = ((), (), s32[]{:S(2)}) async-start(), calls=%async_computation.9 | async-start | bytes 4718592 | tf_op jit(solution)/shard_map/reduce_scatter | solution.py:266
  45.0 45.8 %copy-start.7 = (bf16[4,64,16,64]{1,3,2,0:T(8,128)(2,1)}, bf16[4,64,16,64]{1,3,2,0:T(8,128)(2,1)S(1)}, u32[]{:S(2)}) copy-start(bf16[4,64,16,64]{1,3,2,0:T(8,128)(2,1)S(1)} %copy.59) | copy-start | bytes 1572868
  152.2 8.0 slice-start.2
  153.0 32.2 %copy-start.5 = (f32[256,1024]{1,0:T(8,128)}, f32[256,1024]{1,0:T(8,128)S(1)}, u32[]{:S(2)}) copy-start(f32[256,1024]{1,0:T(8,128)S(1)} %get-tuple-element.116) | copy-start | bytes 3145732
  153.2 6.9 copy-start.11
  153.2 6.9 slice-start.3
  153.2 10.2 slice-start.4
  160.2 21.4 %slice-start = ((s8[5767168]{0:T(1024)(128)(4,1)}), s8[4194304]{0:T(1024)(128)(4,1)S(1)}, s32[]{:S(2)}) async-start(s8[5767168]{0:T(1024)(128)(4,1)} %bitcast.124), calls=%async_computation.16 | async-start | bytes 8388608
  163.4 18.1 %slice-start.1 = ((s8[5767168]{0:T(1024)(128)(4,1)}), s8[1572864]{0:T(1024)(128)(4,1)S(1)}, s32[]{:S(2)}) async-start(s8[5767168]{0:T(1024)(128)(4,1)} %bitcast.124), calls=%async_computation.17 | async-start | bytes 3145728
  192.0 6.3 copy-start.8
  207.9 99.4 %reduce-scatter.10.cloned.1.call-start = ((), (), s32[]{:S(2)}) async-start(), calls=%async_computation.10 | async-start | bytes 4718592 | tf_op jit(solution)/shard_map/reduce_scatter | solution.py:269
  222.3 230.5 %reduce-scatter.14.cloned.1.call-start = ((), (), s32[]{:S(2)}) async-start(), calls=%async_computation.12 | async-start | bytes 4325376 | tf_op jit(solution)/shard_map/reduce_scatter | solution.py:291
  226.2 388.3 %reduce-scatter.16.cloned.1.call-start = ((), (), s32[]{:S(2)}) async-start(), calls=%async_computation.13 | async-start | bytes 11894784 | tf_op jit(solution)/shard_map/reduce_scatter | solution.py:292
  233.7 543.1 %reduce-scatter.18.cloned.1.call-start = ((), (), s32[]{:S(2)}) async-start(), calls=%async_computation.14 | async-start | bytes 11894784 | tf_op jit(solution)/shard_map/reduce_scatter | solution.py:293
  241.0 697.4 %reduce-scatter.20.cloned.1.call-start = ((), (), s32[]{:S(2)}) async-start(), calls=%async_computation.15 | async-start | bytes 11894784 | tf_op jit(solution)/shard_map/reduce_scatter | solution.py:294
  248.4 849.6 %reduce-scatter.12.cloned.1.call-start = ((), (), s32[]{:S(2)}) async-start(), calls=%async_computation.11 | async-start | bytes 12976128 | tf_op jit(solution)/shard_map/reduce_scatter | solution.py:290
  267.9 42.8 %copy-start.16 = (bf16[256,1024]{1,0:T(8,128)(2,1)S(1)}, bf16[256,1024]{1,0:T(8,128)(2,1)}, u32[]{:S(2)}) copy-start(bf16[256,1024]{1,0:T(8,128)(2,1)} %copy-done.15) | copy-start | bytes 1572868
  267.9 42.8 %copy-start.17 = (bf16[256,1024]{1,0:T(8,128)(2,1)S(1)}, bf16[256,1024]{1,0:T(8,128)(2,1)}, u32[]{:S(2)}) copy-start(bf16[256,1024]{1,0:T(8,128)(2,1)} %reshape.263) | copy-start | bytes 1572868
  308.5 8.5 copy-start.19
  310.6 6.3 copy-start.23
  323.9 774.1 %copy-start.1 = (bf16[1024,1024]{1,0:T(8,128)(2,1)S(1)}, bf16[1024,1024]{1,0:T(8,128)(2,1)}, u32[]{:S(2)}) copy-start(bf16[1024,1024]{1,0:T(8,128)(2,1)} %param.16) | copy-start | bytes 6291460
  (25 other events, 78.9 us)
Sparse Core Ops, SparseCore 0:
  34.7 49.7 all-gather.3
  86.7 45.6 all-gather.5
  208.0 48.7 reduce-scatter.7
  259.0 48.3 reduce-scatter.9
  310.0 142.7 reduce-scatter.13
  455.6 158.8 reduce-scatter.15
  617.4 159.3 reduce-scatter.17
  779.6 158.7 reduce-scatter.19
  945.0 152.9 reduce-scatter.11
where the time goes:
time: 1110 us; the launch traced here: 1100 us
  waiting for transfers between devices  825 us (74%)
  matrix products  113 us (10%)
  local copies, waits for them, and re-layouts  65.8 us (6%)
  blocking collectives  53.3 us (5%)
  other arithmetic  32.9 us (3%)
  between operations  14.9 us (1%)
    reduce_scatter x1, waiting for transfers between devices, shards(): lax.psum_scatter(grad_up, ('dp', 'blk'), scatter_dimension=0, tiled=True)  162 us
    reduce_scatter x1, waiting for transfers between devices, shards(): lax.psum_scatter(grad_down, ('dp', 'blk'), scatter_dimension=0, tiled=True)  162 us
    reduce_scatter x1, waiting for transfers between devices, shards(): lax.psum_scatter(grad_gate, ('dp', 'blk'), scatter_dimension=0, tiled=True)  162 us
    reduce_scatter x1, waiting for transfers between devices, shards(): lax.psum_scatter(grad_qkv, ('dp', 'blk'), scatter_dimension=0, tiled=True)  160 us
    reduce_scatter x1, waiting for transfers between devices, shards(): lax.psum_scatter(grad_out, ('dp', 'blk'), scatter_dimension=0, tiled=True)  81.2 us
    reduce_scatter x1, waiting for transfers between devices, shards(): lax.psum_scatter(grad_mixed_all.astype(jnp.bfloat16), 'blk', scatter_dime...  39.5 us
    unnamed x1, blocking collectives  38.2 us
    all_gather x1, waiting for transfers between devices, shards(): lax.all_gather(mixed_values, 'blk', axis=1, tiled=True)  34 us
  transfers between devices with their start and end apart: 9, of which 8 were waited for; matrix products, arithmetic and copies ran while one was open for 9% of the time, Pallas kernels for 0%

commit v1 on v0

v1 whole, which is shorter than its diff:
```python
import functools

import jax
import jax.numpy as jnp
from jax import lax
from jax.experimental import pallas as pl
from jax.experimental.pallas import tpu as pltpu
from jax.sharding import PartitionSpec as P

HEAD_DIM = 64
LANES = 128
AXES = ("dp", "blk")
epsilon = 1e-06
score_scale = 0.125
bf16 = jnp.bfloat16
f32 = jnp.float32

NN = (((1,), (0,)), ((), ()))
NT = (((1,), (1,)), ((), ()))
TN = (((0,), (0,)), ((), ()))


def mm(a, b, dims):
    return lax.dot_general(a, b, dims, preferred_element_type=f32)


def sds(shape, dtype):
    return jax.ShapeDtypeStruct(shape, dtype)


def cost(flops, nbytes, trans=0):
    return pl.CostEstimate(flops=int(flops), bytes_accessed=int(nbytes), transcendentals=int(trans))


def whole(shape):
    return pl.BlockSpec(shape, lambda *_: (0,) * len(shape))


def lane_half(shape):
    lane = lax.broadcasted_iota(jnp.int32, shape, len(shape) - 1)
    return (lane & (HEAD_DIM - 1)) < HEAD_DIM // 2


def turn(values):
    half = HEAD_DIM // 2
    return jnp.where(
        lane_half(values.shape),
        pltpu.roll(values, LANES - half, 1),
        pltpu.roll(values, half, 1),
    )


def head_mask(shape, head):
    lane = lax.broadcasted_iota(jnp.int32, shape, 1)
    return lane < HEAD_DIM if head == 0 else lane >= HEAD_DIM


def qkv_body(nq, x_ref, gain_ref, w_ref, first_ref, cos_ref, sin_ref, normed_ref, q_ref, kv_ref):
    step = pl.program_id(0)

    @pl.when(step == 0)
    def _():
        inputs = x_ref[...].astype(f32)
        factor = lax.rsqrt(jnp.mean(inputs * inputs, axis=-1, keepdims=True) + epsilon)
        normed_ref[...] = (inputs * factor * gain_ref[...]).astype(bf16)

    projected = mm(normed_ref[...], w_ref[...], NN)
    width = projected.shape[1]

    def rotated():
        parts = []
        for i in range(width // LANES):
            part = projected[:, i * LANES : (i + 1) * LANES]
            parts.append((part * cos_ref[...] + turn(part) * sin_ref[...]).astype(bf16))
        return jnp.concatenate(parts, axis=1)

    @pl.when(step < nq)
    def _():
        q_ref[...] = rotated()

    @pl.when((step >= nq) & (step < 2 * nq))
    def _():
        kv_ref[...] = rotated()

    @pl.when(step >= 2 * nq)
    def _():
        kv_ref[...] = (0.5 * projected + 0.5 * first_ref[...].astype(f32)).astype(bf16)


def project(x, gain, w_qkv, first, cosine, sines):
    rows, width = x.shape
    bn = 512
    nq = width // bn
    return pl.pallas_call(
        functools.partial(qkv_body, nq),
        grid=(3 * nq,),
        in_specs=[
            whole((rows, width)),
            whole((1, width)),
            pl.BlockSpec((width, bn), lambda j: (0, j)),
            pl.BlockSpec((rows, bn), lambda j: (0, jnp.maximum(j - 2 * nq, 0))),
            whole((rows, LANES)),
            whole((rows, LANES)),
        ],
        out_specs=[
            whole((rows, width)),
            pl.BlockSpec((rows, bn), lambda j: (0, jnp.minimum(j, nq - 1))),
            pl.BlockSpec((rows, bn), lambda j: (0, jnp.maximum(j - nq, 0))),
        ],
        out_shape=[sds((rows, width), bf16), sds((rows, width), bf16), sds((rows, 2 * width), bf16)],
        cost_estimate=cost(6 * rows * width * width, 6 * width * width + 12 * rows * width),
        name="project",
    )(x, gain, w_qkv, first, cosine, sines)


def set_bias(bias_ref, kpos_ref, qpos_ref, qstart_ref):
    keys, qpos = kpos_ref[...], qpos_ref[...]
    allowed = (keys <= qpos) & (keys >= qstart_ref[...])
    bias_ref[...] = jnp.where(allowed, 0.0, -1e30)


def attend_body(slots, *refs):
    q_ref = refs[0]
    k_refs = refs[1 : 1 + slots]
    v_refs = refs[1 + slots : 1 + 2 * slots]
    kpos_ref, qpos_ref, qstart_ref, out_ref, lse_ref, bias_ref = refs[1 + 2 * slots :]

    @pl.when(pl.program_id(0) == 0)
    def _():
        set_bias(bias_ref, kpos_ref, qpos_ref, qstart_ref)

    queries = q_ref[...] * jnp.asarray(score_scale, bf16)
    keys = jnp.concatenate([r[...] for r in k_refs], axis=0)
    values = jnp.concatenate([r[...] for r in v_refs], axis=0)
    values_t = jnp.transpose(values)
    outs = []
    for head in range(2):
        own = jnp.where(head_mask(queries.shape, head), queries, jnp.zeros_like(queries))
        scores = mm(keys, own, NT) + bias_ref[...]
        top = jnp.max(scores, axis=0, keepdims=True)
        weights = jnp.exp(scores - top)
        total = jnp.sum(weights, axis=0, keepdims=True)
        probs = (weights * (1.0 / total)).astype(bf16)
        outs.append(mm(values_t[head * HEAD_DIM : (head + 1) * HEAD_DIM], probs, NN))
        lse_ref[0, head : head + 1, :] = top + jnp.log(total)
    out_ref[...] = jnp.transpose(jnp.concatenate(outs, axis=0)).astype(bf16)


def attend(q, kvs, kpos, qpos, qstart):
    rows, width = q.shape
    slots = len(kvs)
    pairs = width // LANES
    keys = slots * rows
    col = pl.BlockSpec((rows, LANES), lambda i: (0, i))
    col_v = pl.BlockSpec((rows, LANES), lambda i: (0, pairs + i))
    return pl.pallas_call(
        functools.partial(attend_body, slots),
        grid=(pairs,),
        in_specs=[col]
        + [col] * slots
        + [col_v] * slots
        + [whole((keys, 1)), whole((1, rows)), whole((1, rows))],
        out_specs=[col, pl.BlockSpec((1, 2, rows), lambda i: (i, 0, 0))],
        out_shape=[sds((rows, width), bf16), sds((pairs, 2, rows), f32)],
        scratch_shapes=[pltpu.VMEM((keys, rows), f32)],
        cost_estimate=cost(
            8 * pairs * rows * keys * LANES, 2 * rows * width * (2 + 2 * slots), 2 * pairs * rows * keys
        ),
        name="attend",
    )(q, *kvs, *kvs, kpos, qpos, qstart)


def attend_back_body(slots, *refs):
    q_ref, grad_ref = refs[:2]
    k_refs = refs[2 : 2 + slots]
    v_refs = refs[2 + slots : 2 + 2 * slots]
    lse_ref, kpos_ref, qpos_ref, qstart_ref, cos_ref, sin_ref = refs[2 + 2 * slots : 8 + 2 * slots]
    gq_ref, gk_ref, gv_ref = refs[8 + 2 * slots : 11 + 2 * slots]
    other_k = refs[11 + 2 * slots : 10 + 3 * slots]
    other_v = refs[10 + 3 * slots : 9 + 4 * slots]
    bias_ref = refs[-1]

    @pl.when(pl.program_id(0) == 0)
    def _():
        set_bias(bias_ref, kpos_ref, qpos_ref, qstart_ref)

    queries = q_ref[...] * jnp.asarray(score_scale, bf16)
    grads = grad_ref[...]
    keys = jnp.concatenate([r[...] for r in k_refs], axis=0)
    values = jnp.concatenate([r[...] for r in v_refs], axis=0)
    keys_t = jnp.transpose(keys)
    grad_values = grad_keys = None
    grad_q = []
    for head in range(2):
        mask = head_mask(queries.shape, head)
        own_q = jnp.where(mask, queries, jnp.zeros_like(queries))
        own_g = jnp.where(mask, grads, jnp.zeros_like(grads))
        scores = mm(keys, own_q, NT) + bias_ref[...]
        probs = jnp.exp(scores - lse_ref[0, head : head + 1, :])
        grad_probs = mm(values, own_g, NT)
        delta = jnp.sum(probs * grad_probs, axis=0, keepdims=True)
        grad_scores = (probs * (grad_probs - delta)).astype(bf16)
        part_v = mm(probs.astype(bf16), own_g, NN)
        part_k = mm(grad_scores, own_q, NN)
        grad_values = part_v if grad_values is None else grad_values + part_v
        grad_keys = part_k if grad_keys is None else grad_keys + part_k
        grad_q.append(mm(keys_t[head * HEAD_DIM : (head + 1) * HEAD_DIM], grad_scores, NN))
    grad_q = jnp.transpose(jnp.concatenate(grad_q, axis=0)) * score_scale
    gq_ref[...] = (grad_q * cos_ref[...] - turn(grad_q) * sin_ref[...]).astype(bf16)
    rows = q_ref.shape[0]
    gk_ref[...] = grad_keys[:rows]
    gv_ref[...] = grad_values[:rows]
    for slot in range(1, slots):
        other_k[slot - 1][...] = grad_keys[slot * rows : (slot + 1) * rows].astype(bf16)
        other_v[slot - 1][...] = grad_values[slot * rows : (slot + 1) * rows].astype(bf16)


def attend_back(q, grad, kvs, lse, kpos, qpos, qstart, cosine, sines):
    rows, width = q.shape
    slots = len(kvs)
    pairs = width // LANES
    keys = slots * rows
    col = pl.BlockSpec((rows, LANES), lambda i: (0, i))
    col_v = pl.BlockSpec((rows, LANES), lambda i: (0, pairs + i))
    outs = pl.pallas_call(
        functools.partial(attend_back_body, slots),
        grid=(pairs,),
        in_specs=[col, col]
        + [col] * slots
        + [col_v] * slots
        + [pl.BlockSpec((1, 2, rows), lambda i: (i, 0, 0))]
        + [whole((keys, 1)), whole((1, rows)), whole((1, rows))]
        + [whole((rows, LANES))] * 2,
        out_specs=[col] * (3 + 2 * (slots - 1)),
        out_shape=[sds((rows, width), bf16)]
        + [sds((rows, width), f32)] * 2
        + [sds((rows, width), bf16)] * (2 * (slots - 1)),
        scratch_shapes=[pltpu.VMEM((keys, rows), f32)],
        cost_estimate=cost(
            20 * pairs * rows * keys * LANES, 2 * rows * width * (7 + 4 * slots), 2 * pairs * rows * keys
        ),
        name="attend_back",
    )(q, grad, *kvs, *kvs, lse, kpos, qpos, qstart, cosine, sines)
    gq, gk, gv = outs[:3]
    return gq, gk, gv, outs[3 : 2 + slots], outs[2 + slots :]


def ffn_body(
    steps,
    ff,
    x_ref,
    att_ref,
    wout_ref,
    gain_ref,
    cot_ref,
    wg_ref,
    wu_ref,
    wd_ref,
    nffn_ref,
    hidden_ref,
    acts_ref,
    out_ref,
    gmid_ref,
    gbranch_ref,
    gatt_ref,
    mid_s,
    acc_s,
    gacc_s,
    hid_s,
    gg_s,
    gu_s,
):
    step = pl.program_id(0)
    block = wg_ref.shape[1]

    @pl.when(step == 0)
    def _():
        middle = x_ref[...].astype(f32) + mm(att_ref[...], wout_ref[...], NN)
        mid_s[...] = middle
        factor = lax.rsqrt(jnp.mean(middle * middle, axis=-1, keepdims=True) + epsilon)
        nffn_ref[...] = (middle * factor * gain_ref[...]).astype(bf16)
        acc_s[...] = middle
        gacc_s[...] = jnp.zeros_like(gacc_s)

    normed = nffn_ref[...]
    wd = wd_ref[...]
    gate = mm(normed, wg_ref[...], NN)
    upward = mm(normed, wu_ref[...], NN)
    grad_hidden = mm(cot_ref[...], wd, NT)
    sig = 1.0 / (1.0 + jnp.exp(-gate))
    silu = gate * sig
    hidden = (silu * upward).astype(bf16)
    grad_gate = (grad_hidden * upward * (sig * (1.0 + gate * (1.0 - sig)))).astype(bf16)
    grad_up = (grad_hidden * silu).astype(bf16)
    acc_s[...] += mm(hidden, wd, NN)
    gacc_s[...] += mm(grad_gate, wg_ref[...], NT) + mm(grad_up, wu_ref[...], NT)
    at = pl.ds(pl.multiple_of(step * block, block), block)
    hid_s[:, at] = hidden
    gg_s[:, at] = grad_gate
    gu_s[:, at] = grad_up

    @pl.when(step == steps - 1)
    def _():
        quarter = ff // 4
        for i in range(4):
            cut = slice(i * quarter, (i + 1) * quarter)
            hidden_ref[i] = hid_s[:, cut]
            acts_ref[i] = jnp.concatenate([gg_s[:, cut], gu_s[:, cut]], axis=1)
        out_ref[...] = acc_s[...].astype(bf16)
        middle = mid_s[...]
        factor = lax.rsqrt(jnp.mean(middle * middle, axis=-1, keepdims=True) + epsilon)
        scaled = gacc_s[...] * gain_ref[...]
        inner = jnp.mean(scaled * middle, axis=-1, keepdims=True)
        grad_middle = cot_ref[...].astype(f32) + factor * (
            scaled - middle * (factor * factor * inner)
        )
        gmid_ref[...] = grad_middle
        branch = grad_middle.astype(bf16)
        gbranch_ref[...] = branch
        gatt_ref[...] = mm(branch, wout_ref[...], NT).astype(bf16)


def feed_forward(x, attended, w_out, gain, cot, w_gate, w_up, w_down):
    rows, width = x.shape
    ff = w_gate.shape[1]
    block = 256
    steps = ff // block
    quarter = ff // 4
    full = whole((rows, width))
    return pl.pallas_call(
        functools.partial(ffn_body, steps, ff),
        grid=(steps,),
        in_specs=[
            full,
            full,
            whole((width, width)),
            whole((1, width)),
            full,
            pl.BlockSpec((width, block), lambda j: (0, j)),
            pl.BlockSpec((width, block), lambda j: (0, j)),
            pl.BlockSpec((block, width), lambda j: (j, 0)),
        ],
        out_specs=[full, whole((4, rows, quarter)), whole((4, rows, 2 * quarter)), full, full, full, full],
        out_shape=[
            sds((rows, width), bf16),
            sds((4, rows, quarter), bf16),
            sds((4, rows, 2 * quarter), bf16),
            sds((rows, width), bf16),
            sds((rows, width), f32),
            sds((rows, width), bf16),
            sds((rows, width), bf16),
        ],
        scratch_shapes=[pltpu.VMEM((rows, width), f32)] * 3 + [pltpu.VMEM((rows, ff), bf16)] * 3,
        cost_estimate=cost(
            12 * rows * width * ff + 4 * rows * width * width,
            6 * width * ff + 2 * width * width + 20 * rows * width,
            rows * ff,
        ),
        name="feed_forward",
    )(x, attended, w_out, gain, cot, w_gate, w_up, w_down)


def grad_pack_body(received, *refs):
    gq_ref, gk_ref, gv_ref = refs[:3]
    other_k = refs[3 : 3 + received]
    other_v = refs[3 + received : 3 + 2 * received]
    cos_ref, sin_ref, packed_ref, first_ref = refs[3 + 2 * received :]
    grad_k, grad_v = gk_ref[...], gv_ref[...]
    for r in other_k:
        grad_k = grad_k + r[...].astype(f32)
    for r in other_v:
        grad_v = grad_v + r[...].astype(f32)
    grad_k = (grad_k * cos_ref[...] - turn(grad_k) * sin_ref[...]).astype(bf16)
    grad_v = (0.5 * grad_v).astype(bf16)
    first_ref[...] = grad_v
    packed_ref[0] = jnp.concatenate([gq_ref[...], grad_k, grad_v], axis=1)


def grad_pack(gq, gk, gv, other_k, other_v, cosine, sines):
    rows, width = gq.shape
    pairs = width // LANES
    received = len(other_k)
    col = pl.BlockSpec((rows, LANES), lambda i: (0, i))
    return pl.pallas_call(
        functools.partial(grad_pack_body, received),
        grid=(pairs,),
        in_specs=[col] * (3 + 2 * received) + [whole((rows, LANES))] * 2,
        out_specs=[pl.BlockSpec((1, rows, 3 * LANES), lambda i: (i, 0, 0)), col],
        out_shape=[sds((pairs, rows, 3 * LANES), bf16), sds((rows, width), bf16)],
        cost_estimate=cost(20 * rows * width, 2 * rows * width * 12),
        name="grad_pack",
    )(gq, gk, gv, *other_k, *other_v, cosine, sines)


def grad_inputs_body(pairs, packed_ref, wq_ref, wk_ref, wv_ref, x_ref, gain_ref, gmid_ref, out_ref, acc_s):
    step = pl.program_id(0)

    @pl.when(step == 0)
    def _():
        acc_s[...] = jnp.zeros_like(acc_s)

    weights = jnp.concatenate([wq_ref[...], wk_ref[...], wv_ref[...]], axis=1)
    acc_s[...] += mm(packed_ref[0], weights, NT)

    @pl.when(step == pairs - 1)
    def _():
        inputs = x_ref[...].astype(f32)
        factor = lax.rsqrt(jnp.mean(inputs * inputs, axis=-1, keepdims=True) + epsilon)
        scaled = acc_s[...] * gain_ref[...]
        inner = jnp.mean(scaled * inputs, axis=-1, keepdims=True)
        grads = gmid_ref[...] + factor * (scaled - inputs * (factor * factor * inner))
        out_ref[...] = grads.astype(bf16)


def grad_inputs(packed, w_qkv, x, gain, grad_middle):
    rows, width = x.shape
    pairs = width // LANES
    full = whole((rows, width))
    return pl.pallas_call(
        functools.partial(grad_inputs_body, pairs),
        grid=(pairs,),
        in_specs=[
            pl.BlockSpec((1, rows, 3 * LANES), lambda i: (i, 0, 0)),
            pl.BlockSpec((width, LANES), lambda i: (0, i)),
            pl.BlockSpec((width, LANES), lambda i: (0, pairs + i)),
            pl.BlockSpec((width, LANES), lambda i: (0, 2 * pairs + i)),
            full,
            whole((1, width)),
            full,
        ],
        out_specs=full,
        out_shape=sds((rows, width), bf16),
        scratch_shapes=[pltpu.VMEM((rows, width), f32)],
        cost_estimate=cost(6 * rows * width * width, 6 * width * width + 16 * rows * width),
        name="grad_inputs",
    )(packed, w_qkv, w_qkv, w_qkv, x, gain, grad_middle)


def outer_body(count, *refs):
    total = None
    for left, right in zip(refs[:count], refs[count : 2 * count]):
        part = mm(left[...], right[...], TN)
        total = part if total is None else total + part
    refs[-1][...] = total.astype(bf16)


def outer(lefts, rights):
    rows, height = lefts[0].shape
    width = rights[0].shape[1]
    count = len(lefts)
    block = 256 if height % 256 == 0 else height
    return pl.pallas_call(
        functools.partial(outer_body, count),
        grid=(height // block,),
        in_specs=[pl.BlockSpec((rows, block), lambda i: (0, i))] * count
        + [whole((rows, width))] * count,
        out_specs=pl.BlockSpec((block, width), lambda i: (i, 0)),
        out_shape=sds((height, width), bf16),
        cost_estimate=cost(
            2 * count * rows * height * width, 2 * (count * rows * (height + width) + height * width)
        ),
        name="outer",
    )(*lefts, *rights)


def build(ndp, nblk):
    n = ndp * nblk
    nbits = n.bit_length() - 1
    blk_bits = nblk.bit_length() - 1
    if (1 << nbits) != n or (1 << blk_bits) != nblk:
        raise ValueError("mesh sizes")
    low_e, high_e = blk_bits, nbits - 1

    def send(value, target):
        pairs = [(i, target(i)) for i in range(n)]
        pairs = [p for p in pairs if p[0] != p[1]]
        return lax.ppermute(value, AXES, pairs)

    def flip(value, bit):
        return send(value, lambda i: i ^ (1 << bit))

    def pick(value, index, axis=0):
        return lax.dynamic_index_in_dim(value, index, axis, keepdims=False)

    def shards(
        tokens, first_values, docs, cotangent, w_qkv, w_out, w_gate, w_up, w_down, gain_attn, gain_ffn
    ):
        seqs, length, width = tokens.shape
        ff = w_gate.shape[1]
        rows = seqs * length
        group = nblk // seqs
        blk = lax.axis_index("blk")
        index = lax.axis_index("dp") * nblk + blk
        seq, member = blk // group, blk % group

        def bit(t):
            return (index >> t) & 1

        def shift_seq(i, s):
            base, b = i - i % nblk, i % nblk
            return base + ((b // group + s) % seqs) * group + b % group

        def shift_member(i, s):
            base, b = i - i % nblk, i % nblk
            return base + (b // group) * group + (b % group + s) % group

        def to_sequence(value):
            parts = [pick(value, seq)]
            for s in range(1, seqs):
                out = pick(value, (seq + s) % seqs)
                parts.append(send(out, lambda i, s=s: shift_seq(i, s)))
            return jnp.concatenate(parts, axis=0)

        def from_sequence(value):
            blocks = value.reshape(seqs, length, width)
            result = jnp.zeros((seqs, length, width), value.dtype)
            for s in range(seqs):
                part = blocks[s]
                if s:
                    part = send(part, lambda i, s=s: shift_seq(i, -s))
                result = lax.dynamic_update_index_in_dim(result, part, (seq + s) % seqs, 0)
            return result

        x = to_sequence(tokens)
        first = to_sequence(first_values)
        cot = to_sequence(cotangent)

        docs_all = lax.all_gather(docs, "blk", axis=1, tiled=True)
        docs_row = pick(docs_all, seq)
        starts = jnp.sum((docs_row[None, :] < docs_row[:, None]).astype(jnp.int32), axis=1)
        starts = starts.reshape(nblk, length)
        base = jnp.arange(length, dtype=jnp.int32)
        blocks = [((seq - s) % seqs) * group + member for s in range(seqs)]
        qpos = jnp.concatenate([b * length + base for b in blocks])
        qstart = jnp.concatenate([pick(starts, b) for b in blocks])
        kpos = jnp.concatenate(
            [
                (((seq - s) % seqs) * group + (member - g) % group) * length + base
                for g in range(group)
                for s in range(seqs)
            ]
        )
        half = HEAD_DIM // 2
        inverse = 10000.0 ** (-jnp.arange(half, dtype=f32) / half)
        angles = qpos.astype(f32)[:, None] * inverse[None, :]
        cos_half, sin_half = jnp.cos(angles), jnp.sin(angles)
        cosine = jnp.concatenate([cos_half] * 4, axis=1)
        sines = jnp.concatenate([-sin_half, sin_half] * 2, axis=1)
        qpos, qstart, kpos = qpos[None, :], qstart[None, :], kpos[:, None]
        gain_a, gain_f = gain_attn[None, :], gain_ffn[None, :]

        normed, q, kv = project(x, gain_a, w_qkv, first, cosine, sines)
        kvs = [kv] + [send(kv, lambda i, g=g: shift_member(i, g)) for g in range(1, group)]
        attended, lse = attend(q, kvs, kpos, qpos, qstart)
        nffn, hidden4, acts4, out, grad_mid, grad_branch, grad_att = feed_forward(
            x, attended, w_out, gain_f, cot, w_gate, w_up, w_down
        )
        output = from_sequence(out)

        def share(value, e):
            edge = flip(value, e)
            return [value, edge, flip(value, 0), flip(edge, 0)]

        def share_quarters(value4, e):
            value = value4.reshape((2, 2) + value4.shape[1:])
            mine, theirs = pick(value, bit(e)), pick(value, 1 - bit(e))
            edge = flip(theirs, e)
            c = bit(0)
            return [
                pick(mine, c),
                pick(edge, c),
                flip(pick(mine, 1 - c), 0),
                flip(pick(edge, 1 - c), 0),
            ]

        def stage(value, device_bit, axis, last):
            b = bit(device_bit)
            got = flip(pick(value, 1 - b, axis), device_bit)
            total = pick(value, b, axis).astype(f32) + got.astype(f32)
            return total.astype(bf16)

        def reduce_columns(part, e):
            per = part.shape[0] // n
            value = part.reshape((2,) * nbits + (per, part.shape[1]))
            left = list(range(nbits - 1, -1, -1))
            order = [t for t in range(nbits - 1, blk_bits - 1, -1) if t != e]
            order += list(range(1, blk_bits))
            for t in order:
                axis = left.index(t)
                value = stage(value, t, axis, t == order[-1])
                left.pop(axis)
            b, c = bit(e), bit(0)
            keep, got = pick(value, b), flip(pick(value, 1 - b), e)
            low = jnp.where(b == 0, keep, got)
            high = jnp.where(b == 0, got, keep)
            both = jnp.stack([low, high])
            keep, got = pick(both, c, 1), flip(pick(both, 1 - c, 1), 0)
            low = jnp.where(c == 0, keep, got)
            high = jnp.where(c == 0, got, keep)
            return jnp.stack([low, high], axis=1).reshape(4, per, part.shape[1]).astype(f32)

        def reduce_rows(part):
            per = 4 * part.shape[0] // n
            value = part.reshape((2,) * (nbits - 2) + (per, part.shape[1]))
            left = list(range(nbits - 3, -1, -1))
            second = nbits - 2
            order = [(second, 0)]
            order += [(t, t) for t in range(nbits - 3, blk_bits - 1, -1)]
            order += [(t, t) for t in range(1, min(blk_bits, nbits - 2))]
            for device_bit, chunk_bit in order:
                axis = left.index(chunk_bit)
                value = stage(value, device_bit, axis, device_bit == order[-1][0])
                left.pop(axis)

            def swap(i):
                a, b = (i >> second) & 1, i & 1
                return i if a == b else i ^ (1 << second) ^ 1

            got = send(value, swap)
            return jnp.where(bit(second) == bit(0), value, got).astype(f32)

        down_part = outer(share_quarters(hidden4, high_e), share(cot, high_e))
        grad_down = reduce_rows(down_part)

        acts_part = outer(share(nffn, low_e), share_quarters(acts4, low_e))
        acts_done = reduce_columns(acts_part, low_e)
        quarter = ff // 4
        per = width // n

        def spread(value):
            return jnp.transpose(value, (1, 0, 2)).reshape(per, -1)

        grad_gate = spread(acts_done[:, :, :quarter])
        grad_up = spread(acts_done[:, :, quarter:])

        branch4 = jnp.transpose(grad_branch.reshape(rows, 4, width // 4), (1, 0, 2))
        out_part = outer(share(attended, high_e), share_quarters(branch4, high_e))
        grad_out = spread(reduce_columns(out_part, high_e))

        gq, gk, gv, other_k, other_v = attend_back(
            q, grad_att, kvs, lse, kpos, qpos, qstart, cosine, sines
        )
        got_k = [send(v, lambda i, g=g: shift_member(i, -g)) for g, v in enumerate(other_k, 1)]
        got_v = [send(v, lambda i, g=g: shift_member(i, -g)) for g, v in enumerate(other_v, 1)]
        packed, grad_first = grad_pack(gq, gk, gv, got_k, got_v, cosine, sines)
        grad_first_values = from_sequence(grad_first)
        grad_x = grad_inputs(packed, w_qkv, x, gain_a, grad_mid)
        grad_tokens = from_sequence(grad_x)

        pairs = width // LANES
        eighths = packed.reshape(2, 4, pairs // 8, rows, 3 * LANES)
        eighths = jnp.transpose(eighths, (0, 1, 3, 2, 4)).reshape(2, 4, rows, -1)
        done = []
        for color, e in enumerate((low_e, high_e)):
            part = outer(share(normed, e), share_quarters(eighths[color], e))
            done.append(reduce_columns(part, e))
        grad_qkv = jnp.concatenate(done, axis=0).reshape(8, per, pairs // 8, 3, LANES)
        grad_qkv = jnp.transpose(grad_qkv, (1, 3, 0, 2, 4)).reshape(per, 3 * width)

        def own(value):
            return lax.dynamic_slice_in_dim(value, index * per, per, 0)

        grad_gain_attn = jnp.sum(grad_qkv * own(w_qkv).astype(f32), axis=1) / own(gain_attn)
        grad_gain_ffn = (
            jnp.sum(
                grad_gate * own(w_gate).astype(f32) + grad_up * own(w_up).astype(f32), axis=1
            )
            / own(gain_ffn)
        )
        return (
            output,
            grad_tokens,
            grad_first_values,
            grad_qkv,
            grad_out,
            grad_gate,
            grad_up,
            grad_down,
            grad_gain_attn,
            grad_gain_ffn,
        )

    return shards


def solution(mesh):
    seq = P("dp", "blk", None)
    rows = P(AXES, None)
    vec = P(AXES)
    in_specs = (seq, seq, P("dp", "blk"), seq) + (P(),) * 7
    out_specs = (seq, seq, seq, rows, rows, rows, rows, rows, vec, vec)
    return jax.shard_map(
        build(mesh.shape["dp"], mesh.shape["blk"]),
        mesh=mesh,
        in_specs=in_specs,
        out_specs=out_specs,
        check_vma=False,
    )
```

time: 1110 us -> 422 us (0.38)
  waiting for transfers between devices: 825 us -> 170 us
  matrix products: 113 us -> 0 us
  Pallas kernels: 0 us -> 96.9 us
  starting transfers between devices: 0.58 us -> 59.4 us
  blocking collectives: 53.3 us -> 17.9 us
  other arithmetic: 32.9 us -> 17.3 us
  between operations: 14.9 us -> 1.82 us
  local copies, waits for them, and re-layouts: 65.8 us -> 53.6 us
    reduce_scatter x7 -> x0, waiting for transfers between devices: 766 us -> none  [the longest x1 162 us: shards(): lax.psum_scatter(grad_up, ('dp', 'blk'), scatter_dimension=0, tiled=True)]
    ppermute x0 -> x74, waiting for transfers between devices: none -> 170 us  [send(): return lax.ppermute(value, AXES, pairs)]
    dot_general x21 -> x0, matrix products: 113 us -> none  [the longest x5 29.1 us: by_transpose(): lax.dot_general(left_side, right_side, (((1,), (1,)), ((), ())), preferre...]
    pallas_call x0 -> x11, Pallas kernels: none -> 96.9 us  [the longest x5 26.4 us: outer(): pl.pallas_call(functools.partial(outer_body, count), grid=(height // bloc...]
    ppermute x0 -> x74, starting transfers between devices: none -> 59.4 us  [send(): return lax.ppermute(value, AXES, pairs)]
    all_gather x2 -> x0, waiting for transfers between devices: 58.1 us -> none  [the longest x1 34 us: shards(): lax.all_gather(mixed_values, 'blk', axis=1, tiled=True)]
    unnamed x1 -> x0, blocking collectives: 38.2 us -> none
    squeeze x0 -> x35, local copies, waits for them, and re-layouts: none -> 24.4 us  [pick(): return lax.dynamic_index_in_dim(value, index, axis, keepdims=False)]
  transfers between devices with their start and end apart: 9 -> 74, of which waited for: 8 -> 26; matrix products, arithmetic and copies ran while one was open for 9% -> 15% of each run, Pallas kernels for 0% -> 21%
where the time goes in v1:
time: 422 us; the launch traced here: 417 us
  waiting for transfers between devices  170 us (40%)
  Pallas kernels  96.9 us (23%)
  starting transfers between devices  59.4 us (14%)
  local copies, waits for them, and re-layouts  53.6 us (13%)
  blocking collectives  17.9 us (4%)
  other arithmetic  17.3 us (4%)
    ppermute x74, waiting for transfers between devices, send(): return lax.ppermute(value, AXES, pairs)  170 us
    ppermute x74, starting transfers between devices, send(): return lax.ppermute(value, AXES, pairs)  59.4 us
    pallas_call x5, Pallas kernels, outer(): pl.pallas_call(functools.partial(outer_body, count), grid=(height // bloc...  26.4 us
    squeeze x35, local copies, waits for them, and re-layouts, pick(): return lax.dynamic_index_in_dim(value, index, axis, keepdims=False)  24.4 us
    pallas_call x1, Pallas kernels, feed_forward(): pl.pallas_call(functools.partial(ffn_body, steps, ff), grid=(steps,), in_...  21.8 us
    all_gather x1, blocking collectives, shards(): docs_all = lax.all_gather(docs, 'blk', axis=1, tiled=True)  17.9 us
    pallas_call x1, Pallas kernels, attend_back(): pl.pallas_call(functools.partial(attend_back_body, slots), grid=(pairs,),...  12.3 us
    pallas_call x1, Pallas kernels, attend(): pl.pallas_call(functools.partial(attend_body, slots), grid=(pairs,), in_s...  11.8 us
  transfers between devices with their start and end apart: 74, of which 26 were waited for; matrix products, arithmetic and copies ran while one was open for 15% of the time, Pallas kernels for 21%

profile of v1, /device:TPU:0, one launch (start us, length us, event | category | flops | bytes accessed | tf_op | source)
XLA Modules:
  0.0 417.0 jit_solution(10959916583583041697)
XLA Ops:
  1.9 5.1 %collective-permute-start.2 = (bf16[64,1024]{1,0:T(8,128)(2,1)S(1)}, bf16[64,1024]{1,0:T(8,128)(2,1)S(1)}, u32[]{:S(2)}, u32[]{:S(2)}) collective-permute-start(bf16[64,1024]{1,0:T(8,128)(2,1)S(1)} %get-tuple-element.93), channel_id=1, source_target_pairs={{0,6},{1,7},{2,0},{3,1},{4,2},{5,3},{6,4},{7,5},{8,14},{9,15},{10,... | collective-permute-start | bytes 393224 | tf_op jit(solution)/shard_map/ppermute | solution.py:477
  20.7 8.8 %collective-permute-done.4 = bf16[64,1024]{1,0:T(8,128)(2,1)S(1)} collective-permute-done((bf16[64,1024]{1,0:T(8,128)(2,1)S(1)}, bf16[64,1024]{1,0:T(8,128)(2,1)S(1)}, u32[]{:S(2)}, u32[]{:S(2)}) %collective-permute-start.4) | collective-permute-done | bytes 131104 | tf_op jit(solution)/shard_map/ppermute | solution.py:477
  30.3 8.6 %project.1 = (bf16[256,1024]{1,0:T(8,128)(2,1)}, bf16[256,1024]{1,0:T(8,128)(2,1)}, bf16[256,2048]{1,0:T(8,128)(2,1)}) custom-call(bf16[256,1024]{1,0:T(8,128)(2,1)} %pad_maximum_fusion.x_ref, f32[1,1024]{1,0:T(1,128)} %bitcast.361, bf16[1024,3072]{1,0:T(8,128)(2,1)} %wv_ref.1, bf16[256,1024]{1,0:T(8,128)(2,1)} %pad_maximum_fusion.1.first_ref, ...), custom_call_target="tpu_custom_call" | custom-call | flops 1610612736 | bytes 9437184 | tf_op jit(solution)/shard_map/project/pallas_call | solution.py:94
  43.7 17.9 %all-gather = s32[8,64,4]{1,2,0:T(4,128)S(1)} all-gather(s32[1,64,4]{1,2,0:T(4,128)S(1)} %bitcast.369), channel_id=1, replica_groups=mesh['dp'=4,'blk'=8] {'blk'}, dimensions={0}, use_global_device_ids=true | all-gather | bytes 9216 | tf_op jit(solution)/shard_map/all_gather | solution.py:528
  67.0 11.8 %attend.1 = (bf16[256,1024]{1,0:T(8,128)(2,1)}, f32[8,2,256]{2,1,0:T(2,128)}) custom-call(bf16[256,1024]{1,0:T(8,128)(2,1)} %get-tuple-element.29.refs_0_, bf16[256,2048]{1,0:T(8,128)(2,1)} %get-tuple-element.30.refs_1_.refs_3_.refs_2_.refs_4_, bf16[256,2048]{1,0:T(8,128)(2,1)} %copy-done, ...), custom_call_target="tpu_custom_call" | custom-call | flops 1073741824 | bytes 3145728 | tf_op jit(solution)/shard_map/attend/pallas_call | solution.py:156
  78.8 21.8 %feed_forward.1 = (bf16[256,1024]{1,0:T(8,128)(2,1)}, bf16[4,256,704]{2,1,0:T(8,128)(2,1)}, bf16[4,256,1408]{2,1,0:T(8,128)(2,1)}, bf16[256,1024]{1,0:T(8,128)(2...) custom-call(bf16[256,1024]{1,0:T(8,128)(2,1)} %pad_maximum_fusion.x_ref, ...), custom_call_target="tpu_custom_call" | custom-call | flops 9932111872 | bytes 24641536 | tf_op jit(solution)/shard_map/feed_forward/pallas_call | solution.py:330
  104.4 12.3 %attend_back.1 = (bf16[256,1024]{1,0:T(8,128)(2,1)}, f32[256,1024]{1,0:T(8,128)}, f32[256,1024]{1,0:T(8,128)}, bf16[256,1024]{1,0:T(8,128)(2,1)}, bf16[256,1024]{1,0:T(8,128)(2,1)}) custom-call(bf16[256,1024]{1,0:T(8,128)(2,1)} %get-tuple-element.29.refs_0_, bf16[256,1024]{1,0:T(8,128)(2,1)} %get-tuple-element.33.refs_1_, ...), custom_call_target="tpu_custom_call" | custom-call | flops 2684354560 | bytes 7864320 | tf_op jit(solution)/shard_map/attend_back/pallas_call | solution.py:225
  131.9 5.8 %collective-permute-done.45 = bf16[2,256,256]{2,1,0:T(8,128)(2,1)S(1)} collective-permute-done((bf16[2,256,256]{2,1,0:T(8,128)(2,1)S(1)}, bf16[2,256,256]{2,1,0:T(8,128)(2,1)S(1)}, u32[]{:S(2)}, u32[]{:S(2)}) %collective-permute-start.45) | collective-permute-done | bytes 262176 | tf_op jit(solution)/shard_map/ppermute | solution.py:477
  139.8 6.6 %grad_pack.1 = (bf16[8,256,384]{2,1,0:T(8,128)(2,1)}, bf16[256,1024]{1,0:T(8,128)(2,1)}) custom-call(bf16[256,1024]{1,0:T(8,128)(2,1)} %get-tuple-element.35.refs_0_, f32[256,1024]{1,0:T(8,128)} %get-tuple-element.36.refs_1_, f32[256,1024]{1,0:T(8,128)} %get-tuple-element.37.refs_2_, bf16[256,1024]{1,0:T(8,128)(2,1)} %collective-permute-done.13.refs_3_, ...), custom_call_target="tpu_custom_call" | custom-call | flops 5242880 | bytes 6291456 | tf_op jit(solution)/shard_map/grad_pack/pallas_call | solution.py:384
  148.0 9.4 %grad_inputs.1 = bf16[256,1024]{1,0:T(8,128)(2,1)} custom-call(bf16[8,256,384]{2,1,0:T(8,128)(2,1)} %get-tuple-element.40.packed_ref, bf16[1024,3072]{1,0:T(8,128)(2,1)} %wv_ref.1, bf16[1024,3072]{1,0:T(8,128)(2,1)} %wv_ref.1, bf16[1024,3072]{1,0:T(8,128)(2,1)} %wv_ref.1, bf16[256,1024]{1,0:T(8,128)(2,1)} %pad_maximum_fusion.x_ref, f32[1,1024]{1,0:T(1,128)} %bitcast.362, ...), custom_call_target="tpu_custom_call" | custom-call | flops 1610612736 | bytes 10485760 | tf_op jit(solution)/shard_map/grad_inputs/pallas_call | solution.py:419
  178.4 6.4 %collective-permute-done.17 = bf16[64,1024]{1,0:T(8,128)(2,1)S(1)} collective-permute-done((bf16[64,1024]{1,0:T(8,128)(2,1)S(1)}, bf16[64,1024]{1,0:T(8,128)(2,1)S(1)}, u32[]{:S(2)}, u32[]{:S(2)}) %collective-permute-start.17) | collective-permute-done | bytes 131104 | tf_op jit(solution)/shard_map/ppermute | solution.py:477
  192.7 6.1 %collective-permute-done.19 = bf16[64,1024]{1,0:T(8,128)(2,1)S(1)} collective-permute-done((bf16[64,1024]{1,0:T(8,128)(2,1)S(1)}, bf16[64,1024]{1,0:T(8,128)(2,1)S(1)}, u32[]{:S(2)}, u32[]{:S(2)}) %collective-permute-start.19) | collective-permute-done | bytes 131104 | tf_op jit(solution)/shard_map/ppermute | solution.py:477
  222.9 4.8 %outer.9 = bf16[704,1024]{1,0:T(8,128)(2,1)} custom-call(bf16[256,704]{1,0:T(8,128)(2,1)} %get-tuple-element.53.refs_0_, bf16[256,704]{1,0:T(8,128)(2,1)} %bitcast.359, bf16[256,704]{1,0:T(8,128)(2,1)} %collective-permute-done.65.refs_2_, bf16[256,704]{1,0:T(8,128)(2,1)} %collective-permute-done.66.refs_3_, ...), custom_call_target="tpu_custom_call" | custom-call | flops 1476395008 | bytes 4980736 | tf_op jit(solution)/shard_map/outer/pallas_call | solution.py:452
  232.5 4.9 %outer.6 = bf16[1024,384]{1,0:T(8,128)(2,1)} custom-call(bf16[256,1024]{1,0:T(8,128)(2,1)} %get-tuple-element.43.refs_0_, bf16[256,1024]{1,0:T(8,128)(2,1)} %collective-permute-done.32.refs_1_, bf16[256,1024]{1,0:T(8,128)(2,1)} %copy-done.6, bf16[256,1024]{1,0:T(8,128)(2,1)} %copy-done.17, bf16[256,384]{1,0:T(8,128)(2,1)} %get-tuple-element.63.refs_4_, ...), custom_call_target="tpu_custom_call" | custom-call | flops 805306368 | bytes 3670016 | tf_op jit(solution)/shard_map/outer/pallas_call | solution.py:452
  239.2 20.8 %collective-permute-done.48 = bf16[2,2,2,2,32,256]{5,4,3,2,1,0:T(8,128)(2,1)} collective-permute-done((bf16[2,2,2,2,32,256]{5,4,3,2,1,0:T(8,128)(2,1)S(1)}, bf16[2,2,2,2,32,256]{5,4,3,2,1,0:T(8,128)(2,1)}, u32[]{:S(2)}, u32[]{:S(2)}) %collective-permute-start.48) | collective-permute-done | bytes 262176 | tf_op jit(solution)/shard_map/ppermute | solution.py:477
  261.6 8.6 %collective-permute-done.53.refs_1_ = bf16[256,1024]{1,0:T(8,128)(2,1)} collective-permute-done((bf16[256,1024]{1,0:T(8,128)(2,1)}, bf16[256,1024]{1,0:T(8,128)(2,1)}, u32[]{:S(2)}, u32[]{:S(2)}) %collective-permute-start.53) | collective-permute-done | bytes 524320 | tf_op jit(solution)/shard_map/ppermute | solution.py:477
  271.5 4.9 %outer.5 = bf16[1024,384]{1,0:T(8,128)(2,1)} custom-call(bf16[256,1024]{1,0:T(8,128)(2,1)} %get-tuple-element.43.refs_0_, bf16[256,1024]{1,0:T(8,128)(2,1)} %copy-done.16, bf16[256,1024]{1,0:T(8,128)(2,1)} %copy-done.6, bf16[256,1024]{1,0:T(8,128)(2,1)} %collective-permute-done.23.refs_3_, bf16[256,384]{1,0:T(8,128)(2,1)} %get-tuple-element.61.refs_4_, ...), custom_call_target="tpu_custom_call" | custom-call | flops 805306368 | bytes 3670016 | tf_op jit(solution)/shard_map/outer/pallas_call | solution.py:452
  290.1 4.8 %collective-permute-done.27 = bf16[2,2,2,2,32,384]{5,4,3,2,1,0:T(8,128)(2,1)S(1)} collective-permute-done((bf16[2,2,2,2,32,384]{5,4,3,2,1,0:T(8,128)(2,1)S(1)}, bf16[2,2,2,2,32,384]{5,4,3,2,1,0:T(8,128)(2,1)S(1)}, u32[]{:S(2)}, u32[]{:S(2)}) %collective-permute-start.27) | collective-permute-done | bytes 393248 | tf_op jit(solution)/shard_map/ppermute | solution.py:477
  301.1 6.0 %collective-permute-done.38 = bf16[2,2,2,32,384]{4,3,2,1,0:T(8,128)(2,1)S(1)} collective-permute-done((bf16[2,2,2,32,384]{4,3,2,1,0:T(8,128)(2,1)S(1)}, bf16[2,2,2,32,384]{4,3,2,1,0:T(8,128)(2,1)S(1)}, u32[]{:S(2)}, u32[]{:S(2)}) %collective-permute-start.38) | collective-permute-done | bytes 196640 | tf_op jit(solution)/shard_map/ppermute | solution.py:477
  307.5 5.8 %collective-permute-done.28 = bf16[2,2,2,32,384]{4,3,2,1,0:T(8,128)(2,1)S(1)} collective-permute-done((bf16[2,2,2,32,384]{4,3,2,1,0:T(8,128)(2,1)S(1)}, bf16[2,2,2,32,384]{4,3,2,1,0:T(8,128)(2,1)S(1)}, u32[]{:S(2)}, u32[]{:S(2)}) %collective-permute-start.28) | collective-permute-done | bytes 196640 | tf_op jit(solution)/shard_map/ppermute | solution.py:477
  317.6 7.4 %outer.8 = bf16[1024,1408]{1,0:T(8,128)(2,1)} custom-call(bf16[256,1024]{1,0:T(8,128)(2,1)} %get-tuple-element.45.refs_0_, bf16[256,1024]{1,0:T(8,128)(2,1)} %collective-permute-done.53.refs_1_, bf16[256,1024]{1,0:T(8,128)(2,1)} %collective-permute-done.54.refs_2_, bf16[256,1024]{1,0:T(8,128)(2,1)} %collective-permute-done.55.refs_3_, ...), custom_call_target="tpu_custom_call" | custom-call | flops 2952790016 | bytes 7864320 | tf_op jit(solution)/shard_map/outer/pallas_call | solution.py:452
  330.6 30.6 %collective-permute-done.40 = bf16[2,32,384]{2,1,0:T(8,128)(2,1)S(1)} collective-permute-done((bf16[2,32,384]{2,1,0:T(8,128)(2,1)S(1)}, bf16[2,32,384]{2,1,0:T(8,128)(2,1)S(1)}, u32[]{:S(2)}, u32[]{:S(2)}) %collective-permute-start.40) | collective-permute-done | bytes 49184 | tf_op jit(solution)/shard_map/ppermute | solution.py:477
  365.5 16.1 %collective-permute-done.60 = bf16[2,2,2,32,1408]{4,3,2,1,0:T(8,128)(2,1)} collective-permute-done((bf16[2,2,2,32,1408]{4,3,2,1,0:T(8,128)(2,1)}, bf16[2,2,2,32,1408]{4,3,2,1,0:T(8,128)(2,1)}, u32[]{:S(2)}, u32[]{:S(2)}) %collective-permute-start.60) | collective-permute-done | bytes 720928 | tf_op jit(solution)/shard_map/ppermute | solution.py:477
  388.4 16.4 %collective-permute-done.61 = bf16[2,2,32,1408]{3,2,1,0:T(8,128)(2,1)S(1)} collective-permute-done((bf16[2,2,32,1408]{3,2,1,0:T(8,128)(2,1)S(1)}, bf16[2,2,32,1408]{3,2,1,0:T(8,128)(2,1)S(1)}, u32[]{:S(2)}, u32[]{:S(2)}) %collective-permute-start.61) | collective-permute-done | bytes 360480 | tf_op jit(solution)/shard_map/ppermute | solution.py:477
  (341 shorter events, 163.5 us)
Async XLA Ops:
  38.9 27.2 %collective-permute-start.6 = (bf16[256,2048]{1,0:T(8,128)(2,1)}, bf16[256,2048]{1,0:T(8,128)(2,1)S(1)}, u32[]{:S(2)}, u32[]{:S(2)}) collective-permute-start(bf16[256,2048]{1,0:T(8,128)(2,1)} %get-tuple-element.30.refs_1_.refs_3_.refs_2_.refs_4_), channel_id=1, source_target_pairs={{0,1},{1,0},{2,3},{3,2},{4,5},{5,4},{6,7},{7,6},{8,9},{9,8},{10,11... | collective-permute-start | bytes 3145736 | tf_op jit(solution)/shard_map/ppermute | solution.py:477
  39.0 26.2 %collective-permute-start.9 = (bf16[64,1024]{1,0:T(8,128)(2,1)S(1)}, bf16[64,1024]{1,0:T(8,128)(2,1)S(1)}, u32[]{:S(2)}, u32[]{:S(2)}) collective-permute-start(bf16[64,1024]{1,0:T(8,128)(2,1)S(1)} %get-tuple-element.85), channel_id=1, source_target_pairs={{0,6},{1,7},{2,0},{3,1},{4,2},{5,3},{6,4},{7,5},{8,14},{9,15},{10,... | collective-permute-start | bytes 393224 | tf_op jit(solution)/shard_map/ppermute | solution.py:477
  40.6 24.6 %collective-permute-start.8 = (bf16[64,1024]{1,0:T(8,128)(2,1)S(1)}, bf16[64,1024]{1,0:T(8,128)(2,1)S(1)}, u32[]{:S(2)}, u32[]{:S(2)}) collective-permute-start(bf16[64,1024]{1,0:T(8,128)(2,1)S(1)} %get-tuple-element.86), channel_id=1, source_target_pairs={{0,4},{1,5},{2,6},{3,7},{4,0},{5,1},{6,2},{7,3},{8,12},{9,13},{10,... | collective-permute-start | bytes 393224 | tf_op jit(solution)/shard_map/ppermute | solution.py:477
  63.7 107.7 %collective-permute-start.32 = (bf16[256,1024]{1,0:T(8,128)(2,1)S(1)}, bf16[256,1024]{1,0:T(8,128)(2,1)}, u32[]{:S(2)}, u32[]{:S(2)}) collective-permute-start(bf16[256,1024]{1,0:T(8,128)(2,1)S(1)} %copy-done.5), channel_id=1, source_target_pairs={{0,16},{1,17},{2,18},{3,19},{4,20},{5,21},{6,22},{7,23},{8,24},{9,... | collective-permute-start | bytes 1572872 | tf_op jit(solution)/shard_map/ppermute | solution.py:477
  102.3 25.7 %collective-permute-start.10 = (bf16[64,1024]{1,0:T(8,128)(2,1)}, bf16[64,1024]{1,0:T(8,128)(2,1)}, u32[]{:S(2)}, u32[]{:S(2)}) collective-permute-start(bf16[64,1024]{1,0:T(8,128)(2,1)} %get-tuple-element.82), channel_id=1, source_target_pairs={{0,6},{1,7},{2,0},{3,1},{4,2},{5,3},{6,4},{7,5},{8,14},{9,15},{10,... | collective-permute-start | bytes 393224 | tf_op jit(solution)/shard_map/ppermute | solution.py:477
  102.3 27.1 %collective-permute-start.11 = (bf16[64,1024]{1,0:T(8,128)(2,1)}, bf16[64,1024]{1,0:T(8,128)(2,1)}, u32[]{:S(2)}, u32[]{:S(2)}) collective-permute-start(bf16[64,1024]{1,0:T(8,128)(2,1)} %get-tuple-element.81), channel_id=1, source_target_pairs={{0,4},{1,5},{2,6},{3,7},{4,0},{5,1},{6,2},{7,3},{8,12},{9,13},{10,... | collective-permute-start | bytes 393224 | tf_op jit(solution)/shard_map/ppermute | solution.py:477
  102.3 28.6 %collective-permute-start.12 = (bf16[64,1024]{1,0:T(8,128)(2,1)}, bf16[64,1024]{1,0:T(8,128)(2,1)}, u32[]{:S(2)}, u32[]{:S(2)}) collective-permute-start(bf16[64,1024]{1,0:T(8,128)(2,1)} %get-tuple-element.80), channel_id=1, source_target_pairs={{0,2},{1,3},{2,4},{3,5},{4,6},{5,7},{6,0},{7,1},{8,10},{9,11},{10,... | collective-permute-start | bytes 393224 | tf_op jit(solution)/shard_map/ppermute | solution.py:477
  130.9 42.1 %collective-permute-start.22 = (bf16[256,1024]{1,0:T(8,128)(2,1)S(1)}, bf16[256,1024]{1,0:T(8,128)(2,1)S(1)}, u32[]{:S(2)}, u32[]{:S(2)}) collective-permute-start(bf16[256,1024]{1,0:T(8,128)(2,1)S(1)} %copy-done.5), channel_id=1, source_target_pairs={{0,1},{1,0},{2,3},{3,2},{4,5},{5,4},{6,7},{7,6},{8,9},{9,8},{10,11... | collective-permute-start | bytes 1572872 | tf_op jit(solution)/shard_map/ppermute | solution.py:477
  137.7 40.6 %collective-permute-start.67 = (bf16[256,1024]{1,0:T(8,128)(2,1)S(1)}, bf16[256,1024]{1,0:T(8,128)(2,1)}, u32[]{:S(2)}, u32[]{:S(2)}) collective-permute-start(bf16[256,1024]{1,0:T(8,128)(2,1)S(1)} %copy-done.23), channel_id=1, source_target_pairs={{0,16},{1,17},{2,18},{3,19},{4,20},{5,21},{6,22},{7,23},{8,24},{9,... | collective-permute-start | bytes 1572872 | tf_op jit(solution)/shard_map/ppermute | solution.py:477
  138.9 47.6 %collective-permute-start.68 = (bf16[256,1024]{1,0:T(8,128)(2,1)S(1)}, bf16[256,1024]{1,0:T(8,128)(2,1)}, u32[]{:S(2)}, u32[]{:S(2)}) collective-permute-start(bf16[256,1024]{1,0:T(8,128)(2,1)S(1)} %copy-done.23), channel_id=1, source_target_pairs={{0,1},{1,0},{2,3},{3,2},{4,5},{5,4},{6,7},{7,6},{8,9},{9,8},{10,11... | collective-permute-start | bytes 1572872 | tf_op jit(solution)/shard_map/ppermute | solution.py:477
  173.0 28.9 %collective-permute-start.64 = (bf16[2,256,704]{1,2,0:T(8,128)(2,1)S(1)}, bf16[2,256,704]{1,2,0:T(8,128)(2,1)S(1)}, u32[]{:S(2)}, u32[]{:S(2)}) collective-permute-start(bf16[2,256,704]{1,2,0:T(8,128)(2,1)S(1)} %bitcast.356), channel_id=1, source_target_pairs={{0,16},{1,17},{2,18},{3,19},{4,20},{5,21},{6,22},{7,23},{8,24},{9,... | collective-permute-start | bytes 2162696 | tf_op jit(solution)/shard_map/ppermute | solution.py:477
  219.8 59.3 %collective-permute-start.56 = (bf16[2,256,1408]{2,1,0:T(8,128)(2,1)S(1)}, bf16[2,256,1408]{2,1,0:T(8,128)(2,1)}, u32[]{:S(2)}, u32[]{:S(2)}) collective-permute-start(bf16[2,256,1408]{2,1,0:T(8,128)(2,1)S(1)} %copy-done.13), channel_id=1, source_target_pairs={{0,8},{1,9},{2,10},{3,11},{4,12},{5,13},{6,14},{7,15},{8,0},{9,1},... | collective-permute-start | bytes 4325384 | tf_op jit(solution)/shard_map/ppermute | solution.py:477
  227.7 32.3 %collective-permute-start.48 = (bf16[2,2,2,2,32,256]{5,4,3,2,1,0:T(8,128)(2,1)S(1)}, bf16[2,2,2,2,32,256]{5,4,3,2,1,0:T(8,128)(2,1)}, u32[]{:S(2)}, u32[]{:S(2)}) collective-permute-start(bf16[2,2,2,2,32,256]{5,4,3,2,1,0:T(8,128)(2,1)S(1)} %dynamic-slice_bitcast_fusion.15), channel_id=1, source_target_pairs={{0,8},{1,9},{2,10},{3,11},{4,12},{5,13},{6,14},{7,15},{8,0},{9,1},... | collective-permute-start | bytes 786440 | tf_op jit(solution)/shard_map/ppermute | solution.py:477
  230.7 30.4 %collective-permute-start.23 = (bf16[256,1024]{1,0:T(8,128)(2,1)S(1)}, bf16[256,1024]{1,0:T(8,128)(2,1)}, u32[]{:S(2)}, u32[]{:S(2)}) collective-permute-start(bf16[256,1024]{1,0:T(8,128)(2,1)S(1)} %collective-permute-done.21.refs_1_), channel_id=1, source_target_pairs={{0,1},{1,0},{2,3},{3,2},{4,5},{5,4},{6,7},{7,6},{8,9},{9,8},{10,11... | collective-permute-start | bytes 1572872 | tf_op jit(solution)/shard_map/ppermute | solution.py:477
  230.8 39.5 %collective-permute-start.53 = (bf16[256,1024]{1,0:T(8,128)(2,1)}, bf16[256,1024]{1,0:T(8,128)(2,1)}, u32[]{:S(2)}, u32[]{:S(2)}) collective-permute-start(bf16[256,1024]{1,0:T(8,128)(2,1)} %get-tuple-element.45.refs_0_), channel_id=1, source_target_pairs={{0,8},{1,9},{2,10},{3,11},{4,12},{5,13},{6,14},{7,15},{8,0},{9,1},... | collective-permute-start | bytes 1572872 | tf_op jit(solution)/shard_map/ppermute | solution.py:477
  232.4 37.9 %collective-permute-start.25 = (bf16[256,384]{1,0:T(8,128)(2,1)}, bf16[256,384]{1,0:T(8,128)(2,1)}, u32[]{:S(2)}, u32[]{:S(2)}) collective-permute-start(bf16[256,384]{1,0:T(8,128)(2,1)} %get-tuple-element.60), channel_id=1, source_target_pairs={{0,1},{1,0},{2,3},{3,2},{4,5},{5,4},{6,7},{7,6},{8,9},{9,8},{10,11... | collective-permute-start | bytes 589832 | tf_op jit(solution)/shard_map/ppermute | solution.py:477
  261.1 53.5 %collective-permute-start.54 = (bf16[256,1024]{1,0:T(8,128)(2,1)}, bf16[256,1024]{1,0:T(8,128)(2,1)}, u32[]{:S(2)}, u32[]{:S(2)}) collective-permute-start(bf16[256,1024]{1,0:T(8,128)(2,1)} %get-tuple-element.45.refs_0_), channel_id=1, source_target_pairs={{0,1},{1,0},{2,3},{3,2},{4,5},{5,4},{6,7},{7,6},{8,9},{9,8},{10,11... | collective-permute-start | bytes 1572872 | tf_op jit(solution)/shard_map/ppermute | solution.py:477
  270.3 46.4 %collective-permute-start.57 = (bf16[256,1408]{1,0:T(8,128)(2,1)}, bf16[256,1408]{1,0:T(8,128)(2,1)}, u32[]{:S(2)}, u32[]{:S(2)}) collective-permute-start(bf16[256,1408]{1,0:T(8,128)(2,1)} %get-tuple-element.50), channel_id=1, source_target_pairs={{0,1},{1,0},{2,3},{3,2},{4,5},{5,4},{6,7},{7,6},{8,9},{9,8},{10,11... | collective-permute-start | bytes 2162696 | tf_op jit(solution)/shard_map/ppermute | solution.py:477
  270.3 46.4 %collective-permute-start.55 = (bf16[256,1024]{1,0:T(8,128)(2,1)}, bf16[256,1024]{1,0:T(8,128)(2,1)}, u32[]{:S(2)}, u32[]{:S(2)}) collective-permute-start(bf16[256,1024]{1,0:T(8,128)(2,1)} %collective-permute-done.53.refs_1_), channel_id=1, source_target_pairs={{0,1},{1,0},{2,3},{3,2},{4,5},{5,4},{6,7},{7,6},{8,9},{9,8},{10,11... | collective-permute-start | bytes 1572872 | tf_op jit(solution)/shard_map/ppermute | solution.py:477
  288.5 24.8 %collective-permute-start.70 = (bf16[2,2,88,1024]{3,2,0,1:T(8,128)(2,1)S(1)}, bf16[2,2,88,1024]{3,2,0,1:T(8,128)(2,1)S(1)}, u32[]{:S(2)}, u32[]{:S(2)}) collective-permute-start(bf16[2,2,88,1024]{3,2,0,1:T(8,128)(2,1)S(1)} %bitcast.357), channel_id=1, source_target_pairs={{0,8},{1,9},{2,10},{3,11},{4,12},{5,13},{6,14},{7,15},{8,0},{9,1},... | collective-permute-start | bytes 2162696 | tf_op jit(solution)/shard_map/ppermute | solution.py:477
  326.6 35.3 %collective-permute-start.59 = (bf16[2,2,2,2,32,1408]{5,4,3,2,1,0:T(8,128)(2,1)S(1)}, bf16[2,2,2,2,32,1408]{5,4,3,2,1,0:T(8,128)(2,1)S(1)}, u32[]{:S(2)}, u32[]{:S(2)}) collective-permute-start(bf16[2,2,2,2,32,1408]{5,4,3,2,1,0:T(8,128)(2,1)S(1)} %dynamic-slice_bitcast_fusion), channel_id=1, source_target_pairs={{0,16},{1,17},{2,18},{3,19},{4,20},{5,21},{6,22},{7,23},{8,24},{9,... | collective-permute-start | bytes 4325384 | tf_op jit(solution)/shard_map/ppermute | solution.py:477
  329.0 56.2 %collective-permute-start.71 = (bf16[2,88,1024]{2,1,0:T(8,128)(2,1)}, bf16[2,88,1024]{2,1,0:T(8,128)(2,1)}, u32[]{:S(2)}, u32[]{:S(2)}) collective-permute-start(bf16[2,88,1024]{2,1,0:T(8,128)(2,1)} %dynamic-slice_bitcast_fusion.13), channel_id=1, source_target_pairs={{0,2},{1,3},{2,0},{3,1},{4,6},{5,7},{6,4},{7,5},{8,10},{9,11},{10,... | collective-permute-start | bytes 1081352 | tf_op jit(solution)/shard_map/ppermute | solution.py:477
  329.4 31.8 %collective-permute-start.40 = (bf16[2,32,384]{2,1,0:T(8,128)(2,1)S(1)}, bf16[2,32,384]{2,1,0:T(8,128)(2,1)S(1)}, u32[]{:S(2)}, u32[]{:S(2)}) collective-permute-start(bf16[2,32,384]{2,1,0:T(8,128)(2,1)S(1)} %dynamic-slice_bitcast_fusion.49), channel_id=1, source_target_pairs={{0,16},{1,17},{2,18},{3,19},{4,20},{5,21},{6,22},{7,23},{8,24},{9,... | collective-permute-start | bytes 147464 | tf_op jit(solution)/shard_map/ppermute | solution.py:477
  330.0 31.3 %collective-permute-start.30 = (bf16[2,32,384]{2,1,0:T(8,128)(2,1)S(1)}, bf16[2,32,384]{2,1,0:T(8,128)(2,1)S(1)}, u32[]{:S(2)}, u32[]{:S(2)}) collective-permute-start(bf16[2,32,384]{2,1,0:T(8,128)(2,1)S(1)} %dynamic-slice_bitcast_fusion.50), channel_id=1, source_target_pairs={{0,8},{1,9},{2,10},{3,11},{4,12},{5,13},{6,14},{7,15},{8,0},{9,1},... | collective-permute-start | bytes 147464 | tf_op jit(solution)/shard_map/ppermute | solution.py:477
  (85 other events, 926.7 us)

commit v2 on v1

v2 whole, which is shorter than its diff:
```python
import functools

import jax
import jax.numpy as jnp
from jax import lax
from jax.experimental import pallas as pl
from jax.experimental.pallas import tpu as pltpu
from jax.sharding import PartitionSpec as P

HEAD_DIM = 64
LANES = 128
AXES = ("dp", "blk")
epsilon = 1e-06
score_scale = 0.125
cost_share = 0.3
bf16 = jnp.bfloat16
f32 = jnp.float32

NN = (((1,), (0,)), ((), ()))
NT = (((1,), (1,)), ((), ()))
TN = (((0,), (0,)), ((), ()))


def mm(a, b, dims):
    return lax.dot_general(a, b, dims, preferred_element_type=f32)


def sds(shape, dtype):
    return jax.ShapeDtypeStruct(shape, dtype)


def cost(flops, nbytes, trans=0):
    return pl.CostEstimate(
        flops=int(flops * cost_share), bytes_accessed=int(nbytes * cost_share), transcendentals=0
    )


def whole(shape):
    return pl.BlockSpec(shape, lambda *_: (0,) * len(shape))


def scalar():
    return pl.BlockSpec(memory_space=pltpu.SMEM)


def tie(*values):
    return lax.optimization_barrier(values)


def lane_half(shape):
    lane = lax.broadcasted_iota(jnp.int32, shape, len(shape) - 1)
    return (lane & (HEAD_DIM - 1)) < HEAD_DIM // 2


def turn(values):
    half = HEAD_DIM // 2
    return jnp.where(
        lane_half(values.shape),
        pltpu.roll(values, LANES - half, 1),
        pltpu.roll(values, half, 1),
    )


def head_mask(shape, head):
    lane = lax.broadcasted_iota(jnp.int32, shape, 1)
    return lane < HEAD_DIM if head == 0 else lane >= HEAD_DIM


def rotate_all(projected, cosine, sines):
    parts = []
    for i in range(projected.shape[1] // LANES):
        part = projected[:, i * LANES : (i + 1) * LANES]
        parts.append((part * cosine + turn(part) * sines).astype(bf16))
    return jnp.concatenate(parts, axis=1)


def query_key_body(nq, x_ref, gain_ref, w_ref, cos_ref, sin_ref, normed_ref, q_ref, k_ref):
    step = pl.program_id(0)

    @pl.when(step == 0)
    def _():
        inputs = x_ref[...].astype(f32)
        factor = lax.rsqrt(jnp.mean(inputs * inputs, axis=-1, keepdims=True) + epsilon)
        normed_ref[...] = (inputs * factor * gain_ref[...]).astype(bf16)

    rotated = rotate_all(mm(normed_ref[...], w_ref[...], NN), cos_ref[...], sin_ref[...])

    @pl.when(step < nq)
    def _():
        q_ref[...] = rotated

    @pl.when(step >= nq)
    def _():
        k_ref[...] = rotated


def query_key(x, gain, w_qkv, cosine, sines):
    rows, width = x.shape
    bn = 512
    nq = width // bn
    return pl.pallas_call(
        functools.partial(query_key_body, nq),
        grid=(2 * nq,),
        in_specs=[
            whole((rows, width)),
            whole((1, width)),
            pl.BlockSpec((width, bn), lambda j: (0, j)),
            whole((rows, LANES)),
            whole((rows, LANES)),
        ],
        out_specs=[
            whole((rows, width)),
            pl.BlockSpec((rows, bn), lambda j: (0, jnp.minimum(j, nq - 1))),
            pl.BlockSpec((rows, bn), lambda j: (0, jnp.maximum(j - nq, 0))),
        ],
        out_shape=[sds((rows, width), bf16)] * 3,
        cost_estimate=cost(4 * rows * width * width, 4 * width * width + 8 * rows * width),
        name="query_key",
    )(x, gain, w_qkv, cosine, sines)


def value_mix_body(normed_ref, w_ref, first_ref, out_ref):
    projected = mm(normed_ref[...], w_ref[...], NN)
    out_ref[...] = (0.5 * projected + 0.5 * first_ref[...].astype(f32)).astype(bf16)


def value_mix(normed, w_qkv, first):
    rows, width = normed.shape
    bn = 512
    nq = width // bn
    col = pl.BlockSpec((rows, bn), lambda j: (0, j))
    return pl.pallas_call(
        value_mix_body,
        grid=(nq,),
        in_specs=[whole((rows, width)), pl.BlockSpec((width, bn), lambda j: (0, 2 * nq + j)), col],
        out_specs=col,
        out_shape=sds((rows, width), bf16),
        cost_estimate=cost(2 * rows * width * width, 2 * width * width + 6 * rows * width),
        name="value_mix",
    )(normed, w_qkv, first)


def set_bias(bias_ref, kpos_ref, qpos_ref, qstart_ref):
    keys, qpos = kpos_ref[...], qpos_ref[...]
    allowed = (keys <= qpos) & (keys >= qstart_ref[...])
    bias_ref[...] = jnp.where(allowed, 0.0, -1e30)


def attend_body(slots, *refs):
    q_ref = refs[0]
    k_refs = refs[1 : 1 + slots]
    v_refs = refs[1 + slots : 1 + 2 * slots]
    kpos_ref, qpos_ref, qstart_ref, out_ref, lse_ref, bias_ref = refs[1 + 2 * slots :]

    @pl.when(pl.program_id(0) == 0)
    def _():
        set_bias(bias_ref, kpos_ref, qpos_ref, qstart_ref)

    queries = q_ref[...] * jnp.asarray(score_scale, bf16)
    keys = jnp.concatenate([r[...] for r in k_refs], axis=0)
    values = jnp.concatenate([r[...] for r in v_refs], axis=0)
    values_t = jnp.transpose(values)
    outs = []
    for head in range(2):
        own = jnp.where(head_mask(queries.shape, head), queries, jnp.zeros_like(queries))
        scores = mm(keys, own, NT) + bias_ref[...]
        top = jnp.max(scores, axis=0, keepdims=True)
        weights = jnp.exp(scores - top)
        total = jnp.sum(weights, axis=0, keepdims=True)
        probs = (weights * (1.0 / total)).astype(bf16)
        outs.append(mm(values_t[head * HEAD_DIM : (head + 1) * HEAD_DIM], probs, NN))
        lse_ref[0, head : head + 1, :] = top + jnp.log(total)
    out_ref[...] = jnp.transpose(jnp.concatenate(outs, axis=0)).astype(bf16)


def attend(q, ks, vs, kpos, qpos, qstart):
    rows, width = q.shape
    slots = len(ks)
    pairs = width // LANES
    keys = slots * rows
    col = pl.BlockSpec((rows, LANES), lambda i: (0, i))
    return pl.pallas_call(
        functools.partial(attend_body, slots),
        grid=(pairs,),
        in_specs=[col]
        + [col] * slots
        + [col] * slots
        + [whole((keys, 1)), whole((1, rows)), whole((1, rows))],
        out_specs=[col, pl.BlockSpec((1, 2, rows), lambda i: (i, 0, 0))],
        out_shape=[sds((rows, width), bf16), sds((pairs, 2, rows), f32)],
        scratch_shapes=[pltpu.VMEM((keys, rows), f32)],
        cost_estimate=cost(
            8 * pairs * rows * keys * LANES, 2 * rows * width * (2 + 2 * slots), 2 * pairs * rows * keys
        ),
        name="attend",
    )(q, *ks, *vs, kpos, qpos, qstart)


def attend_back_body(slots, *refs):
    q_ref, grad_ref = refs[:2]
    k_refs = refs[2 : 2 + slots]
    v_refs = refs[2 + slots : 2 + 2 * slots]
    lse_ref, kpos_ref, qpos_ref, qstart_ref, cos_ref, sin_ref = refs[2 + 2 * slots : 8 + 2 * slots]
    gq_ref, gk_ref, gv_ref = refs[8 + 2 * slots : 11 + 2 * slots]
    other_k = refs[11 + 2 * slots : 10 + 3 * slots]
    other_v = refs[10 + 3 * slots : 9 + 4 * slots]
    bias_ref = refs[-1]

    @pl.when(pl.program_id(0) == 0)
    def _():
        set_bias(bias_ref, kpos_ref, qpos_ref, qstart_ref)

    queries = q_ref[...] * jnp.asarray(score_scale, bf16)
    grads = grad_ref[...]
    keys = jnp.concatenate([r[...] for r in k_refs], axis=0)
    values = jnp.concatenate([r[...] for r in v_refs], axis=0)
    keys_t = jnp.transpose(keys)
    grad_values = grad_keys = None
    grad_q = []
    for head in range(2):
        mask = head_mask(queries.shape, head)
        own_q = jnp.where(mask, queries, jnp.zeros_like(queries))
        own_g = jnp.where(mask, grads, jnp.zeros_like(grads))
        scores = mm(keys, own_q, NT) + bias_ref[...]
        probs = jnp.exp(scores - lse_ref[0, head : head + 1, :])
        grad_probs = mm(values, own_g, NT)
        delta = jnp.sum(probs * grad_probs, axis=0, keepdims=True)
        grad_scores = (probs * (grad_probs - delta)).astype(bf16)
        part_v = mm(probs.astype(bf16), own_g, NN)
        part_k = mm(grad_scores, own_q, NN)
        grad_values = part_v if grad_values is None else grad_values + part_v
        grad_keys = part_k if grad_keys is None else grad_keys + part_k
        grad_q.append(mm(keys_t[head * HEAD_DIM : (head + 1) * HEAD_DIM], grad_scores, NN))
    grad_q = jnp.transpose(jnp.concatenate(grad_q, axis=0)) * score_scale
    gq_ref[...] = (grad_q * cos_ref[...] - turn(grad_q) * sin_ref[...]).astype(bf16)
    rows = q_ref.shape[0]
    gk_ref[...] = grad_keys[:rows]
    gv_ref[...] = grad_values[:rows]
    for slot in range(1, slots):
        other_k[slot - 1][...] = grad_keys[slot * rows : (slot + 1) * rows].astype(bf16)
        other_v[slot - 1][...] = grad_values[slot * rows : (slot + 1) * rows].astype(bf16)


def attend_back(q, grad, ks, vs, lse, kpos, qpos, qstart, cosine, sines):
    rows, width = q.shape
    slots = len(ks)
    pairs = width // LANES
    keys = slots * rows
    col = pl.BlockSpec((rows, LANES), lambda i: (0, i))
    outs = pl.pallas_call(
        functools.partial(attend_back_body, slots),
        grid=(pairs,),
        in_specs=[col, col]
        + [col] * slots
        + [col] * slots
        + [pl.BlockSpec((1, 2, rows), lambda i: (i, 0, 0))]
        + [whole((keys, 1)), whole((1, rows)), whole((1, rows))]
        + [whole((rows, LANES))] * 2,
        out_specs=[col] * (3 + 2 * (slots - 1)),
        out_shape=[sds((rows, width), bf16)]
        + [sds((rows, width), f32)] * 2
        + [sds((rows, width), bf16)] * (2 * (slots - 1)),
        scratch_shapes=[pltpu.VMEM((keys, rows), f32)],
        cost_estimate=cost(
            20 * pairs * rows * keys * LANES, 2 * rows * width * (7 + 4 * slots), 2 * pairs * rows * keys
        ),
        name="attend_back",
    )(q, grad, *ks, *vs, lse, kpos, qpos, qstart, cosine, sines)
    gq, gk, gv = outs[:3]
    return gq, gk, gv, outs[3 : 2 + slots], outs[2 + slots :]


def middle_body(x_ref, att_ref, wout_ref, gain_ref, mid_ref, nffn_ref):
    middle = x_ref[...].astype(f32) + mm(att_ref[...], wout_ref[...], NN)
    mid_ref[...] = middle
    factor = lax.rsqrt(jnp.mean(middle * middle, axis=-1, keepdims=True) + epsilon)
    nffn_ref[...] = (middle * factor * gain_ref[...]).astype(bf16)


def middle_norm(x, attended, w_out, gain):
    rows, width = x.shape
    return pl.pallas_call(
        middle_body,
        out_shape=[sds((rows, width), f32), sds((rows, width), bf16)],
        cost_estimate=cost(2 * rows * width * width, 2 * width * width + 10 * rows * width),
        name="middle_norm",
    )(x, attended, w_out, gain)


def store_half(edge, keep_ref, send_ref, half, offset, value):
    at = pl.ds(pl.multiple_of(offset * LANES, LANES), LANES)

    @pl.when(half == edge)
    def _():
        keep_ref[:, at] = value

    @pl.when(half != edge)
    def _():
        send_ref[:, at] = value


def ffn_acts_body(
    sizes,
    edge_ref,
    nffn_ref,
    cot_ref,
    wg_ref,
    wu_ref,
    wd_ref,
    hid_ref,
    gg_ref,
    gu_ref,
    hk_ref,
    hs_ref,
    ak_ref,
    as_ref,
    bk_ref,
    bs_ref,
):
    step = pl.program_id(0)
    block = wg_ref.shape[1]
    normed = nffn_ref[...]
    gate = mm(normed, wg_ref[...], NN)
    upward = mm(normed, wu_ref[...], NN)
    grad_hidden = mm(cot_ref[...], wd_ref[...], NT)
    sig = 1.0 / (1.0 + jnp.exp(-gate))
    silu = gate * sig
    hidden = (silu * upward).astype(bf16)
    grad_gate = (grad_hidden * upward * (sig * (1.0 + gate * (1.0 - sig)))).astype(bf16)
    grad_up = (grad_hidden * silu).astype(bf16)
    hid_ref[...] = hidden
    gg_ref[...] = grad_gate
    gu_ref[...] = grad_up
    per = block // LANES
    total, hid_half, a_half, b_half = sizes
    low_edge, high_edge = edge_ref[0], edge_ref[1]
    for i in range(per):
        at = slice(i * LANES, (i + 1) * LANES)
        lane_block = step * per + i
        store_half(
            high_edge, hk_ref, hs_ref, lane_block // hid_half, lane_block % hid_half, hidden[:, at]
        )
        for first, value in ((0, grad_gate), (total, grad_up)):
            place = lane_block + first
            piece = value[:, at]

            @pl.when(place < 2 * a_half)
            def _(place=place, piece=piece):
                store_half(low_edge, ak_ref, as_ref, place // a_half, place % a_half, piece)

            @pl.when(place >= 2 * a_half)
            def _(place=place, piece=piece):
                rest = place - 2 * a_half
                store_half(low_edge, bk_ref, bs_ref, rest // b_half, rest % b_half, piece)


def half_blocks(ff):
    total = ff // LANES
    a_half = (total + 1) // 2 + (total // 2) % 2
    return total, total // 2, a_half, total - a_half


def ffn_acts(edges, nffn, cot, w_gate, w_up, w_down):
    rows, width = nffn.shape
    ff = w_gate.shape[1]
    block = 256
    sizes = half_blocks(ff)
    _, hid_half, a_half, b_half = sizes
    full = whole((rows, width))
    col = pl.BlockSpec((rows, block), lambda j: (0, j))
    widths = [hid_half * LANES] * 2 + [a_half * LANES] * 2 + [b_half * LANES] * 2
    return pl.pallas_call(
        functools.partial(ffn_acts_body, sizes),
        grid=(ff // block,),
        in_specs=[
            scalar(),
            full,
            full,
            pl.BlockSpec((width, block), lambda j: (0, j)),
            pl.BlockSpec((width, block), lambda j: (0, j)),
            pl.BlockSpec((block, width), lambda j: (j, 0)),
        ],
        out_specs=[col] * 3 + [whole((rows, w)) for w in widths],
        out_shape=[sds((rows, ff), bf16)] * 3 + [sds((rows, w), bf16) for w in widths],
        cost_estimate=cost(6 * rows * width * ff, 6 * width * ff + 12 * rows * ff),
        name="ffn_acts",
    )(edges, nffn, cot, w_gate, w_up, w_down)


def ffn_back_body(
    steps,
    seqs,
    edge_ref,
    hid_ref,
    gg_ref,
    gu_ref,
    wg_ref,
    wu_ref,
    wd_ref,
    mid_ref,
    cot_ref,
    wout_ref,
    gain_ref,
    *refs,
):
    out_refs = refs[:seqs]
    gmid_ref, keep_ref, send_ref, gatt_ref, acc_s, gacc_s = refs[seqs:]
    step = pl.program_id(0)

    @pl.when(step == 0)
    def _():
        acc_s[...] = mid_ref[...]
        gacc_s[...] = jnp.zeros_like(gacc_s)

    acc_s[...] += mm(hid_ref[...], wd_ref[...], NN)
    gacc_s[...] += mm(gg_ref[...], wg_ref[...], NT) + mm(gu_ref[...], wu_ref[...], NT)

    @pl.when(step == steps - 1)
    def _():
        length = out_refs[0].shape[0]
        for s in range(seqs):
            out_refs[s][...] = acc_s[s * length : (s + 1) * length].astype(bf16)
        middle = mid_ref[...]
        factor = lax.rsqrt(jnp.mean(middle * middle, axis=-1, keepdims=True) + epsilon)
        scaled = gacc_s[...] * gain_ref[...]
        inner = jnp.mean(scaled * middle, axis=-1, keepdims=True)
        grad_middle = cot_ref[...].astype(f32) + factor * (
            scaled - middle * (factor * factor * inner)
        )
        gmid_ref[...] = grad_middle
        branch = grad_middle.astype(bf16)
        half = branch.shape[1] // 2

        @pl.when(edge_ref[0] == 0)
        def _():
            keep_ref[...] = branch[:, :half]
            send_ref[...] = branch[:, half:]

        @pl.when(edge_ref[0] != 0)
        def _():
            keep_ref[...] = branch[:, half:]
            send_ref[...] = branch[:, :half]

        gatt_ref[...] = mm(branch, wout_ref[...], NT).astype(bf16)


def ffn_back(seqs, edges, hidden, gg, gu, w_gate, w_up, w_down, middle, cot, w_out, gain):
    rows, width = cot.shape
    ff = w_gate.shape[1]
    block = 256
    steps = ff // block
    full = whole((rows, width))
    col = pl.BlockSpec((rows, block), lambda j: (0, j))
    part = whole((rows // seqs, width))
    half = whole((rows, width // 2))
    outs = pl.pallas_call(
        functools.partial(ffn_back_body, steps, seqs),
        grid=(steps,),
        in_specs=[
            scalar(),
            col,
            col,
            col,
            pl.BlockSpec((width, block), lambda j: (0, j)),
            pl.BlockSpec((width, block), lambda j: (0, j)),
            pl.BlockSpec((block, width), lambda j: (j, 0)),
            full,
            full,
            whole((width, width)),
            whole((1, width)),
        ],
        out_specs=[part] * seqs + [full, half, half, full],
        out_shape=[sds((rows // seqs, width), bf16)] * seqs
        + [
            sds((rows, width), f32),
            sds((rows, width // 2), bf16),
            sds((rows, width // 2), bf16),
            sds((rows, width), bf16),
        ],
        scratch_shapes=[pltpu.VMEM((rows, width), f32)] * 2,
        cost_estimate=cost(
            6 * rows * width * ff + 2 * rows * width * width,
            6 * width * ff + 2 * width * width + 6 * rows * ff + 20 * rows * width,
        ),
        name="ffn_back",
    )(edges, hidden, gg, gu, w_gate, w_up, w_down, middle, cot, w_out, gain)
    return outs[:seqs], outs[seqs:]


def grad_pack_body(seqs, received, pairs, edge_ref, *refs):
    gq_ref, gk_ref, gv_ref = refs[:3]
    other_k = refs[3 : 3 + received]
    other_v = refs[3 + received : 3 + 2 * received]
    cos_ref, sin_ref, packed_ref = refs[3 + 2 * received : 6 + 2 * received]
    first_refs = refs[6 + 2 * received : 6 + 2 * received + seqs]
    xk_ref, xs_ref, yk_ref, ys_ref = refs[6 + 2 * received + seqs :]
    step = pl.program_id(0)
    grad_k, grad_v = gk_ref[...], gv_ref[...]
    for r in other_k:
        grad_k = grad_k + r[...].astype(f32)
    for r in other_v:
        grad_v = grad_v + r[...].astype(f32)
    grad_k = (grad_k * cos_ref[...] - turn(grad_k) * sin_ref[...]).astype(bf16)
    grad_v = (0.5 * grad_v).astype(bf16)
    length = first_refs[0].shape[0]
    for s in range(seqs):
        first_refs[s][...] = grad_v[s * length : (s + 1) * length]
    packed = jnp.concatenate([gq_ref[...], grad_k, grad_v], axis=1)
    packed_ref[0] = packed
    quarter = pairs // 4
    part = step // quarter
    at = pl.ds(pl.multiple_of((step % quarter) * packed.shape[1], LANES), packed.shape[1])
    low_edge, high_edge = edge_ref[0], edge_ref[1]
    for color, edge, keep_ref, send_ref in (
        (0, low_edge, xk_ref, xs_ref),
        (1, high_edge, yk_ref, ys_ref),
    ):

        @pl.when(part == 2 * color + edge)
        def _():
            keep_ref[:, at] = packed

        @pl.when(part == 2 * color + 1 - edge)
        def _():
            send_ref[:, at] = packed


def grad_pack(seqs, edges, gq, gk, gv, other_k, other_v, cosine, sines):
    rows, width = gq.shape
    pairs = width // LANES
    received = len(other_k)
    col = pl.BlockSpec((rows, LANES), lambda i: (0, i))
    part = pl.BlockSpec((rows // seqs, LANES), lambda i: (0, i))
    quarter = (rows, pairs // 4 * 3 * LANES)
    outs = pl.pallas_call(
        functools.partial(grad_pack_body, seqs, received, pairs),
        grid=(pairs,),
        in_specs=[scalar()] + [col] * (3 + 2 * received) + [whole((rows, LANES))] * 2,
        out_specs=[pl.BlockSpec((1, rows, 3 * LANES), lambda i: (i, 0, 0))]
        + [part] * seqs
        + [whole(quarter)] * 4,
        out_shape=[sds((pairs, rows, 3 * LANES), bf16)]
        + [sds((rows // seqs, width), bf16)] * seqs
        + [sds(quarter, bf16)] * 4,
        cost_estimate=cost(20 * rows * width, 2 * rows * width * 12),
        name="grad_pack",
    )(edges, gq, gk, gv, *other_k, *other_v, cosine, sines)
    return outs[0], outs[1 : 1 + seqs], outs[1 + seqs :]


def grad_inputs_body(pairs, seqs, packed_ref, wq_ref, wk_ref, wv_ref, x_ref, gain_ref, gmid_ref, *refs):
    out_refs, acc_s = refs[:seqs], refs[seqs]
    step = pl.program_id(0)

    @pl.when(step == 0)
    def _():
        acc_s[...] = jnp.zeros_like(acc_s)

    weights = jnp.concatenate([wq_ref[...], wk_ref[...], wv_ref[...]], axis=1)
    acc_s[...] += mm(packed_ref[0], weights, NT)

    @pl.when(step == pairs - 1)
    def _():
        inputs = x_ref[...].astype(f32)
        factor = lax.rsqrt(jnp.mean(inputs * inputs, axis=-1, keepdims=True) + epsilon)
        scaled = acc_s[...] * gain_ref[...]
        inner = jnp.mean(scaled * inputs, axis=-1, keepdims=True)
        grads = gmid_ref[...] + factor * (scaled - inputs * (factor * factor * inner))
        grads = grads.astype(bf16)
        length = out_refs[0].shape[0]
        for s in range(seqs):
            out_refs[s][...] = grads[s * length : (s + 1) * length]


def grad_inputs(seqs, packed, w_qkv, x, gain, grad_middle):
    rows, width = x.shape
    pairs = width // LANES
    full = whole((rows, width))
    return pl.pallas_call(
        functools.partial(grad_inputs_body, pairs, seqs),
        grid=(pairs,),
        in_specs=[
            pl.BlockSpec((1, rows, 3 * LANES), lambda i: (i, 0, 0)),
            pl.BlockSpec((width, LANES), lambda i: (0, i)),
            pl.BlockSpec((width, LANES), lambda i: (0, pairs + i)),
            pl.BlockSpec((width, LANES), lambda i: (0, 2 * pairs + i)),
            full,
            whole((1, width)),
            full,
        ],
        out_specs=[whole((rows // seqs, width))] * seqs,
        out_shape=[sds((rows // seqs, width), bf16)] * seqs,
        scratch_shapes=[pltpu.VMEM((rows, width), f32)],
        cost_estimate=cost(6 * rows * width * width, 6 * width * width + 16 * rows * width),
        name="grad_inputs",
    )(packed, w_qkv, w_qkv, w_qkv, x, gain, grad_middle)


def place_body(seqs, shift_ref, *refs):
    out_ref = refs[seqs]
    for j in range(seqs):
        for s in range(seqs):

            @pl.when(lax.rem(shift_ref[0] + s, seqs) == j)
            def _(j=j, s=s):
                out_ref[j] = refs[s][...]


def place(parts, seq):
    seqs = len(parts)
    length, width = parts[0].shape
    return pl.pallas_call(
        functools.partial(place_body, seqs),
        in_specs=[scalar()] + [pl.BlockSpec(memory_space=pltpu.VMEM)] * seqs,
        out_specs=pl.BlockSpec(memory_space=pltpu.VMEM),
        out_shape=sds((seqs, length, width), parts[0].dtype),
        cost_estimate=cost(0, 4 * seqs * length * width),
        name="place",
    )(seq[None], *parts)


def outer_body(counts, per, core_ref, *refs):
    keep_ref, send_ref = refs[-2:]
    column = at = 0
    core = core_ref[0]
    for count in counts:
        lefts, rights = refs[at : at + count], refs[at + count : at + 2 * count]
        at += 2 * count
        total = None
        for left, right in zip(lefts, rights):
            part = mm(left[...], right[...], TN)
            total = part if total is None else total + part
        wide = total.shape[1]
        cut = slice(column, column + wide)
        column += wide
        total = total.astype(bf16)
        for i in range(total.shape[0] // (2 * per)):
            even = total[2 * i * per : (2 * i + 1) * per]
            odd = total[(2 * i + 1) * per : (2 * i + 2) * per]

            @pl.when(core == 0)
            def _(i=i, even=even, odd=odd, cut=cut):
                keep_ref[i, :, cut] = even
                send_ref[i, :, cut] = odd

            @pl.when(core != 0)
            def _(i=i, even=even, odd=odd, cut=cut):
                keep_ref[i, :, cut] = odd
                send_ref[i, :, cut] = even


def outer(core, per, *groups):
    rows, height = groups[0][0][0].shape
    width = sum(rights[0].shape[1] for _, rights in groups)
    block = 256 if height % 256 == 0 else height
    specs, args, flops = [], [], 0
    for lefts, rights in groups:
        wide = rights[0].shape[1]
        specs += [pl.BlockSpec((rows, block), lambda i: (0, i))] * len(lefts)
        specs += [whole((rows, wide))] * len(rights)
        args += [*lefts, *rights]
        flops += 2 * len(lefts) * rows * height * wide
    out_spec = pl.BlockSpec((block // (2 * per), per, width), lambda i: (i, 0, 0))
    return pl.pallas_call(
        functools.partial(outer_body, [len(lefts) for lefts, _ in groups], per),
        grid=(height // block,),
        in_specs=[scalar()] + specs,
        out_specs=[out_spec] * 2,
        out_shape=[sds((height // (2 * per), per, width), bf16)] * 2,
        cost_estimate=cost(flops, 2 * (sum(a.size for a in args) + height * width)),
        name="outer",
    )(core[None], *args)


def build(ndp, nblk):
    n = ndp * nblk
    nbits = n.bit_length() - 1
    blk_bits = nblk.bit_length() - 1
    if (1 << nbits) != n or (1 << blk_bits) != nblk:
        raise ValueError("mesh sizes")
    low_e, high_e = blk_bits, nbits - 1

    def send(value, target):
        pairs = [(i, target(i)) for i in range(n)]
        return lax.ppermute(value, AXES, pairs)

    def flip(value, bit):
        return send(value, lambda i: i ^ (1 << bit))

    def pick(value, index, axis=0):
        return lax.dynamic_index_in_dim(value, index, axis, keepdims=False)

    def shards(
        tokens, first_values, docs, cotangent, w_qkv, w_out, w_gate, w_up, w_down, gain_attn, gain_ffn
    ):
        seqs, length, width = tokens.shape
        ff = w_gate.shape[1]
        rows = seqs * length
        group = nblk // seqs
        blk = lax.axis_index("blk")
        index = lax.axis_index("dp") * nblk + blk
        seq, member = blk // group, blk % group

        def bit(t):
            return (index >> t) & 1

        core = bit(0)
        edges = jnp.stack([bit(low_e), bit(high_e)])

        def shift_seq(i, s):
            base, b = i - i % nblk, i % nblk
            return base + ((b // group + s) % seqs) * group + b % group

        def shift_member(i, s):
            base, b = i - i % nblk, i % nblk
            return base + (b // group) * group + (b % group + s) % group

        def to_sequence(value):
            parts = [pick(value, seq)]
            for s in range(1, seqs):
                out = pick(value, (seq + s) % seqs)
                parts.append(send(out, lambda i, s=s: shift_seq(i, s)))
            return parts

        def from_sequence(blocks):
            return [
                part if s == 0 else send(part, lambda i, s=s: shift_seq(i, -s))
                for s, part in enumerate(blocks)
            ]

        def others(value):
            return [send(value, lambda i, g=g: shift_member(i, g)) for g in range(1, group)]

        marks = jnp.pad(docs[:, None, :].astype(bf16), ((0, 0), (0, 7), (0, width - length)))
        token_parts = to_sequence(jnp.concatenate([tokens, marks], axis=1))
        first_parts = to_sequence(first_values)
        cot_parts = to_sequence(cotangent)
        x = jnp.concatenate([p[:length] for p in token_parts], axis=0)
        qdocs = jnp.concatenate([p[length, :length] for p in token_parts]).astype(jnp.int32)[None]

        base = jnp.arange(length, dtype=jnp.int32)
        qpos = jnp.concatenate(
            [(((seq - s) % seqs) * group + member) * length + base for s in range(seqs)]
        )
        kpos = jnp.concatenate(
            [
                (((seq - s) % seqs) * group + (member - g) % group) * length + base
                for g in range(group)
                for s in range(seqs)
            ]
        )
        half = HEAD_DIM // 2
        inverse = 10000.0 ** (-jnp.arange(half, dtype=f32) / half)
        angles = qpos.astype(f32)[:, None] * inverse[None, :]
        cos_half, sin_half = jnp.cos(angles), jnp.sin(angles)
        cosine = jnp.concatenate([cos_half] * 4, axis=1)
        sines = jnp.concatenate([-sin_half, sin_half] * 2, axis=1)
        qpos, kpos = qpos[None, :], kpos[:, None]
        gain_a, gain_f = gain_attn[None, :], gain_ffn[None, :]

        x, cosine, sines, qpos, kpos = tie(x, cosine, sines, qpos, kpos)
        normed, q, k = query_key(x, gain_a, w_qkv, cosine, sines)
        other_docs = others(qdocs)
        ks = [k] + others(k)
        normed_x = flip(normed, low_e)
        normed_y = flip(normed, high_e)
        all_docs = jnp.concatenate([qdocs] + other_docs, axis=1)
        qstart = jnp.sum((all_docs[0][:, None] < qdocs).astype(jnp.int32), axis=0, keepdims=True)
        first = jnp.concatenate(first_parts, axis=0)
        ks, first, qstart = tie(ks, first, qstart)
        v = value_mix(normed, w_qkv, first)
        vs = [v] + others(v)
        attended, lse = attend(q, ks, vs, kpos, qpos, qstart)
        attended, normed_x, normed_y, cot_parts = tie(attended, normed_x, normed_y, cot_parts)
        cot = jnp.concatenate(cot_parts, axis=0)
        attended_x = flip(attended, low_e)
        cot_y = flip(cot, high_e)
        middle, nffn = middle_norm(x, attended, w_out, gain_f)
        nffn_x = flip(nffn, low_e)
        hidden, gg, gu, hk, hs, ak, a_s, bk, bs = ffn_acts(edges, nffn, cot, w_gate, w_up, w_down)
        hidden, gg, gu, hs, a_s, bs, attended_x, cot_y = tie(
            hidden, gg, gu, hs, a_s, bs, attended_x, cot_y
        )
        h_y = flip(hs, high_e)
        a_x = flip(a_s, low_e)
        out_blocks, (grad_mid, gbk, gbs, grad_att) = ffn_back(
            seqs, edges, hidden, gg, gu, w_gate, w_up, w_down, middle, cot, w_out, gain_f
        )
        out_blocks, gbs, grad_att, nffn_x = tie(out_blocks, gbs, grad_att, nffn_x)
        out_parts = from_sequence(out_blocks)
        gq, gk, gv, other_k, other_v = attend_back(
            q, grad_att, ks, vs, lse, kpos, qpos, qstart, cosine, sines
        )
        gq, gk, gv, other_k, other_v, out_parts, h_y = tie(
            gq, gk, gv, other_k, other_v, out_parts, h_y
        )
        b_x = flip(bs, low_e)
        gb_x = flip(gbs, low_e)
        got_k = [send(v, lambda i, g=g: shift_member(i, -g)) for g, v in enumerate(other_k, 1)]
        got_v = [send(v, lambda i, g=g: shift_member(i, -g)) for g, v in enumerate(other_v, 1)]
        per_down = ff // n
        per = width // n
        dk, ds = outer(core, per_down, ([hk, h_y], [cot, cot_y]))
        dk, ds, got_k, got_v = tie(dk, ds, got_k, got_v)
        d_c = flip(ds, 0)
        packed, first_blocks, (qxk, qxs, qyk, qys) = grad_pack(
            seqs, edges, gq, gk, gv, got_k, got_v, cosine, sines
        )
        q_x = flip(qxs, low_e)
        q_y = flip(qys, high_e)

        def reduce_rows(keep, got, top, skip):
            dims = (2,) * top + keep.shape[1:]
            value = keep.reshape(dims).astype(f32) + got.reshape(dims).astype(f32)
            left = list(range(top, 0, -1))
            order = [t for t in left if t >= blk_bits and t != skip]
            order += list(range(1, min(blk_bits, top + 1)))
            for t in order:
                axis = left.index(t)
                b = bit(t)
                other = flip(pick(value, 1 - b, axis).astype(bf16), t)
                value = pick(value, b, axis) + other.astype(f32)
                left.pop(axis)
            return value

        def reduce_columns(keep, got, e):
            value = reduce_rows(keep, got, nbits - 1, e)
            b = bit(e)
            mine = pick(value, b)
            other = flip(pick(value, 1 - b).astype(bf16), e).astype(f32)
            return jnp.stack([jnp.where(b == 0, mine, other), jnp.where(b == 0, other, mine)])

        ak2, as2 = outer(core, per, ([nffn, nffn_x], [ak, a_x]))
        a_c = flip(as2, 0)
        grad_down = reduce_rows(dk, d_c, nbits - 2, -1)
        a_done = reduce_columns(ak2, a_c, low_e)
        bk2, bs2 = outer(
            core, per, ([nffn, nffn_x], [bk, b_x]), ([attended, attended_x], [gbk, gb_x])
        )
        b_c = flip(bs2, 0)
        b_done = reduce_columns(bk2, b_c, low_e)
        grad_x = grad_inputs(seqs, packed, w_qkv, x, gain_a, grad_mid)
        qxk2, qxs2 = outer(core, per, ([normed, normed_x], [qxk, q_x]))
        qyk2, qys2 = outer(core, per, ([normed, normed_y], [qyk, q_y]))
        qx_c, qy_c = flip(qxs2, 0), flip(qys2, 0)
        qx_done = reduce_columns(qxk2, qx_c, low_e)
        qy_done = reduce_columns(qyk2, qy_c, high_e)
        first_out = from_sequence(first_blocks)
        token_out = from_sequence(grad_x)
        output = place(out_parts, seq)
        grad_first_values = place(first_out, seq)
        grad_tokens = place(token_out, seq)

        _, _, a_half, b_half = half_blocks(ff)
        b_wide = b_half * LANES
        acts = jnp.concatenate(
            [a_done[0], a_done[1], b_done[0, :, :b_wide], b_done[1, :, :b_wide]], axis=1
        )
        grad_gate, grad_up = acts[:, :ff], acts[:, ff:]
        grad_out = jnp.concatenate([b_done[0, :, b_wide:], b_done[1, :, b_wide:]], axis=1)
        pairs = width // LANES
        grad_qkv = jnp.concatenate([qx_done, qy_done], axis=0)
        grad_qkv = grad_qkv.reshape(4, per, pairs // 4, 3, LANES)
        grad_qkv = jnp.transpose(grad_qkv, (1, 3, 0, 2, 4)).reshape(per, 3 * width)

        def own(value):
            return lax.dynamic_slice_in_dim(value, index * per, per, 0)

        grad_gain_attn = jnp.sum(grad_qkv * own(w_qkv).astype(f32), axis=1) / own(gain_attn)
        grad_gain_ffn = (
            jnp.sum(
                grad_gate * own(w_gate).astype(f32) + grad_up * own(w_up).astype(f32), axis=1
            )
            / own(gain_ffn)
        )
        return (
            output,
            grad_tokens,
            grad_first_values,
            grad_qkv,
            grad_out,
            grad_gate,
            grad_up,
            grad_down,
            grad_gain_attn,
            grad_gain_ffn,
        )

    return shards


def solution(mesh):
    seq = P("dp", "blk", None)
    rows = P(AXES, None)
    vec = P(AXES)
    in_specs = (seq, seq, P("dp", "blk"), seq) + (P(),) * 7
    out_specs = (seq, seq, seq, rows, rows, rows, rows, rows, vec, vec)
    return jax.shard_map(
        build(mesh.shape["dp"], mesh.shape["blk"]),
        mesh=mesh,
        in_specs=in_specs,
        out_specs=out_specs,
        check_vma=False,
    )
```

time: 422 us -> 328 us (0.78)
  waiting for transfers between devices: 170 us -> 97.7 us
  local copies, waits for them, and re-layouts: 53.6 us -> 13.3 us
  Pallas kernels: 96.9 us -> 123 us
  blocking collectives: 17.9 us -> 0 us
  other arithmetic: 17.3 us -> 25.8 us
  starting transfers between devices: 59.4 us -> 65 us
    ppermute x74 -> x58, waiting for transfers between devices: 170 us -> 97.7 us  [send(): return lax.ppermute(value, AXES, pairs)]
    pallas_call x9 -> x15, Pallas kernels: 72.9 us -> 99.1 us  [the longest x5 28.4 us: outer(): pl.pallas_call(functools.partial(outer_body, [len(lefts) for lefts, _ in...]
    squeeze x35 -> x3, local copies, waits for them, and re-layouts: 24.4 us -> 0.12 us  [pick(): return lax.dynamic_index_in_dim(value, index, axis, keepdims=False)]
    all_gather x1 -> x0, blocking collectives: 17.9 us -> none  [shards(): docs_all = lax.all_gather(docs, 'blk', axis=1, tiled=True)]
    add x2 -> x22, other arithmetic: 0.01 us -> 11.2 us  [the longest x5 5.81 us: reduce_rows(): value = keep.reshape(dims).astype(f32) + got.reshape(dims).astype(f32)]
    dynamic_update_slice x12 -> x0, local copies, waits for them, and re-layouts: 7.37 us -> none  [from_sequence(): result = lax.dynamic_update_index_in_dim(result, part, (seq + s) % seqs, 0)]
    ppermute x74 -> x58, starting transfers between devices: 59.4 us -> 65 us  [send(): return lax.ppermute(value, AXES, pairs)]
    dynamic_slice x7 -> x0, local copies, waits for them, and re-layouts: 5.5 us -> none  [pick(): return lax.dynamic_index_in_dim(value, index, axis, keepdims=False)]
  transfers between devices with their start and end apart: 74 -> 58, of which waited for: 26 -> 19; matrix products, arithmetic and copies ran while one was open for 15% -> 8% of each run, Pallas kernels for 21% -> 35%
where the time goes in v2:
time: 328 us; the launch traced here: 326 us
  Pallas kernels  123 us (38%)
  waiting for transfers between devices  97.7 us (30%)
  starting transfers between devices  65 us (20%)
  other arithmetic  25.8 us (8%)
  local copies, waits for them, and re-layouts  13.3 us (4%)
    ppermute x58, waiting for transfers between devices, send(): return lax.ppermute(value, AXES, pairs)  97.7 us
    ppermute x58, starting transfers between devices, send(): return lax.ppermute(value, AXES, pairs)  65 us
    pallas_call x5, Pallas kernels, outer(): pl.pallas_call(functools.partial(outer_body, [len(lefts) for lefts, _ in...  28.4 us
    pallas_call x1, Pallas kernels, ffn_back(): pl.pallas_call(functools.partial(ffn_back_body, steps, seqs), grid=(steps...  17.3 us
    pallas_call x1, Pallas kernels, ffn_acts(): pl.pallas_call(functools.partial(ffn_acts_body, sizes), grid=(ff // block...  16.7 us
    pallas_call x1, Pallas kernels, attend_back(): pl.pallas_call(functools.partial(attend_back_body, slots), grid=(pairs,),...  12.2 us
    pallas_call x1, Pallas kernels, attend(): pl.pallas_call(functools.partial(attend_body, slots), grid=(pairs,), in_s...  11.6 us
    pallas_call x1, Pallas kernels, grad_inputs(): pl.pallas_call(functools.partial(grad_inputs_body, pairs, seqs), grid=(pa...  9.41 us
  transfers between devices with their start and end apart: 58, of which 19 were waited for; matrix products, arithmetic and copies ran while one was open for 8% of the time, Pallas kernels for 35%

profile of v2, /device:TPU:0, one launch (start us, length us, event | category | flops | bytes accessed | tf_op | source)
XLA Modules:
  0.0 326.4 jit_solution(9583194010900943869)
XLA Ops:
  18.6 7.8 %collective-permute-done.5 = bf16[64,1024]{1,0:T(8,128)(2,1)S(1)} collective-permute-done((bf16[64,1024]{1,0:T(8,128)(2,1)S(1)}, bf16[64,1024]{1,0:T(8,128)(2,1)S(1)}, u32[]{:S(2)}, u32[]{:S(2)}) %collective-permute-start.5) | collective-permute-done | bytes 131104 | tf_op jit(solution)/shard_map/ppermute | solution.py:685
  27.4 5.2 %collective-permute-done.2 = bf16[72,1024]{1,0:T(8,128)(2,1)S(1)} collective-permute-done((bf16[72,1024]{1,0:T(8,128)(2,1)S(1)}, bf16[72,1024]{1,0:T(8,128)(2,1)S(1)}, u32[]{:S(2)}, u32[]{:S(2)}) %collective-permute-start.2) | collective-permute-done | bytes 147488 | tf_op jit(solution)/shard_map/ppermute | solution.py:685
  33.4 6.2 %query_key.1 = (bf16[256,1024]{1,0:T(8,128)(2,1)}, bf16[256,1024]{1,0:T(8,128)(2,1)}, bf16[256,1024]{1,0:T(8,128)(2,1)}) custom-call(bf16[256,1024]{1,0:T(8,128)(2,1)} %pad_maximum_fusion.x_ref, f32[1,1024]{1,0:T(1,128)} %bitcast.155, bf16[1024,3072]{1,0:T(8,128)(2,1)} %wv_ref.1, f32[256,128]{1,0:T(8,128)} %pad_maximum_fusion.5.cos_ref.refs_10_.refs_5_, ...), custom_call_target="tpu_custom_call" | custom-call | flops 322122560 | bytes 1887436 | tf_op jit(solution)/shard_map/query_key/pallas_call | solution.py:101
  56.9 11.6 %attend.1 = (bf16[256,1024]{1,0:T(8,128)(2,1)}, f32[8,2,256]{2,1,0:T(2,128)}) custom-call(bf16[256,1024]{1,0:T(8,128)(2,1)} %get-tuple-element.110.refs_0_, bf16[256,1024]{1,0:T(8,128)(2,1)} %get-tuple-element.112.refs_1_.refs_2_, bf16[256,1024]{1,0:T(8,128)(2,1)} %copy-done.7, bf16[256,1024]{1,0:T(8,128)(2,1)} %value_mix.1.refs_3_.refs_4_, ...), custom_call_target="tpu_custom_call" | custom-call | flops 322122560 | bytes 943718 | tf_op jit(solution)/shard_map/attend/pallas_call | solution.py:182
  75.1 16.7 %ffn_acts.1 = (bf16[256,2816]{1,0:T(8,128)(2,1)}, bf16[256,2816]{1,0:T(8,128)(2,1)}, bf16[256,2816]{1,0:T(8,128)(2,1)}, bf16[256,1408]{1,0:T(8,128)(2,1)}, bf16[...) custom-call(s32[2]{0:T(128)} %pad_add_fusion.2.edge_ref, ...), custom_call_target="tpu_custom_call" | custom-call | flops 1328755456 | bytes 7785676 | tf_op jit(solution)/shard_map/ffn_acts/pallas_call | solution.py:372
  96.1 17.3 %ffn_back.1 = (bf16[64,1024]{1,0:T(8,128)(2,1)}, bf16[64,1024]{1,0:T(8,128)(2,1)}, bf16[64,1024]{1,0:T(8,128)(2,1)}, bf16[64,1024]{1,0:T(8,128)(2,1)}, f32[256,1...) custom-call(s32[2]{0:T(128)} %pad_add_fusion.2.edge_ref, ...), custom_call_target="tpu_custom_call" | custom-call | flops 1489816832 | bytes 8690073 | tf_op jit(solution)/shard_map/ffn_back/pallas_call | solution.py:456
  113.5 8.4 %collective-permute-done.16.refs_1_ = bf16[256,1024]{1,0:T(8,128)(2,1)S(1)} collective-permute-done((bf16[256,1024]{1,0:T(8,128)(2,1)S(1)}, bf16[256,1024]{1,0:T(8,128)(2,1)S(1)}, u32[]{:S(2)}, u32[]{:S(2)}) %collective-permute-start.16) | collective-permute-done | bytes 524320 | tf_op jit(solution)/shard_map/ppermute | solution.py:685
  123.0 5.8 %outer.9 = (bf16[16,32,1536]{2,1,0:T(8,128)(2,1)}, bf16[16,32,1536]{2,1,0:T(8,128)(2,1)}) custom-call(s32[1]{0:T(128)} %bitcast.27.core_ref, bf16[256,1024]{1,0:T(8,128)(2,1)} %get-tuple-element.121.nffn_ref.refs_0_, bf16[256,1024]{1,0:T(8,128)(2,1)} %copy-done.9, bf16[256,1536]{1,0:T(8,128)(2,1)} %get-tuple-element.198.refs_2_, bf16[256,1536]{1,0:T(8,128)(2,1)} %copy-done.16), custom_call_target="tpu_custom_call" | custom-call | flops 483183808 | bytes 1730150 | tf_op jit(solution)/shard_map/outer/pallas_call | solution.py:664
  130.9 4.5 %collective-permute-done.17.refs_1_ = bf16[64,1024]{1,0:T(8,128)(2,1)S(1)} collective-permute-done((bf16[64,1024]{1,0:T(8,128)(2,1)S(1)}, bf16[64,1024]{1,0:T(8,128)(2,1)S(1)}, u32[]{:S(2)}, u32[]{:S(2)}) %collective-permute-start.17) | collective-permute-done | bytes 131104 | tf_op jit(solution)/shard_map/ppermute | solution.py:685
  136.9 12.2 %attend_back.1 = (bf16[256,1024]{1,0:T(8,128)(2,1)}, f32[256,1024]{1,0:T(8,128)}, f32[256,1024]{1,0:T(8,128)}, bf16[256,1024]{1,0:T(8,128)(2,1)}, bf16[256,1024]{1,0:T(8,128)(2,1)}) custom-call(bf16[256,1024]{1,0:T(8,128)(2,1)} %get-tuple-element.110.refs_0_, bf16[256,1024]{1,0:T(8,128)(2,1)} %get-tuple-element.142.refs_1_, ...), custom_call_target="tpu_custom_call" | custom-call | flops 805306368 | bytes 2359296 | tf_op jit(solution)/shard_map/attend_back/pallas_call | solution.py:250
  150.3 5.3 %outer.5 = (bf16[8,88,1024]{2,1,0:T(8,128)(2,1)}, bf16[8,88,1024]{2,1,0:T(8,128)(2,1)}) custom-call(s32[1]{0:T(128)} %bitcast.27.core_ref, bf16[256,1408]{1,0:T(8,128)(2,1)} %get-tuple-element.161.refs_0_, bf16[256,1408]{1,0:T(8,128)(2,1)} %copy-done.17, bf16[256,1024]{1,0:T(8,128)(2,1)} %copy-done.2, bf16[256,1024]{1,0:T(8,128)(2,1)} %copy-done.26), custom_call_target="tpu_custom_call" | custom-call | flops 442918496 | bytes 1612185 | tf_op jit(solution)/shard_map/outer/pallas_call | solution.py:664
  156.5 7.4 %grad_pack.1 = (bf16[8,256,384]{2,1,0:T(8,128)(2,1)}, bf16[64,1024]{1,0:T(8,128)(2,1)}, bf16[64,1024]{1,0:T(8,128)(2,1)}, bf16[64,1024]{1,0:T(8,128)(2,1)}, bf16...) custom-call(s32[2]{0:T(128)} %pad_add_fusion.2.edge_ref, ...), custom_call_target="tpu_custom_call" | custom-call | flops 1572864 | bytes 1887436 | tf_op jit(solution)/shard_map/grad_pack/pallas_call | solution.py:535
  170.2 9.4 %grad_inputs.1 = (bf16[64,1024]{1,0:T(8,128)(2,1)}, bf16[64,1024]{1,0:T(8,128)(2,1)}, bf16[64,1024]{1,0:T(8,128)(2,1)}, bf16[64,1024]{1,0:T(8,128)(2,1)}) custom-call(bf16[8,256,384]{2,1,0:T(8,128)(2,1)} %get-tuple-element.170.packed_ref, bf16[1024,3072]{1,0:T(8,128)(2,1)} %wv_ref.1, bf16[1024,3072]{1,0:T(8,128)(2,1)} %wv_ref.1, bf16[1024,3072]{1,0:T(8,128)(2,1)} %wv_ref.1, ...), custom_call_target="tpu_custom_call" | custom-call | flops 483183808 | bytes 3145728 | tf_op jit(solution)/shard_map/grad_inputs/pallas_call | solution.py:579
  179.7 4.3 %collective-permute-start.23 = (bf16[64,1024]{1,0:T(8,128)(2,1)}, bf16[64,1024]{1,0:T(8,128)(2,1)S(1)}, u32[]{:S(2)}, u32[]{:S(2)}) collective-permute-start(bf16[64,1024]{1,0:T(8,128)(2,1)} %get-tuple-element.173), channel_id=1, source_target_pairs={{0,6},{1,7},{2,0},{3,1},{4,2},{5,3},{6,4},{7,5},{8,14},{9,15},{10,... | collective-permute-start | bytes 393224 | tf_op jit(solution)/shard_map/ppermute | solution.py:685
  188.1 4.7 %collective-permute-start.25 = (bf16[64,1024]{1,0:T(8,128)(2,1)}, bf16[64,1024]{1,0:T(8,128)(2,1)S(1)}, u32[]{:S(2)}, u32[]{:S(2)}) collective-permute-start(bf16[64,1024]{1,0:T(8,128)(2,1)} %get-tuple-element.175), channel_id=1, source_target_pairs={{0,2},{1,3},{2,4},{3,5},{4,6},{5,7},{6,0},{7,1},{8,10},{9,11},{10,... | collective-permute-start | bytes 393224 | tf_op jit(solution)/shard_map/ppermute | solution.py:685
  192.8 7.9 %outer.8 = (bf16[16,32,1792]{2,1,0:T(8,128)(2,1)}, bf16[16,32,1792]{2,1,0:T(8,128)(2,1)}) custom-call(s32[1]{0:T(128)} %bitcast.27.core_ref, bf16[256,1024]{1,0:T(8,128)(2,1)} %get-tuple-element.121.nffn_ref.refs_0_, bf16[256,1024]{1,0:T(8,128)(2,1)} %copy-done.9, bf16[256,1280]{1,0:T(8,128)(2,1)} %get-tuple-element.191.refs_2_, ...), custom_call_target="tpu_custom_call" | custom-call | flops 563714432 | bytes 2280652 | tf_op jit(solution)/shard_map/outer/pallas_call | solution.py:664
  208.6 4.8 %outer.6 = (bf16[16,32,768]{2,1,0:T(8,128)(2,1)}, bf16[16,32,768]{2,1,0:T(8,128)(2,1)}) custom-call(s32[1]{0:T(128)} %bitcast.27.core_ref, bf16[256,1024]{1,0:T(8,128)(2,1)} %get-tuple-element.114.normed_ref.refs_0_, bf16[256,1024]{1,0:T(8,128)(2,1)} %copy-done.25, bf16[256,768]{1,0:T(8,128)(2,1)} %get-tuple-element.181.refs_2_, bf16[256,768]{1,0:T(8,128)(2,1)} %copy-done.27), custom_call_target="tpu_custom_call" | custom-call | flops 241591904 | bytes 1022361 | tf_op jit(solution)/shard_map/outer/pallas_call | solution.py:664
  213.9 4.7 %outer.7 = (bf16[16,32,768]{2,1,0:T(8,128)(2,1)}, bf16[16,32,768]{2,1,0:T(8,128)(2,1)}) custom-call(s32[1]{0:T(128)} %bitcast.27.core_ref, bf16[256,1024]{1,0:T(8,128)(2,1)} %get-tuple-element.114.normed_ref.refs_0_, bf16[256,1024]{1,0:T(8,128)(2,1)} %copy-done.24, bf16[256,768]{1,0:T(8,128)(2,1)} %get-tuple-element.186.refs_2_, ...), custom_call_target="tpu_custom_call" | custom-call | flops 241591904 | bytes 1022361 | tf_op jit(solution)/shard_map/outer/pallas_call | solution.py:664
  233.5 16.0 %collective-permute-done.31 = bf16[2,2,2,32,768]{4,3,0,1,2:T(8,128)(2,1)S(1)} collective-permute-done((bf16[2,2,2,32,768]{4,3,0,1,2:T(8,128)(2,1)S(1)}, bf16[2,2,2,32,768]{4,3,0,1,2:T(8,128)(2,1)S(1)}, u32[]{:S(2)}, u32[]{:S(2)}) %collective-permute-start.31) | collective-permute-done | bytes 393248 | tf_op jit(solution)/shard_map/ppermute | solution.py:685
  251.9 5.6 %collective-permute-done.32 = bf16[2,2,32,768]{3,2,0,1:T(8,128)(2,1)S(1)} collective-permute-done((bf16[2,2,32,768]{3,2,0,1:T(8,128)(2,1)S(1)}, bf16[2,2,32,768]{3,2,0,1:T(8,128)(2,1)S(1)}, u32[]{:S(2)}, u32[]{:S(2)}) %collective-permute-start.32) | collective-permute-done | bytes 196640 | tf_op jit(solution)/shard_map/ppermute | solution.py:685
  261.1 5.6 %collective-permute-done.33 = bf16[2,32,768]{2,1,0:T(8,128)(2,1)S(1)} collective-permute-done((bf16[2,32,768]{2,1,0:T(8,128)(2,1)S(1)}, bf16[2,32,768]{2,1,0:T(8,128)(2,1)S(1)}, u32[]{:S(2)}, u32[]{:S(2)}) %collective-permute-start.33) | collective-permute-done | bytes 98336 | tf_op jit(solution)/shard_map/ppermute | solution.py:685
  286.3 7.7 %collective-permute-done.52 = bf16[2,32,1536]{2,1,0:T(8,128)(2,1)S(1)} collective-permute-done((bf16[2,32,1536]{2,1,0:T(8,128)(2,1)S(1)}, bf16[2,32,1536]{2,1,0:T(8,128)(2,1)S(1)}, u32[]{:S(2)}, u32[]{:S(2)}) %collective-permute-start.52) | collective-permute-done | bytes 196640 | tf_op jit(solution)/shard_map/ppermute | solution.py:685
  298.7 8.0 %collective-permute-done.45 = bf16[2,2,32,1792]{3,2,0,1:T(8,128)(2,1)S(1)} collective-permute-done((bf16[2,2,32,1792]{3,2,0,1:T(8,128)(2,1)S(1)}, bf16[2,2,32,1792]{3,2,0,1:T(8,128)(2,1)S(1)}, u32[]{:S(2)}, u32[]{:S(2)}) %collective-permute-start.45) | collective-permute-done | bytes 458784 | tf_op jit(solution)/shard_map/ppermute | solution.py:685
  306.9 10.5 %collective-permute-done.46 = bf16[2,32,1792]{2,1,0:T(8,128)(2,1)S(1)} collective-permute-done((bf16[2,32,1792]{2,1,0:T(8,128)(2,1)S(1)}, bf16[2,32,1792]{2,1,0:T(8,128)(2,1)S(1)}, u32[]{:S(2)}, u32[]{:S(2)}) %collective-permute-start.46) | collective-permute-done | bytes 229408 | tf_op jit(solution)/shard_map/ppermute | solution.py:685
  (286 shorter events, 127.2 us)
Async XLA Ops:
  2.6 24.7 %collective-permute-start = (bf16[72,1024]{1,0:T(8,128)(2,1)S(1)}, bf16[72,1024]{1,0:T(8,128)(2,1)S(1)}, u32[]{:S(2)}, u32[]{:S(2)}) collective-permute-start(bf16[72,1024]{1,0:T(8,128)(2,1)S(1)} %get-tuple-element.212), channel_id=1, source_target_pairs={{0,2},{1,3},{2,4},{3,5},{4,6},{5,7},{6,0},{7,1},{8,10},{9,11},{10,... | collective-permute-start | bytes 442376 | tf_op jit(solution)/shard_map/ppermute | solution.py:685
  5.7 21.6 %collective-permute-start.1 = (bf16[72,1024]{1,0:T(8,128)(2,1)S(1)}, bf16[72,1024]{1,0:T(8,128)(2,1)S(1)}, u32[]{:S(2)}, u32[]{:S(2)}) collective-permute-start(bf16[72,1024]{1,0:T(8,128)(2,1)S(1)} %get-tuple-element.211), channel_id=1, source_target_pairs={{0,4},{1,5},{2,6},{3,7},{4,0},{5,1},{6,2},{7,3},{8,12},{9,13},{10,... | collective-permute-start | bytes 442376 | tf_op jit(solution)/shard_map/ppermute | solution.py:685
  46.1 22.5 %collective-permute-start.10 = (bf16[256,1024]{1,0:T(8,128)(2,1)S(1)}, bf16[256,1024]{1,0:T(8,128)(2,1)S(1)}, u32[]{:S(2)}, u32[]{:S(2)}) collective-permute-start(bf16[256,1024]{1,0:T(8,128)(2,1)S(1)} %copy-done.5), channel_id=1, source_target_pairs={{0,16},{1,17},{2,18},{3,19},{4,20},{5,21},{6,22},{7,23},{8,24},{9,... | collective-permute-start | bytes 1572872 | tf_op jit(solution)/shard_map/ppermute | solution.py:685
  47.6 21.0 %collective-permute-start.9 = (bf16[256,1024]{1,0:T(8,128)(2,1)S(1)}, bf16[256,1024]{1,0:T(8,128)(2,1)S(1)}, u32[]{:S(2)}, u32[]{:S(2)}) collective-permute-start(bf16[256,1024]{1,0:T(8,128)(2,1)S(1)} %copy-done.5), channel_id=1, source_target_pairs={{0,8},{1,9},{2,10},{3,11},{4,12},{5,13},{6,14},{7,15},{8,0},{9,1},... | collective-permute-start | bytes 1572872 | tf_op jit(solution)/shard_map/ppermute | solution.py:685
  49.1 19.4 %collective-permute-start.11 = (bf16[64,1024]{1,0:T(8,128)(2,1)S(1)}, bf16[64,1024]{1,0:T(8,128)(2,1)S(1)}, u32[]{:S(2)}, u32[]{:S(2)}) collective-permute-start(bf16[64,1024]{1,0:T(8,128)(2,1)S(1)} %get-tuple-element.216), channel_id=1, source_target_pairs={{0,2},{1,3},{2,4},{3,5},{4,6},{5,7},{6,0},{7,1},{8,10},{9,11},{10,... | collective-permute-start | bytes 393224 | tf_op jit(solution)/shard_map/ppermute | solution.py:685
  69.6 22.2 %collective-permute-start.15 = (bf16[256,1024]{1,0:T(8,128)(2,1)S(1)}, bf16[256,1024]{1,0:T(8,128)(2,1)S(1)}, u32[]{:S(2)}, u32[]{:S(2)}) collective-permute-start(bf16[256,1024]{1,0:T(8,128)(2,1)S(1)} %constant_dynamic-update-slice_fusion.cot_ref.refs_2_), channel_id=1, source_target_pairs={{0,16},{1,17},{2,18},{3,19},{4,20},{5,21},{6,22},{7,23},{8,24},{9,... | collective-permute-start | bytes 1572872 | tf_op jit(solution)/shard_map/ppermute | solution.py:685
  70.1 21.7 %collective-permute-start.14 = (bf16[256,1024]{1,0:T(8,128)(2,1)}, bf16[256,1024]{1,0:T(8,128)(2,1)S(1)}, u32[]{:S(2)}, u32[]{:S(2)}) collective-permute-start(bf16[256,1024]{1,0:T(8,128)(2,1)} %get-tuple-element.120.att_ref.refs_4_), channel_id=1, source_target_pairs={{0,8},{1,9},{2,10},{3,11},{4,12},{5,13},{6,14},{7,15},{8,0},{9,1},... | collective-permute-start | bytes 1572872 | tf_op jit(solution)/shard_map/ppermute | solution.py:685
  92.6 29.3 %collective-permute-start.48 = (bf16[256,1536]{1,0:T(8,128)(2,1)}, bf16[256,1536]{1,0:T(8,128)(2,1)S(1)}, u32[]{:S(2)}, u32[]{:S(2)}) collective-permute-start(bf16[256,1536]{1,0:T(8,128)(2,1)} %get-tuple-element.199), channel_id=1, source_target_pairs={{0,8},{1,9},{2,10},{3,11},{4,12},{5,13},{6,14},{7,15},{8,0},{9,1},... | collective-permute-start | bytes 2359304 | tf_op jit(solution)/shard_map/ppermute | solution.py:685
  94.1 27.8 %collective-permute-start.16 = (bf16[256,1024]{1,0:T(8,128)(2,1)S(1)}, bf16[256,1024]{1,0:T(8,128)(2,1)S(1)}, u32[]{:S(2)}, u32[]{:S(2)}) collective-permute-start(bf16[256,1024]{1,0:T(8,128)(2,1)S(1)} %copy-done.6), channel_id=1, source_target_pairs={{0,8},{1,9},{2,10},{3,11},{4,12},{5,13},{6,14},{7,15},{8,0},{9,1},... | collective-permute-start | bytes 1572872 | tf_op jit(solution)/shard_map/ppermute | solution.py:685
  94.6 54.6 %collective-permute-start.20 = (bf16[256,1408]{1,0:T(8,128)(2,1)}, bf16[256,1408]{1,0:T(8,128)(2,1)S(1)}, u32[]{:S(2)}, u32[]{:S(2)}) collective-permute-start(bf16[256,1408]{1,0:T(8,128)(2,1)} %get-tuple-element.153), channel_id=1, source_target_pairs={{0,16},{1,17},{2,18},{3,19},{4,20},{5,21},{6,22},{7,23},{8,24},{9,... | collective-permute-start | bytes 2162696 | tf_op jit(solution)/shard_map/ppermute | solution.py:685
  128.8 89.8 %collective-permute-start.49 = (bf16[16,32,1536]{2,1,0:T(8,128)(2,1)}, bf16[16,32,1536]{2,1,0:T(8,128)(2,1)}, u32[]{:S(2)}, u32[]{:S(2)}) collective-permute-start(bf16[16,32,1536]{2,1,0:T(8,128)(2,1)} %get-tuple-element.201), channel_id=1, source_target_pairs={{0,1},{1,0},{2,3},{3,2},{4,5},{5,4},{6,7},{7,6},{8,9},{9,8},{10,11... | collective-permute-start | bytes 4718600 | tf_op jit(solution)/shard_map/ppermute | solution.py:685
  129.2 20.0 %collective-permute-start.18 = (bf16[64,1024]{1,0:T(8,128)(2,1)}, bf16[64,1024]{1,0:T(8,128)(2,1)S(1)}, u32[]{:S(2)}, u32[]{:S(2)}) collective-permute-start(bf16[64,1024]{1,0:T(8,128)(2,1)} %get-tuple-element.151), channel_id=1, source_target_pairs={{0,4},{1,5},{2,6},{3,7},{4,0},{5,1},{6,2},{7,3},{8,12},{9,13},{10,... | collective-permute-start | bytes 393224 | tf_op jit(solution)/shard_map/ppermute | solution.py:685
  135.4 32.2 %collective-permute-start.41 = (bf16[256,1280]{1,0:T(8,128)(2,1)}, bf16[256,1280]{1,0:T(8,128)(2,1)S(1)}, u32[]{:S(2)}, u32[]{:S(2)}) collective-permute-start(bf16[256,1280]{1,0:T(8,128)(2,1)} %get-tuple-element.192), channel_id=1, source_target_pairs={{0,8},{1,9},{2,10},{3,11},{4,12},{5,13},{6,14},{7,15},{8,0},{9,1},... | collective-permute-start | bytes 1966088 | tf_op jit(solution)/shard_map/ppermute | solution.py:685
  166.0 41.8 %collective-permute-start.29 = (bf16[256,768]{1,0:T(8,128)(2,1)}, bf16[256,768]{1,0:T(8,128)(2,1)S(1)}, u32[]{:S(2)}, u32[]{:S(2)}) collective-permute-start(bf16[256,768]{1,0:T(8,128)(2,1)} %get-tuple-element.182), channel_id=1, source_target_pairs={{0,8},{1,9},{2,10},{3,11},{4,12},{5,13},{6,14},{7,15},{8,0},{9,1},... | collective-permute-start | bytes 1179656 | tf_op jit(solution)/shard_map/ppermute | solution.py:685
  167.6 46.3 %collective-permute-start.35 = (bf16[256,768]{1,0:T(8,128)(2,1)}, bf16[256,768]{1,0:T(8,128)(2,1)}, u32[]{:S(2)}, u32[]{:S(2)}) collective-permute-start(bf16[256,768]{1,0:T(8,128)(2,1)} %get-tuple-element.187), channel_id=1, source_target_pairs={{0,16},{1,17},{2,18},{3,19},{4,20},{5,21},{6,22},{7,23},{8,24},{9,... | collective-permute-start | bytes 1179656 | tf_op jit(solution)/shard_map/ppermute | solution.py:685
  200.7 25.7 %collective-permute-start.43 = (bf16[16,32,1792]{2,1,0:T(8,128)(2,1)}, bf16[16,32,1792]{2,1,0:T(8,128)(2,1)S(1)}, u32[]{:S(2)}, u32[]{:S(2)}) collective-permute-start(bf16[16,32,1792]{2,1,0:T(8,128)(2,1)} %get-tuple-element.197), channel_id=1, source_target_pairs={{0,1},{1,0},{2,3},{3,2},{4,5},{5,4},{6,7},{7,6},{8,9},{9,8},{10,11... | collective-permute-start | bytes 5505032 | tf_op jit(solution)/shard_map/ppermute | solution.py:685
  204.9 24.2 %collective-permute-start.54 = (bf16[8,88,1024]{2,1,0:T(8,128)(2,1)}, bf16[8,88,1024]{2,1,0:T(8,128)(2,1)}, u32[]{:S(2)}, u32[]{:S(2)}) collective-permute-start(bf16[8,88,1024]{2,1,0:T(8,128)(2,1)} %get-tuple-element.203), channel_id=1, source_target_pairs={{0,1},{1,0},{2,3},{3,2},{4,5},{5,4},{6,7},{7,6},{8,9},{9,8},{10,11... | collective-permute-start | bytes 4325384 | tf_op jit(solution)/shard_map/ppermute | solution.py:685
  220.6 49.4 %collective-permute-start.50 = (bf16[2,2,2,32,1536]{4,3,0,1,2:T(8,128)(2,1)S(1)}, bf16[2,2,2,32,1536]{4,3,0,1,2:T(8,128)(2,1)S(1)}, u32[]{:S(2)}, u32[]{:S(2)}) collective-permute-start(bf16[2,2,2,32,1536]{4,3,0,1,2:T(8,128)(2,1)S(1)} %fusion.2), channel_id=1, source_target_pairs={{0,16},{1,17},{2,18},{3,19},{4,20},{5,21},{6,22},{7,23},{8,24},{9,... | collective-permute-start | bytes 2359304 | tf_op jit(solution)/shard_map/ppermute | solution.py:685
  223.6 25.9 %collective-permute-start.31 = (bf16[2,2,2,32,768]{4,3,0,1,2:T(8,128)(2,1)S(1)}, bf16[2,2,2,32,768]{4,3,0,1,2:T(8,128)(2,1)S(1)}, u32[]{:S(2)}, u32[]{:S(2)}) collective-permute-start(bf16[2,2,2,32,768]{4,3,0,1,2:T(8,128)(2,1)S(1)} %fusion.7), channel_id=1, source_target_pairs={{0,16},{1,17},{2,18},{3,19},{4,20},{5,21},{6,22},{7,23},{8,24},{9,... | collective-permute-start | bytes 1179656 | tf_op jit(solution)/shard_map/ppermute | solution.py:685
  224.9 24.8 %collective-permute-start.37 = (bf16[2,2,2,32,768]{4,3,0,1,2:T(8,128)(2,1)S(1)}, bf16[2,2,2,32,768]{4,3,0,1,2:T(8,128)(2,1)S(1)}, u32[]{:S(2)}, u32[]{:S(2)}) collective-permute-start(bf16[2,2,2,32,768]{4,3,0,1,2:T(8,128)(2,1)S(1)} %fusion.8), channel_id=1, source_target_pairs={{0,8},{1,9},{2,10},{3,11},{4,12},{5,13},{6,14},{7,15},{8,0},{9,1},... | collective-permute-start | bytes 1179656 | tf_op jit(solution)/shard_map/ppermute | solution.py:685
  228.1 52.9 %collective-permute-start.44 = (bf16[2,2,2,32,1792]{4,3,0,1,2:T(8,128)(2,1)}, bf16[2,2,2,32,1792]{4,3,0,1,2:T(8,128)(2,1)}, u32[]{:S(2)}, u32[]{:S(2)}) collective-permute-start(bf16[2,2,2,32,1792]{4,3,0,1,2:T(8,128)(2,1)} %fusion.1), channel_id=1, source_target_pairs={{0,16},{1,17},{2,18},{3,19},{4,20},{5,21},{6,22},{7,23},{8,24},{9,... | collective-permute-start | bytes 2752520 | tf_op jit(solution)/shard_map/ppermute | solution.py:685
  232.3 45.4 %collective-permute-start.55 = (bf16[2,2,88,1024]{3,2,0,1:T(8,128)(2,1)}, bf16[2,2,88,1024]{3,2,0,1:T(8,128)(2,1)}, u32[]{:S(2)}, u32[]{:S(2)}) collective-permute-start(bf16[2,2,88,1024]{3,2,0,1:T(8,128)(2,1)} %fusion.3), channel_id=1, source_target_pairs={{0,8},{1,9},{2,10},{3,11},{4,12},{5,13},{6,14},{7,15},{8,0},{9,1},... | collective-permute-start | bytes 2162696 | tf_op jit(solution)/shard_map/ppermute | solution.py:685
  284.8 21.8 %collective-permute-start.45 = (bf16[2,2,32,1792]{3,2,0,1:T(8,128)(2,1)S(1)}, bf16[2,2,32,1792]{3,2,0,1:T(8,128)(2,1)S(1)}, u32[]{:S(2)}, u32[]{:S(2)}) collective-permute-start(bf16[2,2,32,1792]{3,2,0,1:T(8,128)(2,1)S(1)} %fusion.5), channel_id=1, source_target_pairs={{0,2},{1,3},{2,0},{3,1},{4,6},{5,7},{6,4},{7,5},{8,10},{9,11},{10,... | collective-permute-start | bytes 1376264 | tf_op jit(solution)/shard_map/ppermute | solution.py:685
  297.4 21.6 %collective-permute-start.57 = (bf16[88,1024]{1,0:T(8,128)(2,1)S(1)}, bf16[88,1024]{1,0:T(8,128)(2,1)S(1)}, u32[]{:S(2)}, u32[]{:S(2)}) collective-permute-start(bf16[88,1024]{1,0:T(8,128)(2,1)S(1)} %fusion.16), channel_id=1, source_target_pairs={{0,4},{1,5},{2,6},{3,7},{4,0},{5,1},{6,2},{7,3},{8,12},{9,13},{10,... | collective-permute-start | bytes 540680 | tf_op jit(solution)/shard_map/ppermute | solution.py:685
  (74 other events, 668.6 us)

commit v3 on v2

v3 whole, which is shorter than its diff:
```python
import functools

import jax
import jax.numpy as jnp
from jax import lax
from jax.experimental import pallas as pl
from jax.experimental.pallas import tpu as pltpu
from jax.sharding import PartitionSpec as P

HEAD_DIM = 64
LANES = 128
AXES = ("dp", "blk")
epsilon = 1e-06
score_scale = 0.125
cost_share = 0.3
VMEM_LIMIT = 16 << 20
bf16 = jnp.bfloat16
f32 = jnp.float32

NN = (((1,), (0,)), ((), ()))
NT = (((1,), (1,)), ((), ()))
TN = (((0,), (0,)), ((), ()))


def mm(a, b, dims):
    return lax.dot_general(a, b, dims, preferred_element_type=f32)


def sds(shape, dtype):
    return jax.ShapeDtypeStruct(shape, dtype)


def cost(flops, nbytes, trans=0):
    return pl.CostEstimate(
        flops=int(flops * cost_share), bytes_accessed=int(nbytes * cost_share), transcendentals=0
    )


def whole(shape):
    return pl.BlockSpec(shape, lambda *_: (0,) * len(shape))


def scalar():
    return pl.BlockSpec(memory_space=pltpu.SMEM)


RESIDENT = pl.BlockSpec(memory_space=pltpu.VMEM)


def lanes(step, width):
    return pl.ds(pl.multiple_of(step * width, width), width)


def resident_call(body, ins, outs, name, flops, scratch=(), scalars=1):
    nbytes = sum(a.size * a.dtype.itemsize for a in (*ins, *outs))
    return pl.pallas_call(
        body,
        in_specs=[scalar()] * scalars + [RESIDENT] * (len(ins) - scalars),
        out_specs=[RESIDENT] * len(outs),
        out_shape=list(outs),
        scratch_shapes=list(scratch),
        compiler_params=pltpu.CompilerParams(vmem_limit_bytes=VMEM_LIMIT),
        cost_estimate=cost(flops, nbytes),
        name=name,
    )(*ins)


def tie(*values):
    return lax.optimization_barrier(values)


def lane_half(shape):
    lane = lax.broadcasted_iota(jnp.int32, shape, len(shape) - 1)
    return (lane & (HEAD_DIM - 1)) < HEAD_DIM // 2


def turn(values):
    half = HEAD_DIM // 2
    return jnp.where(
        lane_half(values.shape),
        pltpu.roll(values, LANES - half, 1),
        pltpu.roll(values, half, 1),
    )


def head_mask(shape, head):
    lane = lax.broadcasted_iota(jnp.int32, shape, 1)
    return lane < HEAD_DIM if head == 0 else lane >= HEAD_DIM


def rotate_all(projected, cosine, sines):
    parts = []
    for i in range(projected.shape[1] // LANES):
        part = projected[:, i * LANES : (i + 1) * LANES]
        parts.append((part * cosine + turn(part) * sines).astype(bf16))
    return jnp.concatenate(parts, axis=1)


def query_key_body(x_ref, gain_ref, w_ref, cos_ref, sin_ref, normed_ref, q_ref, k_ref):
    inputs = x_ref[...].astype(f32)
    factor = lax.rsqrt(jnp.mean(inputs * inputs, axis=-1, keepdims=True) + epsilon)
    normed = (inputs * factor * gain_ref[...]).astype(bf16)
    normed_ref[...] = normed
    width = q_ref.shape[1]
    block = 256
    for j in range(2 * width // block):
        at = slice(j * block, (j + 1) * block)
        rotated = rotate_all(mm(normed, w_ref[:, at], NN), cos_ref[...], sin_ref[...])
        if j * block < width:
            q_ref[:, at] = rotated
        else:
            k_ref[:, slice(j * block - width, (j + 1) * block - width)] = rotated


def query_key(x, gain, w_qkv, cosine, sines):
    rows, width = x.shape
    return resident_call(
        query_key_body,
        (x, gain, w_qkv, cosine, sines),
        [sds((rows, width), bf16)] * 3,
        "query_key",
        4 * rows * width * width,
        scalars=0,
    )


def value_mix_body(normed_ref, w_ref, first_ref, out_ref):
    width = out_ref.shape[1]
    block = 256
    for j in range(width // block):
        at = slice(j * block, (j + 1) * block)
        projected = mm(normed_ref[...], w_ref[:, 2 * width + j * block : 2 * width + (j + 1) * block], NN)
        out_ref[:, at] = (0.5 * projected + 0.5 * first_ref[:, at].astype(f32)).astype(bf16)


def value_mix(normed, w_qkv, first):
    rows, width = normed.shape
    return resident_call(
        value_mix_body,
        (normed, w_qkv, first),
        [sds((rows, width), bf16)],
        "value_mix",
        2 * rows * width * width,
        scalars=0,
    )[0]


def set_bias(bias_ref, kpos_ref, qpos_ref, qstart_ref):
    keys, qpos = kpos_ref[...], qpos_ref[...]
    allowed = (keys <= qpos) & (keys >= qstart_ref[...])
    bias_ref[...] = jnp.where(allowed, 0.0, -1e30)


def attend_body(slots, *refs):
    q_ref = refs[0]
    k_refs = refs[1 : 1 + slots]
    v_refs = refs[1 + slots : 1 + 2 * slots]
    kpos_ref, qpos_ref, qstart_ref, out_ref, lse_ref, bias_ref = refs[1 + 2 * slots :]

    @pl.when(pl.program_id(0) == 0)
    def _():
        set_bias(bias_ref, kpos_ref, qpos_ref, qstart_ref)

    queries = q_ref[...] * jnp.asarray(score_scale, bf16)
    keys = jnp.concatenate([r[...] for r in k_refs], axis=0)
    values = jnp.concatenate([r[...] for r in v_refs], axis=0)
    values_t = jnp.transpose(values)
    outs = []
    for head in range(2):
        own = jnp.where(head_mask(queries.shape, head), queries, jnp.zeros_like(queries))
        scores = mm(keys, own, NT) + bias_ref[...]
        top = jnp.max(scores, axis=0, keepdims=True)
        weights = jnp.exp(scores - top)
        total = jnp.sum(weights, axis=0, keepdims=True)
        probs = (weights * (1.0 / total)).astype(bf16)
        outs.append(mm(values_t[head * HEAD_DIM : (head + 1) * HEAD_DIM], probs, NN))
        lse_ref[0, head : head + 1, :] = top + jnp.log(total)
    out_ref[...] = jnp.transpose(jnp.concatenate(outs, axis=0)).astype(bf16)


def attend(q, ks, vs, kpos, qpos, qstart):
    rows, width = q.shape
    slots = len(ks)
    pairs = width // LANES
    keys = slots * rows
    col = pl.BlockSpec((rows, LANES), lambda i: (0, i))
    return pl.pallas_call(
        functools.partial(attend_body, slots),
        grid=(pairs,),
        in_specs=[col]
        + [col] * slots
        + [col] * slots
        + [whole((keys, 1)), whole((1, rows)), whole((1, rows))],
        out_specs=[col, pl.BlockSpec((1, 2, rows), lambda i: (i, 0, 0))],
        out_shape=[sds((rows, width), bf16), sds((pairs, 2, rows), f32)],
        scratch_shapes=[pltpu.VMEM((keys, rows), f32)],
        compiler_params=pltpu.CompilerParams(vmem_limit_bytes=VMEM_LIMIT),
        cost_estimate=cost(
            8 * pairs * rows * keys * LANES, 2 * rows * width * (2 + 2 * slots), 2 * pairs * rows * keys
        ),
        name="attend",
    )(q, *ks, *vs, kpos, qpos, qstart)


def attend_back_body(slots, *refs):
    q_ref, grad_ref = refs[:2]
    k_refs = refs[2 : 2 + slots]
    v_refs = refs[2 + slots : 2 + 2 * slots]
    lse_ref, kpos_ref, qpos_ref, qstart_ref, cos_ref, sin_ref = refs[2 + 2 * slots : 8 + 2 * slots]
    gq_ref, gk_ref, gv_ref = refs[8 + 2 * slots : 11 + 2 * slots]
    other_refs = refs[11 + 2 * slots : 10 + 3 * slots]
    bias_ref = refs[-1]

    @pl.when(pl.program_id(0) == 0)
    def _():
        set_bias(bias_ref, kpos_ref, qpos_ref, qstart_ref)

    queries = q_ref[...] * jnp.asarray(score_scale, bf16)
    grads = grad_ref[...]
    keys = jnp.concatenate([r[...] for r in k_refs], axis=0)
    values = jnp.concatenate([r[...] for r in v_refs], axis=0)
    keys_t = jnp.transpose(keys)
    grad_values = grad_keys = None
    grad_q = []
    for head in range(2):
        mask = head_mask(queries.shape, head)
        own_q = jnp.where(mask, queries, jnp.zeros_like(queries))
        own_g = jnp.where(mask, grads, jnp.zeros_like(grads))
        scores = mm(keys, own_q, NT) + bias_ref[...]
        probs = jnp.exp(scores - lse_ref[0, head : head + 1, :])
        grad_probs = mm(values, own_g, NT)
        delta = jnp.sum(probs * grad_probs, axis=0, keepdims=True)
        grad_scores = (probs * (grad_probs - delta)).astype(bf16)
        part_v = mm(probs.astype(bf16), own_g, NN)
        part_k = mm(grad_scores, own_q, NN)
        grad_values = part_v if grad_values is None else grad_values + part_v
        grad_keys = part_k if grad_keys is None else grad_keys + part_k
        grad_q.append(mm(keys_t[head * HEAD_DIM : (head + 1) * HEAD_DIM], grad_scores, NN))
    grad_q = jnp.transpose(jnp.concatenate(grad_q, axis=0)) * score_scale
    gq_ref[...] = (grad_q * cos_ref[...] - turn(grad_q) * sin_ref[...]).astype(bf16)
    rows = q_ref.shape[0]
    gk_ref[...] = grad_keys[:rows]
    gv_ref[...] = grad_values[:rows]
    for slot in range(1, slots):
        other_refs[slot - 1][0] = grad_keys[slot * rows : (slot + 1) * rows].astype(bf16)
        other_refs[slot - 1][1] = grad_values[slot * rows : (slot + 1) * rows].astype(bf16)


def attend_back(q, grad, ks, vs, lse, kpos, qpos, qstart, cosine, sines):
    rows, width = q.shape
    slots = len(ks)
    pairs = width // LANES
    keys = slots * rows
    col = pl.BlockSpec((rows, LANES), lambda i: (0, i))
    outs = pl.pallas_call(
        functools.partial(attend_back_body, slots),
        grid=(pairs,),
        in_specs=[col, col]
        + [col] * slots
        + [col] * slots
        + [pl.BlockSpec((1, 2, rows), lambda i: (i, 0, 0))]
        + [whole((keys, 1)), whole((1, rows)), whole((1, rows))]
        + [whole((rows, LANES))] * 2,
        out_specs=[col] * 3 + [pl.BlockSpec((2, rows, LANES), lambda i: (0, 0, i))] * (slots - 1),
        out_shape=[sds((rows, width), bf16)]
        + [sds((rows, width), f32)] * 2
        + [sds((2, rows, width), bf16)] * (slots - 1),
        scratch_shapes=[pltpu.VMEM((keys, rows), f32)],
        compiler_params=pltpu.CompilerParams(vmem_limit_bytes=VMEM_LIMIT),
        cost_estimate=cost(
            20 * pairs * rows * keys * LANES, 2 * rows * width * (7 + 4 * slots), 2 * pairs * rows * keys
        ),
        name="attend_back",
    )(q, grad, *ks, *vs, lse, kpos, qpos, qstart, cosine, sines)
    return (*outs[:3], outs[3:])


def middle_body(x_ref, att_ref, wout_ref, gain_ref, mid_ref, nffn_ref):
    middle = x_ref[...].astype(f32) + mm(att_ref[...], wout_ref[...], NN)
    mid_ref[...] = middle
    factor = lax.rsqrt(jnp.mean(middle * middle, axis=-1, keepdims=True) + epsilon)
    nffn_ref[...] = (middle * factor * gain_ref[...]).astype(bf16)


def middle_norm(x, attended, w_out, gain):
    rows, width = x.shape
    return resident_call(
        middle_body,
        (x, attended, w_out, gain),
        [sds((rows, width), f32), sds((rows, width), bf16)],
        "middle_norm",
        2 * rows * width * width,
        scalars=0,
    )


def ffn_acts_body(
    sizes,
    edge_ref,
    nffn_ref,
    cot_ref,
    wg_ref,
    wu_ref,
    wd_ref,
    hid_ref,
    gg_ref,
    gu_ref,
    hk_ref,
    hs_ref,
    ak_ref,
    as_ref,
    bk_ref,
    bs_ref,
):
    total, hid_half, a_half, b_half = sizes
    block = 256
    per = block // LANES
    for step in range(total // per):
        at = slice(step * block, (step + 1) * block)
        gate = mm(nffn_ref[...], wg_ref[:, at], NN)
        upward = mm(nffn_ref[...], wu_ref[:, at], NN)
        grad_hidden = mm(cot_ref[...], wd_ref[at, :], NT)
        sig = 1.0 / (1.0 + jnp.exp(-gate))
        silu = gate * sig
        hid_ref[:, at] = (silu * upward).astype(bf16)
        gg_ref[:, at] = (grad_hidden * upward * (sig * (1.0 + gate * (1.0 - sig)))).astype(bf16)
        gu_ref[:, at] = (grad_hidden * silu).astype(bf16)

    low_edge, high_edge = edge_ref[0], edge_ref[1]

    def halves(edge, keep_ref, send_ref, size, places):
        for half in range(2):
            runs = []
            for offset in range(size):
                source, start = places[half * size + offset]
                if runs and runs[-1][0] is source and runs[-1][2] == start:
                    runs[-1][2] += 1
                else:
                    runs.append([source, start, start + 1, offset])
            for source, start, stop, offset in runs:
                src = slice(start * LANES, stop * LANES)
                dst = slice(offset * LANES, (offset + stop - start) * LANES)

                @pl.when(edge == half)
                def _(source=source, src=src, dst=dst):
                    keep_ref[:, dst] = source[:, src]

                @pl.when(edge != half)
                def _(source=source, src=src, dst=dst):
                    send_ref[:, dst] = source[:, src]

    acts = [(gg_ref, i) for i in range(total)] + [(gu_ref, i) for i in range(total)]
    halves(high_edge, hk_ref, hs_ref, hid_half, [(hid_ref, i) for i in range(total)])
    halves(low_edge, ak_ref, as_ref, a_half, acts[: 2 * a_half])
    halves(low_edge, bk_ref, bs_ref, b_half, acts[2 * a_half :])


def half_blocks(ff):
    total = ff // LANES
    a_half = (total + 1) // 2 + (total // 2) % 2
    return total, total // 2, a_half, total - a_half


def ffn_acts(edges, nffn, cot, w_gate, w_up, w_down):
    rows, width = nffn.shape
    ff = w_gate.shape[1]
    sizes = half_blocks(ff)
    _, hid_half, a_half, b_half = sizes
    widths = [ff] * 3 + [hid_half * LANES] * 2 + [a_half * LANES] * 2 + [b_half * LANES] * 2
    return resident_call(
        functools.partial(ffn_acts_body, sizes),
        (edges, nffn, cot, w_gate, w_up, w_down),
        [sds((rows, w), bf16) for w in widths],
        "ffn_acts",
        6 * rows * width * ff,
    )


def ffn_back_body(
    seqs,
    edge_ref,
    hid_ref,
    gg_ref,
    gu_ref,
    wg_ref,
    wu_ref,
    wd_ref,
    mid_ref,
    cot_ref,
    wout_ref,
    gain_ref,
    *refs,
):
    out_refs = refs[:seqs]
    gmid_ref, keep_ref, send_ref, gatt_ref = refs[seqs:]
    length = out_refs[0].shape[0]
    middle = mid_ref[...]
    grads = mm(gg_ref[...], wg_ref[...], NT) + mm(gu_ref[...], wu_ref[...], NT)
    factor = lax.rsqrt(jnp.mean(middle * middle, axis=-1, keepdims=True) + epsilon)
    scaled = grads * gain_ref[...]
    inner = jnp.mean(scaled * middle, axis=-1, keepdims=True)
    grad_middle = cot_ref[...].astype(f32) + factor * (scaled - middle * (factor * factor * inner))
    gmid_ref[...] = grad_middle
    branch = grad_middle.astype(bf16)
    half = branch.shape[1] // 2

    @pl.when(edge_ref[1] == 0)
    def _():
        keep_ref[...] = branch[:, :half]
        send_ref[...] = branch[:, half:]

    @pl.when(edge_ref[1] != 0)
    def _():
        keep_ref[...] = branch[:, half:]
        send_ref[...] = branch[:, :half]

    gatt_ref[...] = mm(branch, wout_ref[...], NT).astype(bf16)
    out = middle + mm(hid_ref[...], wd_ref[...], NN)
    for s in range(seqs):
        out_refs[s][...] = out[s * length : (s + 1) * length].astype(bf16)


def ffn_back(seqs, edges, hidden, gg, gu, w_gate, w_up, w_down, middle, cot, w_out, gain):
    rows, width = cot.shape
    ff = w_gate.shape[1]
    outs = resident_call(
        functools.partial(ffn_back_body, seqs),
        (edges, hidden, gg, gu, w_gate, w_up, w_down, middle, cot, w_out, gain),
        [sds((rows // seqs, width), bf16)] * seqs
        + [
            sds((rows, width), f32),
            sds((rows, width // 2), bf16),
            sds((rows, width // 2), bf16),
            sds((rows, width), bf16),
        ],
        "ffn_back",
        6 * rows * width * ff + 2 * rows * width * width,
    )
    return outs[:seqs], outs[seqs:]


def grad_pack_body(seqs, received, edge_ref, *refs):
    gq_ref, gk_ref, gv_ref = refs[:3]
    others = refs[3 : 3 + received]
    cos_ref, sin_ref, packed_ref = refs[3 + received : 6 + received]
    first_refs = refs[6 + received : 6 + received + seqs]
    xk_ref, xs_ref, yk_ref, ys_ref = refs[6 + received + seqs :]
    width = gq_ref.shape[1]
    length = first_refs[0].shape[0]
    low_edge, high_edge = edge_ref[0], edge_ref[1]
    pairs = width // LANES
    quarter = pairs // 4
    for pair in range(pairs):
        at = slice(pair * LANES, (pair + 1) * LANES)
        at_v = slice(width + pair * LANES, width + (pair + 1) * LANES)
        grad_k, grad_v = gk_ref[:, at], gv_ref[:, at]
        for r in others:
            grad_k = grad_k + r[0, :, at].astype(f32)
            grad_v = grad_v + r[1, :, at].astype(f32)
        grad_k = (grad_k * cos_ref[...] - turn(grad_k) * sin_ref[...]).astype(bf16)
        grad_v = (0.5 * grad_v).astype(bf16)
        for s in range(seqs):
            first_refs[s][:, at] = grad_v[s * length : (s + 1) * length]
        packed_ref[:, at] = gq_ref[:, at]
        packed_ref[:, at_v] = grad_k
        packed_ref[:, 2 * width + pair * LANES : 2 * width + (pair + 1) * LANES] = grad_v
        packed = jnp.concatenate([gq_ref[:, at], grad_k, grad_v], axis=1)
        color, half = pair // (2 * quarter), pair // quarter % 2
        edge = high_edge if color else low_edge
        keep_ref, send_ref = (yk_ref, ys_ref) if color else (xk_ref, xs_ref)
        dst = slice(pair % quarter * 3 * LANES, (pair % quarter + 1) * 3 * LANES)

        @pl.when(edge == half)
        def _(keep_ref=keep_ref, dst=dst, packed=packed):
            keep_ref[:, dst] = packed

        @pl.when(edge != half)
        def _(send_ref=send_ref, dst=dst, packed=packed):
            send_ref[:, dst] = packed


def grad_pack(seqs, edges, gq, gk, gv, others, cosine, sines):
    rows, width = gq.shape
    outs = resident_call(
        functools.partial(grad_pack_body, seqs, len(others)),
        (edges, gq, gk, gv, *others, cosine, sines),
        [sds((rows, 3 * width), bf16)]
        + [sds((rows // seqs, width), bf16)] * seqs
        + [sds((rows, 3 * width // 4), bf16)] * 4,
        "grad_pack",
        20 * rows * width,
    )
    return outs[0], outs[1 : 1 + seqs], outs[1 + seqs :]


def grad_inputs_body(seqs, packed_ref, w_ref, x_ref, gain_ref, gmid_ref, *refs):
    given, out_refs = refs[: 2 * seqs], refs[2 * seqs :]
    grads = mm(packed_ref[...], w_ref[...], NT)
    inputs = x_ref[...].astype(f32)
    factor = lax.rsqrt(jnp.mean(inputs * inputs, axis=-1, keepdims=True) + epsilon)
    scaled = grads * gain_ref[...]
    inner = jnp.mean(scaled * inputs, axis=-1, keepdims=True)
    grads = gmid_ref[...] + factor * (scaled - inputs * (factor * factor * inner))
    grads = grads.astype(bf16)
    length = out_refs[0].shape[1]
    for s in range(seqs):
        out_refs[s][0] = given[s][...]
        out_refs[s][1] = grads[s * length : (s + 1) * length]
        out_refs[s][2] = given[seqs + s][...]


def grad_inputs(seqs, packed, w_qkv, x, gain, grad_middle, out_blocks, first_blocks):
    rows, width = x.shape
    return resident_call(
        functools.partial(grad_inputs_body, seqs),
        (packed, w_qkv, x, gain, grad_middle, *out_blocks, *first_blocks),
        [sds((3, rows // seqs, width), bf16)] * seqs,
        "grad_inputs",
        6 * rows * width * width,
        scalars=0,
    )


def place_body(seqs, shift_ref, *refs):
    for i, out_ref in enumerate(refs[seqs:]):
        for j in range(seqs):
            for s in range(seqs):

                @pl.when(lax.rem(shift_ref[0] + s, seqs) == j)
                def _(i=i, j=j, s=s, out_ref=out_ref):
                    out_ref[j] = refs[s][i]


def place(parts, seq):
    seqs = len(parts)
    count, length, width = parts[0].shape
    part = pl.BlockSpec((count, length, width // 4), lambda i: (0, 0, i))
    return pl.pallas_call(
        functools.partial(place_body, seqs),
        grid=(4,),
        in_specs=[scalar()] + [part] * seqs,
        out_specs=[pl.BlockSpec((seqs, length, width // 4), lambda i: (0, 0, i))] * count,
        out_shape=[sds((seqs, length, width), bf16)] * count,
        compiler_params=pltpu.CompilerParams(vmem_limit_bytes=VMEM_LIMIT),
        cost_estimate=cost(0, 4 * seqs * count * length * width),
        name="place",
    )(seq[None], *parts)


def outer_body(counts, per, core_ref, *refs):
    keep_ref, send_ref = refs[-2:]
    column = at = 0
    core = core_ref[0]
    for count in counts:
        lefts, rights = refs[at : at + count], refs[at + count : at + 2 * count]
        at += 2 * count
        total = None
        for left, right in zip(lefts, rights):
            part = mm(left[...], right[...], TN)
            total = part if total is None else total + part
        wide = total.shape[1]
        cut = slice(column, column + wide)
        column += wide
        total = total.astype(bf16)
        for i in range(total.shape[0] // (2 * per)):
            even = total[2 * i * per : (2 * i + 1) * per]
            odd = total[(2 * i + 1) * per : (2 * i + 2) * per]

            @pl.when(core == 0)
            def _(i=i, even=even, odd=odd, cut=cut):
                keep_ref[i, :, cut] = even
                send_ref[i, :, cut] = odd

            @pl.when(core != 0)
            def _(i=i, even=even, odd=odd, cut=cut):
                keep_ref[i, :, cut] = odd
                send_ref[i, :, cut] = even


def outer(core, per, *groups):
    rows, height = groups[0][0][0].shape
    width = sum(rights[0].shape[1] for _, rights in groups)
    block = 256 if height % 256 == 0 else height
    specs, args, flops = [], [], 0
    for lefts, rights in groups:
        wide = rights[0].shape[1]
        specs += [pl.BlockSpec((rows, block), lambda i: (0, i))] * len(lefts)
        specs += [whole((rows, wide))] * len(rights)
        args += [*lefts, *rights]
        flops += 2 * len(lefts) * rows * height * wide
    out_spec = pl.BlockSpec((block // (2 * per), per, width), lambda i: (i, 0, 0))
    return pl.pallas_call(
        functools.partial(outer_body, [len(lefts) for lefts, _ in groups], per),
        grid=(height // block,),
        in_specs=[scalar()] + specs,
        out_specs=[out_spec] * 2,
        out_shape=[sds((height // (2 * per), per, width), bf16)] * 2,
        compiler_params=pltpu.CompilerParams(vmem_limit_bytes=VMEM_LIMIT),
        cost_estimate=cost(flops, 2 * (sum(a.size for a in args) + height * width)),
        name="outer",
    )(core[None], *args)


def build(ndp, nblk):
    n = ndp * nblk
    nbits = n.bit_length() - 1
    blk_bits = nblk.bit_length() - 1
    if (1 << nbits) != n or (1 << blk_bits) != nblk:
        raise ValueError("mesh sizes")
    low_e, high_e = blk_bits, nbits - 1

    def send(value, target):
        pairs = [(i, target(i)) for i in range(n)]
        return lax.ppermute(value, AXES, pairs)

    def flip(value, bit):
        return send(value, lambda i: i ^ (1 << bit))

    def pick(value, index, axis=0):
        return lax.dynamic_index_in_dim(value, index, axis, keepdims=False)

    def shards(
        tokens, first_values, docs, cotangent, w_qkv, w_out, w_gate, w_up, w_down, gain_attn, gain_ffn
    ):
        seqs, length, width = tokens.shape
        ff = w_gate.shape[1]
        rows = seqs * length
        group = nblk // seqs
        blk = lax.axis_index("blk")
        index = lax.axis_index("dp") * nblk + blk
        seq, member = blk // group, blk % group

        def bit(t):
            return (index >> t) & 1

        core = bit(0)
        edges = jnp.stack([bit(low_e), bit(high_e)])

        def shift_seq(i, s):
            base, b = i - i % nblk, i % nblk
            return base + ((b // group + s) % seqs) * group + b % group

        def shift_member(i, s):
            base, b = i - i % nblk, i % nblk
            return base + (b // group) * group + (b % group + s) % group

        def to_sequence(value):
            parts = [pick(value, seq)]
            for s in range(1, seqs):
                out = pick(value, (seq + s) % seqs)
                parts.append(send(out, lambda i, s=s: shift_seq(i, s)))
            return parts

        def from_sequence(blocks):
            return [
                part if s == 0 else send(part, lambda i, s=s: shift_seq(i, -s))
                for s, part in enumerate(blocks)
            ]

        def others(value):
            return [send(value, lambda i, g=g: shift_member(i, g)) for g in range(1, group)]

        marks = jnp.pad(docs[:, None, :].astype(bf16), ((0, 0), (0, 7), (0, width - length)))
        parts = to_sequence(jnp.concatenate([tokens, marks, first_values], axis=1))

        base = jnp.arange(length, dtype=jnp.int32)
        qpos = jnp.concatenate(
            [(((seq - s) % seqs) * group + member) * length + base for s in range(seqs)]
        )
        kpos = jnp.concatenate(
            [
                (((seq - s) % seqs) * group + (member - g) % group) * length + base
                for g in range(group)
                for s in range(seqs)
            ]
        )
        half = HEAD_DIM // 2
        inverse = 10000.0 ** (-jnp.arange(half, dtype=f32) / half)
        angles = qpos.astype(f32)[:, None] * inverse[None, :]
        cos_half, sin_half = jnp.cos(angles), jnp.sin(angles)
        cosine = jnp.concatenate([cos_half] * 4, axis=1)
        sines = jnp.concatenate([-sin_half, sin_half] * 2, axis=1)
        qpos, kpos = qpos[None, :], kpos[:, None]
        gain_a, gain_f = gain_attn[None, :], gain_ffn[None, :]

        cosine, sines, qpos, kpos, parts, cotangent = tie(
            cosine, sines, qpos, kpos, parts, cotangent
        )
        x = jnp.concatenate([p[:length] for p in parts], axis=0)
        first = jnp.concatenate([p[-length:] for p in parts], axis=0)
        qdocs = jnp.concatenate([p[length, :length] for p in parts]).astype(jnp.int32)[None]
        normed, q, k = query_key(x, gain_a, w_qkv, cosine, sines)
        other_docs = others(qdocs)
        ks = [k] + others(k)
        cot_parts = to_sequence(cotangent)
        all_docs = jnp.concatenate([qdocs] + other_docs, axis=1)
        qstart = jnp.sum((all_docs[0][:, None] < qdocs).astype(jnp.int32), axis=0, keepdims=True)
        v = value_mix(normed, w_qkv, first)
        normed_x = flip(normed, low_e)
        normed_y = flip(normed, high_e)
        vs = [v] + others(v)
        attended, lse = attend(q, ks, vs, kpos, qpos, qstart)
        attended, normed_x, normed_y, cot_parts = tie(attended, normed_x, normed_y, cot_parts)
        cot = jnp.concatenate(cot_parts, axis=0)
        attended_y = flip(attended, high_e)
        cot_y = flip(cot, high_e)
        middle, nffn = middle_norm(x, attended, w_out, gain_f)
        nffn_x = flip(nffn, low_e)
        hidden, gg, gu, hk, hs, ak, a_s, bk, bs = ffn_acts(edges, nffn, cot, w_gate, w_up, w_down)
        hidden, gg, gu, hs, a_s, bs, nffn_x, cot_y = tie(
            hidden, gg, gu, hs, a_s, bs, nffn_x, cot_y
        )
        h_y = flip(hs, high_e)
        a_x = flip(a_s, low_e)
        out_blocks, (grad_mid, gbk, gbs, grad_att) = ffn_back(
            seqs, edges, hidden, gg, gu, w_gate, w_up, w_down, middle, cot, w_out, gain_f
        )
        gbs, bs, grad_att = tie(gbs, bs, grad_att)
        b_x = flip(bs, low_e)
        gb_y = flip(gbs, high_e)
        gq, gk, gv, other_kv = attend_back(
            q, grad_att, ks, vs, lse, kpos, qpos, qstart, cosine, sines
        )
        gq, gk, gv, other_kv, h_y, a_x = tie(gq, gk, gv, other_kv, h_y, a_x)
        got_kv = [send(v, lambda i, g=g: shift_member(i, -g)) for g, v in enumerate(other_kv, 1)]
        per_down = ff // n
        per = width // n
        dk, ds = outer(core, per_down, ([hk, h_y], [cot, cot_y]))
        dk, ds, got_kv = tie(dk, ds, got_kv)
        d_c = flip(ds, 0)
        packed, first_blocks, (qxk, qxs, qyk, qys) = grad_pack(
            seqs, edges, gq, gk, gv, got_kv, cosine, sines
        )
        packed, first_blocks, qxs, qys, d_c = tie(packed, first_blocks, qxs, qys, d_c)
        q_x = flip(qxs, low_e)
        q_y = flip(qys, high_e)
        blocks = grad_inputs(seqs, packed, w_qkv, x, gain_a, grad_mid, out_blocks, first_blocks)

        class Rows:
            def __init__(self, keep, got, top, skip):
                dims = (2,) * top + keep.shape[1:]
                self.terms = [keep.reshape(dims), got.reshape(dims)]
                self.left = list(range(top, 0, -1))
                self.order = [t for t in self.left if t >= blk_bits and t != skip]
                self.order += list(range(1, min(blk_bits, top + 1)))
                self.skip, self.swapped = skip, False

            def total(self, terms):
                return functools.reduce(lambda a, b: a + b, [t.astype(f32) for t in terms])

            def go(self):
                t = self.order.pop(0)
                axis, b = self.left.index(t), bit(t)
                out = self.total([pick(v, 1 - b, axis) for v in self.terms]).astype(bf16)
                self.terms = [pick(v, b, axis) for v in self.terms] + [flip(out, t)]
                self.left.pop(axis)

            def next(self):
                if self.order:
                    self.go()
                elif self.skip >= 0 and not self.swapped:
                    value, b = self.total(self.terms), bit(self.skip)
                    self.swapped = True
                    out = flip(pick(value, 1 - b).astype(bf16), self.skip)
                    self.terms = [pick(value, b), out]
                else:
                    return False
                return True

            def halves(self):
                mine, other = self.terms[0], self.terms[1].astype(f32)
                b = bit(self.skip)
                return jnp.stack([jnp.where(b == 0, mine, other), jnp.where(b == 0, other, mine)])

        def settle(values, *reductions):
            last = [r.terms[-1] for r in reductions]
            values, last = tie(values, last)
            for r, got in zip(reductions, last):
                r.terms[-1] = got
            return values

        ak2, as2 = outer(core, per, ([nffn, nffn_x], [ak, a_x]))
        blocks, ak2, as2, b_x, gb_y, attended_y = tie(blocks, ak2, as2, b_x, gb_y, attended_y)
        a_c = flip(as2, 0)
        down = Rows(dk, d_c, nbits - 2, -1)
        down.next()
        moved = from_sequence(blocks)
        bk2, bs2 = outer(core, per, ([nffn, nffn_x], [bk, b_x]))
        bk2, bs2, a_c, q_x, q_y = tie(bk2, bs2, a_c, q_x, q_y)
        b_c = flip(bs2, 0)
        part_a = Rows(ak2, a_c, nbits - 1, low_e)
        part_a.next()
        qyk2, qys2 = outer(
            core, per, ([normed, normed_y], [qyk, q_y]), ([attended, attended_y], [gbk, gb_y])
        )
        qyk2, qys2, b_c, moved[1::2] = tie(qyk2, qys2, b_c, moved[1::2])
        qy_c = flip(qys2, 0)
        part_b = Rows(bk2, b_c, nbits - 1, low_e)
        qxk2, qxs2 = outer(core, per, ([normed, normed_x], [qxk, q_x]))
        qxk2, qxs2, qy_c, moved = settle((qxk2, qxs2, qy_c, moved), down)
        qx_c = flip(qxs2, 0)
        part_y = Rows(qyk2, qy_c, nbits - 1, high_e)
        part_b.next()
        down.next()
        part_y.next()
        (qx_c,) = settle((qx_c,), part_a, down)
        part_x = Rows(qxk2, qx_c, nbits - 1, low_e)
        part_a.next()
        part_x.next()
        down.next()
        settle((), part_a, part_b, part_y, down)
        everything = (part_a, part_b, part_y, part_x, down)
        while True:
            busy = [part for part in everything if part.next()]
            if not busy:
                break
            settle((), *busy)
        grad_down = down.total(down.terms)
        a_done, b_done, qx_done, qy_done = (
            part.halves() for part in (part_a, part_b, part_x, part_y)
        )
        output, grad_tokens, grad_first_values = place(moved, seq)

        acts = jnp.concatenate([a_done[0], a_done[1], b_done[0], b_done[1]], axis=1)
        grad_gate, grad_up = acts[:, :ff], acts[:, ff:]
        q_wide = 3 * width // 4
        grad_out = jnp.concatenate([qy_done[0, :, q_wide:], qy_done[1, :, q_wide:]], axis=1)
        qy_done = qy_done[:, :, :q_wide]
        pairs = width // LANES
        grad_qkv = jnp.concatenate([qx_done, qy_done], axis=0)
        grad_qkv = grad_qkv.reshape(4, per, pairs // 4, 3, LANES)
        grad_qkv = jnp.transpose(grad_qkv, (1, 3, 0, 2, 4)).reshape(per, 3 * width)

        def own(value):
            return lax.dynamic_slice_in_dim(value, index * per, per, 0)

        grad_gain_attn = jnp.sum(grad_qkv * own(w_qkv).astype(f32), axis=1) / own(gain_attn)
        grad_gain_ffn = (
            jnp.sum(
                grad_gate * own(w_gate).astype(f32) + grad_up * own(w_up).astype(f32), axis=1
            )
            / own(gain_ffn)
        )
        return (
            output,
            grad_tokens,
            grad_first_values,
            grad_qkv,
            grad_out,
            grad_gate,
            grad_up,
            grad_down,
            grad_gain_attn,
            grad_gain_ffn,
        )

    return shards


def solution(mesh):
    seq = P("dp", "blk", None)
    rows = P(AXES, None)
    vec = P(AXES)
    in_specs = (seq, seq, P("dp", "blk"), seq) + (P(),) * 7
    out_specs = (seq, seq, seq, rows, rows, rows, rows, rows, vec, vec)
    return jax.shard_map(
        build(mesh.shape["dp"], mesh.shape["blk"]),
        mesh=mesh,
        in_specs=in_specs,
        out_specs=out_specs,
        check_vma=False,
    )
```

time: 328 us -> 301 us (0.918)
  Pallas kernels: 123 us -> 71.2 us
  local copies, waits for them, and re-layouts: 13.3 us -> 50.4 us
  waiting for transfers between devices: 97.7 us -> 79.9 us
  other arithmetic: 25.8 us -> 43.1 us
  starting transfers between devices: 65 us -> 53 us
    pallas_call x10 -> x8, Pallas kernels: 70.7 us -> 27.4 us  [the longest x7 23.3 us: resident_call(): pl.pallas_call(body, in_specs=[scalar()] * scalars + [RESIDENT] * (len(in...]
    unnamed x83 -> x186, local copies, waits for them, and re-layouts: 6.13 us -> 47.6 us
    convert_element_type x2 -> x17, other arithmetic: 0.16 us -> 26.9 us  [the longest x15 26.8 us: go(): out = self.total([pick(v, 1 - b, axis) for v in self.terms]).astype(bf16)]
    ppermute x58 -> x48, waiting for transfers between devices: 97.7 us -> 79.9 us  [send(): return lax.ppermute(value, AXES, pairs)]
    ppermute x58 -> x48, starting transfers between devices: 65 us -> 53 us  [send(): return lax.ppermute(value, AXES, pairs)]
    pallas_call x5, Pallas kernels: 28.4 us -> 21.4 us  [outer(): pl.pallas_call(functools.partial(outer_body, [len(lefts) for lefts, _ in...]
    add x20 -> x5, other arithmetic: 11.2 us -> 6.92 us  [total(): return functools.reduce(lambda a, b: a + b, [t.astype(f32) for t in terms])]
    convert_element_type x20 -> x4, local copies, waits for them, and re-layouts: 3.52 us -> 0.07 us  [next(): out = flip(pick(value, 1 - b).astype(bf16), self.skip)]
  transfers between devices with their start and end apart: 58 -> 48, of which waited for: 19 -> 21; matrix products, arithmetic and copies ran while one was open for 8% -> 11% of each run, Pallas kernels for 35% -> 23%
where the time goes in v3:
time: 301 us; the launch traced here: 299 us
  waiting for transfers between devices  79.9 us (27%)
  Pallas kernels  71.2 us (24%)
  starting transfers between devices  53 us (18%)
  local copies, waits for them, and re-layouts  50.4 us (17%)
  other arithmetic  43.1 us (14%)
    ppermute x48, waiting for transfers between devices, send(): return lax.ppermute(value, AXES, pairs)  79.9 us
    ppermute x48, starting transfers between devices, send(): return lax.ppermute(value, AXES, pairs)  53 us
    unnamed x186, local copies, waits for them, and re-layouts  47.6 us
    convert_element_type x15, other arithmetic, go(): out = self.total([pick(v, 1 - b, axis) for v in self.terms]).astype(bf16)  26.8 us
    pallas_call x7, Pallas kernels, resident_call(): pl.pallas_call(body, in_specs=[scalar()] * scalars + [RESIDENT] * (len(in...  23.3 us
    pallas_call x5, Pallas kernels, outer(): pl.pallas_call(functools.partial(outer_body, [len(lefts) for lefts, _ in...  21.4 us
    pallas_call x1, Pallas kernels, attend_back(): pl.pallas_call(functools.partial(attend_back_body, slots), grid=(pairs,),...  11.9 us
    pallas_call x1, Pallas kernels, attend(): pl.pallas_call(functools.partial(attend_body, slots), grid=(pairs,), in_s...  10.5 us
  transfers between devices with their start and end apart: 48, of which 21 were waited for; matrix products, arithmetic and copies ran while one was open for 11% of the time, Pallas kernels for 23%

profile of v3, /device:TPU:0, one launch (start us, length us, event | category | flops | bytes accessed | tf_op | source)
XLA Modules:
  0.0 299.2 jit_solution(10570644961942339176)
XLA Ops:
  2.8 3.1 %collective-permute-start = (bf16[136,1024]{1,0:T(8,128)(2,1)S(1)}, bf16[136,1024]{1,0:T(8,128)(2,1)S(1)}, u32[]{:S(2)}, u32[]{:S(2)}) collective-permute-start(bf16[136,1024]{1,0:T(8,128)(2,1)S(1)} %get-tuple-element.303), channel_id=1, source_target_pairs={{0,2},{1,3},{2,4},{3,5},{4,6},{5,7},{6,0},{7,1},{8,10},{9,11},{10,... | collective-permute-start | bytes 835592 | tf_op jit(solution)/shard_map/ppermute | solution.py:614
  11.0 4.6 %collective-permute-done = bf16[136,1024]{1,0:T(8,128)(2,1)S(1)} collective-permute-done((bf16[136,1024]{1,0:T(8,128)(2,1)S(1)}, bf16[136,1024]{1,0:T(8,128)(2,1)S(1)}, u32[]{:S(2)}, u32[]{:S(2)}) %collective-permute-start) | collective-permute-done | bytes 278560 | tf_op jit(solution)/shard_map/ppermute | solution.py:614
  15.6 11.1 %collective-permute-done.1 = bf16[136,1024]{1,0:T(8,128)(2,1)S(1)} collective-permute-done((bf16[136,1024]{1,0:T(8,128)(2,1)S(1)}, bf16[136,1024]{1,0:T(8,128)(2,1)S(1)}, u32[]{:S(2)}, u32[]{:S(2)}) %collective-permute-start.1) | collective-permute-done | bytes 278560 | tf_op jit(solution)/shard_map/ppermute | solution.py:614
  40.6 7.5 %collective-permute-start.10 = (bf16[64,1024]{1,0:T(8,128)(2,1)}, bf16[64,1024]{1,0:T(8,128)(2,1)S(1)}, u32[]{:S(2)}, u32[]{:S(2)}) collective-permute-start(bf16[64,1024]{1,0:T(8,128)(2,1)} %get-tuple-element.305), channel_id=1, source_target_pairs={{0,6},{1,7},{2,0},{3,1},{4,2},{5,3},{6,4},{7,5},{8,14},{9,15},{10,... | collective-permute-start | bytes 393224 | tf_op jit(solution)/shard_map/ppermute | solution.py:614
  55.3 10.5 %attend.1 = (bf16[256,1024]{1,0:T(8,128)(2,1)S(1)}, f32[8,2,256]{2,1,0:T(2,128)S(1)}) custom-call(bf16[256,1024]{1,0:T(8,128)(2,1)S(1)} %copy-done.9, bf16[256,1024]{1,0:T(8,128)(2,1)S(1)} %copy-done.12, bf16[256,1024]{1,0:T(8,128)(2,1)S(1)} %copy-done.18, bf16[256,1024]{1,0:T(8,128)(2,1)S(1)} %value_mix.1.refs_3_.refs_4_, bf16[256,1024]{1,0:T(8,128)(2,1)S(1)} %copy-done.15, ...), custom_call_target="tpu_custom_call" | custom-call | flops 322122560 | bytes 943718 | tf_op jit(solution)/shard_map/attend/pallas_call | solution.py:187
  77.7 6.6 %ffn_acts.1 = (bf16[256,2816]{1,0:T(8,128)(2,1)S(1)}, bf16[256,2816]{1,0:T(8,128)(2,1)S(1)}, bf16[256,2816]{1,0:T(8,128)(2,1)S(1)}, bf16[256,1408]{1,0:T(8,128)(...) custom-call(s32[2]{0:T(128)S(1)} %pad_add_fusion.2.edge_ref, ...), custom_call_target="tpu_custom_call" | custom-call | flops 1328755456 | bytes 8100252 | tf_op jit(solution)/shard_map/ffn_acts/pallas_call | solution.py:56
  90.7 6.3 %ffn_back.1 = (bf16[64,1024]{1,0:T(8,128)(2,1)S(1)}, bf16[64,1024]{1,0:T(8,128)(2,1)S(1)}, bf16[64,1024]{1,0:T(8,128)(2,1)S(1)}, bf16[64,1024]{1,0:T(8,128)(2,1)...) custom-call(s32[2]{0:T(128)S(1)} %pad_add_fusion.2.edge_ref, ...), custom_call_target="tpu_custom_call" | custom-call | flops 1489816832 | bytes 8376732 | tf_op jit(solution)/shard_map/ffn_back/pallas_call | solution.py:56
  99.7 11.9 %attend_back.1 = (bf16[256,1024]{1,0:T(8,128)(2,1)S(1)}, f32[256,1024]{1,0:T(8,128)S(1)}, f32[256,1024]{1,0:T(8,128)S(1)}, bf16[2,256,1024]{2,1,0:T(8,128)(2,1)}) custom-call(bf16[256,1024]{1,0:T(8,128)(2,1)S(1)} %copy-done.10, bf16[256,1024]{1,0:T(8,128)(2,1)S(1)} %get-tuple-element.186.refs_1_, bf16[256,1024]{1,0:T(8,128)(2,1)S(1)} %copy-done.13, ...), custom_call_target="tpu_custom_call" | custom-call | flops 805306368 | bytes 2359296 | tf_op jit(solution)/shard_map/attend_back/pallas_call | solution.py:255
  117.7 3.1 %outer.5 = (bf16[8,88,1024]{2,1,0:T(8,128)(2,1)S(1)}, bf16[8,88,1024]{2,1,0:T(8,128)(2,1)S(1)}) custom-call(s32[1]{0:T(128)} %bitcast.1.core_ref, bf16[256,1408]{1,0:T(8,128)(2,1)S(1)} %copy-done.50, bf16[256,1408]{1,0:T(8,128)(2,1)S(1)} %copy-done.52, bf16[256,1024]{1,0:T(8,128)(2,1)S(1)} %constant_dynamic-update-slice_fusion.cot_ref.refs_2_, ...), custom_call_target="tpu_custom_call" | custom-call | flops 442918496 | bytes 1612185 | tf_op jit(solution)/shard_map/outer/pallas_call | solution.py:592
  127.3 4.1 %outer.6 = (bf16[16,32,1536]{2,1,0:T(8,128)(2,1)S(1)}, bf16[16,32,1536]{2,1,0:T(8,128)(2,1)S(1)}) custom-call(s32[1]{0:T(128)} %bitcast.1.core_ref, bf16[256,1024]{1,0:T(8,128)(2,1)} %get-tuple-element.168.nffn_ref.refs_0_, bf16[256,1024]{1,0:T(8,128)(2,1)} %collective-permute-done.11.refs_1_, bf16[256,1536]{1,0:T(8,128)(2,1)S(1)} %copy-done.44, ...), custom_call_target="tpu_custom_call" | custom-call | flops 483183808 | bytes 1730150 | tf_op jit(solution)/shard_map/outer/pallas_call | solution.py:592
  138.5 2.8 grad_inputs.1
  145.3 3.9 %outer.7 = (bf16[16,32,1280]{2,1,0:T(8,128)(2,1)S(1)}, bf16[16,32,1280]{2,1,0:T(8,128)(2,1)S(1)}) custom-call(s32[1]{0:T(128)} %bitcast.1.core_ref, bf16[256,1024]{1,0:T(8,128)(2,1)} %get-tuple-element.168.nffn_ref.refs_0_, bf16[256,1024]{1,0:T(8,128)(2,1)} %collective-permute-done.11.refs_1_, bf16[256,1280]{1,0:T(8,128)(2,1)S(1)} %copy-done.54, ...), custom_call_target="tpu_custom_call" | custom-call | flops 402653184 | bytes 1494220 | tf_op jit(solution)/shard_map/outer/pallas_call | solution.py:592
  150.3 4.5 %collective-permute-done.21.refs_3_ = bf16[256,768]{1,0:T(8,128)(2,1)S(1)} collective-permute-done((bf16[256,768]{1,0:T(8,128)(2,1)S(1)}, bf16[256,768]{1,0:T(8,128)(2,1)S(1)}, u32[]{:S(2)}, u32[]{:S(2)}) %collective-permute-start.21) | collective-permute-done | bytes 393248 | tf_op jit(solution)/shard_map/ppermute | solution.py:614
  156.1 3.3 %collective-permute-start.24 = (bf16[3,64,1024]{2,1,0:T(8,128)(2,1)S(1)}, bf16[3,64,1024]{2,1,0:T(8,128)(2,1)S(1)}, u32[]{:S(2)}, u32[]{:S(2)}) collective-permute-start(bf16[3,64,1024]{2,1,0:T(8,128)(2,1)S(1)} %get-tuple-element.253), channel_id=1, source_target_pairs={{0,6},{1,7},{2,0},{3,1},{4,2},{5,3},{6,4},{7,5},{8,14},{9,15},{10,... | collective-permute-start | bytes 1179656 | tf_op jit(solution)/shard_map/ppermute | solution.py:614
  160.0 6.2 %outer.9 = (bf16[16,32,1280]{2,1,0:T(8,128)(2,1)S(1)}, bf16[16,32,1280]{2,1,0:T(8,128)(2,1)}) custom-call(s32[1]{0:T(128)} %bitcast.1.core_ref, bf16[256,1024]{1,0:T(8,128)(2,1)} %get-tuple-element.159.normed_ref.refs_0_, bf16[256,1024]{1,0:T(8,128)(2,1)} %collective-permute-done.7.refs_1_, bf16[256,768]{1,0:T(8,128)(2,1)S(1)} %get-tuple-element.245.refs_2_, ...), custom_call_target="tpu_custom_call" | custom-call | flops 402653184 | bytes 1808793 | tf_op jit(solution)/shard_map/outer/pallas_call | solution.py:592
  167.3 10.8 %collective-permute-done.24.refs_1_ = bf16[3,64,1024]{2,1,0:T(8,128)(2,1)S(1)} collective-permute-done((bf16[3,64,1024]{2,1,0:T(8,128)(2,1)S(1)}, bf16[3,64,1024]{2,1,0:T(8,128)(2,1)S(1)}, u32[]{:S(2)}, u32[]{:S(2)}) %collective-permute-start.24) | collective-permute-done | bytes 393248 | tf_op jit(solution)/shard_map/ppermute | solution.py:614
  188.2 4.2 %outer.8 = (bf16[16,32,768]{2,1,0:T(8,128)(2,1)S(1)}, bf16[16,32,768]{2,1,0:T(8,128)(2,1)}) custom-call(s32[1]{0:T(128)} %bitcast.1.core_ref, bf16[256,1024]{1,0:T(8,128)(2,1)} %get-tuple-element.159.normed_ref.refs_0_, bf16[256,1024]{1,0:T(8,128)(2,1)} %collective-permute-done.6.refs_1_, bf16[256,768]{1,0:T(8,128)(2,1)S(1)} %copy-done.60, ...), custom_call_target="tpu_custom_call" | custom-call | flops 241591904 | bytes 1022361 | tf_op jit(solution)/shard_map/outer/pallas_call | solution.py:592
  193.3 11.6 %collective-permute-done.27.refs_2_ = bf16[3,64,1024]{2,1,0:T(8,128)(2,1)} collective-permute-done((bf16[3,64,1024]{2,1,0:T(8,128)(2,1)}, bf16[3,64,1024]{2,1,0:T(8,128)(2,1)}, u32[]{:S(2)}, u32[]{:S(2)}) %collective-permute-start.27) | collective-permute-done | bytes 393248 | tf_op jit(solution)/shard_map/ppermute | solution.py:614
  212.2 5.0 %collective-permute-done.31 = bf16[2,88,1024]{2,1,0:T(8,128)(2,1)S(1)} collective-permute-done((bf16[2,88,1024]{2,1,0:T(8,128)(2,1)S(1)}, bf16[2,88,1024]{2,1,0:T(8,128)(2,1)S(1)}, u32[]{:S(2)}, u32[]{:S(2)}) %collective-permute-start.31) | collective-permute-done | bytes 360480 | tf_op jit(solution)/shard_map/ppermute | solution.py:614
  228.4 3.9 %collective-permute-done.36 = bf16[88,1024]{1,0:T(8,128)(2,1)} collective-permute-done((bf16[88,1024]{1,0:T(8,128)(2,1)S(1)}, bf16[88,1024]{1,0:T(8,128)(2,1)}, u32[]{:S(2)}, u32[]{:S(2)}) %collective-permute-start.36) | collective-permute-done | bytes 180256 | tf_op jit(solution)/shard_map/ppermute | solution.py:614
  248.7 4.0 %place.1 = (bf16[4,64,1024]{2,1,0:T(8,128)(2,1)}, bf16[4,64,1024]{2,1,0:T(8,128)(2,1)}, bf16[4,64,1024]{2,1,0:T(8,128)(2,1)}) custom-call(s32[1]{0:T(128)} %bitcast.shift_ref, bf16[3,64,1024]{2,1,0:T(8,128)(2,1)S(1)} %get-tuple-element.262.refs_0_, bf16[3,64,1024]{2,1,0:T(8,128)(2,1)S(1)} %copy-done.56, ...), custom_call_target="tpu_custom_call" | custom-call | bytes 943718 | tf_op jit(solution)/shard_map/place/pallas_call | solution.py:538
  252.8 7.5 %collective-permute-done.37 = bf16[2,32,1536]{2,1,0:T(8,128)(2,1)} collective-permute-done((bf16[2,32,1536]{2,1,0:T(8,128)(2,1)}, bf16[2,32,1536]{2,1,0:T(8,128)(2,1)}, u32[]{:S(2)}, u32[]{:S(2)}) %collective-permute-start.37) | collective-permute-done | bytes 196640 | tf_op jit(solution)/shard_map/ppermute | solution.py:614
  276.6 3.5 %collective-permute-done.43 = bf16[2,32,1280]{2,1,0:T(8,128)(2,1)S(1)} collective-permute-done((bf16[2,32,1280]{2,1,0:T(8,128)(2,1)S(1)}, bf16[2,32,1280]{2,1,0:T(8,128)(2,1)S(1)}, u32[]{:S(2)}, u32[]{:S(2)}) %collective-permute-start.43) | collective-permute-done | bytes 163872 | tf_op jit(solution)/shard_map/ppermute | solution.py:614
  280.2 3.1 %collective-permute-done.42 = bf16[2,32,1280]{2,1,0:T(8,128)(2,1)S(1)} collective-permute-done((bf16[2,32,1280]{2,1,0:T(8,128)(2,1)S(1)}, bf16[2,32,1280]{2,1,0:T(8,128)(2,1)S(1)}, u32[]{:S(2)}, u32[]{:S(2)}) %collective-permute-start.42) | collective-permute-done | bytes 163872 | tf_op jit(solution)/shard_map/ppermute | solution.py:614
  (348 shorter events, 154.5 us)
Async XLA Ops:
  5.9 20.8 %collective-permute-start.1 = (bf16[136,1024]{1,0:T(8,128)(2,1)S(1)}, bf16[136,1024]{1,0:T(8,128)(2,1)S(1)}, u32[]{:S(2)}, u32[]{:S(2)}) collective-permute-start(bf16[136,1024]{1,0:T(8,128)(2,1)S(1)} %get-tuple-element.302), channel_id=1, source_target_pairs={{0,4},{1,5},{2,6},{3,7},{4,0},{5,1},{6,2},{7,3},{8,12},{9,13},{10,... | collective-permute-start | bytes 835592 | tf_op jit(solution)/shard_map/ppermute | solution.py:614
  8.5 18.2 %collective-permute-start.2 = (bf16[136,1024]{1,0:T(8,128)(2,1)S(1)}, bf16[136,1024]{1,0:T(8,128)(2,1)S(1)}, u32[]{:S(2)}, u32[]{:S(2)}) collective-permute-start(bf16[136,1024]{1,0:T(8,128)(2,1)S(1)} %get-tuple-element.301), channel_id=1, source_target_pairs={{0,6},{1,7},{2,0},{3,1},{4,2},{5,3},{6,4},{7,5},{8,14},{9,15},{10,... | collective-permute-start | bytes 835592 | tf_op jit(solution)/shard_map/ppermute | solution.py:614
  36.2 29.6 %collective-permute-start.6 = (bf16[256,1024]{1,0:T(8,128)(2,1)}, bf16[256,1024]{1,0:T(8,128)(2,1)}, u32[]{:S(2)}, u32[]{:S(2)}) collective-permute-start(bf16[256,1024]{1,0:T(8,128)(2,1)} %get-tuple-element.159.normed_ref.refs_0_), channel_id=1, source_target_pairs={{0,8},{1,9},{2,10},{3,11},{4,12},{5,13},{6,14},{7,15},{8,0},{9,1},... | collective-permute-start | bytes 1572872 | tf_op jit(solution)/shard_map/ppermute | solution.py:614
  37.7 28.1 %collective-permute-start.7 = (bf16[256,1024]{1,0:T(8,128)(2,1)}, bf16[256,1024]{1,0:T(8,128)(2,1)}, u32[]{:S(2)}, u32[]{:S(2)}) collective-permute-start(bf16[256,1024]{1,0:T(8,128)(2,1)} %get-tuple-element.159.normed_ref.refs_0_), channel_id=1, source_target_pairs={{0,16},{1,17},{2,18},{3,19},{4,20},{5,21},{6,22},{7,23},{8,24},{9,... | collective-permute-start | bytes 1572872 | tf_op jit(solution)/shard_map/ppermute | solution.py:614
  40.6 25.2 %collective-permute-start.10 = (bf16[64,1024]{1,0:T(8,128)(2,1)}, bf16[64,1024]{1,0:T(8,128)(2,1)S(1)}, u32[]{:S(2)}, u32[]{:S(2)}) collective-permute-start(bf16[64,1024]{1,0:T(8,128)(2,1)} %get-tuple-element.305), channel_id=1, source_target_pairs={{0,6},{1,7},{2,0},{3,1},{4,2},{5,3},{6,4},{7,5},{8,14},{9,15},{10,... | collective-permute-start | bytes 393224 | tf_op jit(solution)/shard_map/ppermute | solution.py:614
  65.9 21.7 %collective-permute-start.12 = (bf16[256,1024]{1,0:T(8,128)(2,1)S(1)}, bf16[256,1024]{1,0:T(8,128)(2,1)}, u32[]{:S(2)}, u32[]{:S(2)}) collective-permute-start(bf16[256,1024]{1,0:T(8,128)(2,1)S(1)} %constant_dynamic-update-slice_fusion.cot_ref.refs_2_), channel_id=1, source_target_pairs={{0,16},{1,17},{2,18},{3,19},{4,20},{5,21},{6,22},{7,23},{8,24},{9,... | collective-permute-start | bytes 1572872 | tf_op jit(solution)/shard_map/ppermute | solution.py:614
  69.1 18.5 %collective-permute-start.11 = (bf16[256,1024]{1,0:T(8,128)(2,1)}, bf16[256,1024]{1,0:T(8,128)(2,1)}, u32[]{:S(2)}, u32[]{:S(2)}) collective-permute-start(bf16[256,1024]{1,0:T(8,128)(2,1)} %get-tuple-element.168.nffn_ref.refs_0_), channel_id=1, source_target_pairs={{0,8},{1,9},{2,10},{3,11},{4,12},{5,13},{6,14},{7,15},{8,0},{9,1},... | collective-permute-start | bytes 1572872 | tf_op jit(solution)/shard_map/ppermute | solution.py:614
  87.6 26.9 %collective-permute-start.14 = (bf16[256,1536]{1,0:T(8,128)(2,1)S(1)}, bf16[256,1536]{1,0:T(8,128)(2,1)S(1)}, u32[]{:S(2)}, u32[]{:S(2)}) collective-permute-start(bf16[256,1536]{1,0:T(8,128)(2,1)S(1)} %get-tuple-element.193), channel_id=1, source_target_pairs={{0,8},{1,9},{2,10},{3,11},{4,12},{5,13},{6,14},{7,15},{8,0},{9,1},... | collective-permute-start | bytes 2359304 | tf_op jit(solution)/shard_map/ppermute | solution.py:614
  89.1 24.5 %collective-permute-start.13 = (bf16[256,1408]{1,0:T(8,128)(2,1)S(1)}, bf16[256,1408]{1,0:T(8,128)(2,1)S(1)}, u32[]{:S(2)}, u32[]{:S(2)}) collective-permute-start(bf16[256,1408]{1,0:T(8,128)(2,1)S(1)} %get-tuple-element.192), channel_id=1, source_target_pairs={{0,16},{1,17},{2,18},{3,19},{4,20},{5,21},{6,22},{7,23},{8,24},{9,... | collective-permute-start | bytes 2162696 | tf_op jit(solution)/shard_map/ppermute | solution.py:614
  123.6 19.7 %collective-permute-start.17 = (bf16[256,1280]{1,0:T(8,128)(2,1)S(1)}, bf16[256,1280]{1,0:T(8,128)(2,1)S(1)}, u32[]{:S(2)}, u32[]{:S(2)}) collective-permute-start(bf16[256,1280]{1,0:T(8,128)(2,1)S(1)} %copy-done.80), channel_id=1, source_target_pairs={{0,8},{1,9},{2,10},{3,11},{4,12},{5,13},{6,14},{7,15},{8,0},{9,1},... | collective-permute-start | bytes 1966088 | tf_op jit(solution)/shard_map/ppermute | solution.py:614
  124.1 17.1 %collective-permute-start.19 = (bf16[256,1024]{1,0:T(8,128)(2,1)S(1)}, bf16[256,1024]{1,0:T(8,128)(2,1)S(1)}, u32[]{:S(2)}, u32[]{:S(2)}) collective-permute-start(bf16[256,1024]{1,0:T(8,128)(2,1)S(1)} %copy-done.24), channel_id=1, source_target_pairs={{0,16},{1,17},{2,18},{3,19},{4,20},{5,21},{6,22},{7,23},{8,24},{9,... | collective-permute-start | bytes 1572872 | tf_op jit(solution)/shard_map/ppermute | solution.py:614
  124.7 18.7 %collective-permute-start.18 = (bf16[256,512]{1,0:T(8,128)(2,1)S(1)}, bf16[256,512]{1,0:T(8,128)(2,1)S(1)}, u32[]{:S(2)}, u32[]{:S(2)}) collective-permute-start(bf16[256,512]{1,0:T(8,128)(2,1)S(1)} %copy-done.82), channel_id=1, source_target_pairs={{0,16},{1,17},{2,18},{3,19},{4,20},{5,21},{6,22},{7,23},{8,24},{9,... | collective-permute-start | bytes 786440 | tf_op jit(solution)/shard_map/ppermute | solution.py:614
  156.1 23.5 %collective-permute-start.23 = (bf16[16,32,1280]{2,1,0:T(8,128)(2,1)S(1)}, bf16[16,32,1280]{2,1,0:T(8,128)(2,1)S(1)}, u32[]{:S(2)}, u32[]{:S(2)}) collective-permute-start(bf16[16,32,1280]{2,1,0:T(8,128)(2,1)S(1)} %get-tuple-element.252), channel_id=1, source_target_pairs={{0,1},{1,0},{2,3},{3,2},{4,5},{5,4},{6,7},{7,6},{8,9},{9,8},{10,11... | collective-permute-start | bytes 3932168 | tf_op jit(solution)/shard_map/ppermute | solution.py:614
  156.1 22.0 %collective-permute-start.24 = (bf16[3,64,1024]{2,1,0:T(8,128)(2,1)S(1)}, bf16[3,64,1024]{2,1,0:T(8,128)(2,1)S(1)}, u32[]{:S(2)}, u32[]{:S(2)}) collective-permute-start(bf16[3,64,1024]{2,1,0:T(8,128)(2,1)S(1)} %get-tuple-element.253), channel_id=1, source_target_pairs={{0,6},{1,7},{2,0},{3,1},{4,2},{5,3},{6,4},{7,5},{8,14},{9,15},{10,... | collective-permute-start | bytes 1179656 | tf_op jit(solution)/shard_map/ppermute | solution.py:614
  159.4 19.5 %collective-permute-start.25 = (bf16[3,64,1024]{2,1,0:T(8,128)(2,1)S(1)}, bf16[3,64,1024]{2,1,0:T(8,128)(2,1)S(1)}, u32[]{:S(2)}, u32[]{:S(2)}) collective-permute-start(bf16[3,64,1024]{2,1,0:T(8,128)(2,1)S(1)} %get-tuple-element.254), channel_id=1, source_target_pairs={{0,2},{1,3},{2,4},{3,5},{4,6},{5,7},{6,0},{7,1},{8,10},{9,11},{10,... | collective-permute-start | bytes 1179656 | tf_op jit(solution)/shard_map/ppermute | solution.py:614
  180.6 24.3 %collective-permute-start.26 = (bf16[16,32,1280]{2,1,0:T(8,128)(2,1)}, bf16[16,32,1280]{2,1,0:T(8,128)(2,1)}, u32[]{:S(2)}, u32[]{:S(2)}) collective-permute-start(bf16[16,32,1280]{2,1,0:T(8,128)(2,1)} %get-tuple-element.255), channel_id=1, source_target_pairs={{0,1},{1,0},{2,3},{3,2},{4,5},{5,4},{6,7},{7,6},{8,9},{9,8},{10,11... | collective-permute-start | bytes 3932168 | tf_op jit(solution)/shard_map/ppermute | solution.py:614
  182.9 22.0 %collective-permute-start.28 = (bf16[2,2,88,1024]{3,2,1,0:T(8,128)(2,1)}, bf16[2,2,88,1024]{3,2,1,0:T(8,128)(2,1)}, u32[]{:S(2)}, u32[]{:S(2)}) collective-permute-start(bf16[2,2,88,1024]{3,2,1,0:T(8,128)(2,1)} %fusion.6), channel_id=1, source_target_pairs={{0,8},{1,9},{2,10},{3,11},{4,12},{5,13},{6,14},{7,15},{8,0},{9,1},... | collective-permute-start | bytes 2162696 | tf_op jit(solution)/shard_map/ppermute | solution.py:614
  184.0 20.9 %collective-permute-start.27 = (bf16[3,64,1024]{2,1,0:T(8,128)(2,1)}, bf16[3,64,1024]{2,1,0:T(8,128)(2,1)}, u32[]{:S(2)}, u32[]{:S(2)}) collective-permute-start(bf16[3,64,1024]{2,1,0:T(8,128)(2,1)} %get-tuple-element.258), channel_id=1, source_target_pairs={{0,4},{1,5},{2,6},{3,7},{4,0},{5,1},{6,2},{7,3},{8,12},{9,13},{10,... | collective-permute-start | bytes 1179656 | tf_op jit(solution)/shard_map/ppermute | solution.py:614
  187.7 24.5 %collective-permute-start.30 = (bf16[2,2,2,32,1536]{4,3,0,2,1:T(8,128)(2,1)}, bf16[2,2,2,32,1536]{4,3,0,2,1:T(8,128)(2,1)}, u32[]{:S(2)}, u32[]{:S(2)}) collective-permute-start(bf16[2,2,2,32,1536]{4,3,0,2,1:T(8,128)(2,1)} %fusion.4), channel_id=1, source_target_pairs={{0,16},{1,17},{2,18},{3,19},{4,20},{5,21},{6,22},{7,23},{8,24},{9,... | collective-permute-start | bytes 2359304 | tf_op jit(solution)/shard_map/ppermute | solution.py:614
  208.6 17.9 %collective-permute-start.34 = (bf16[2,2,2,32,1280]{4,3,0,2,1:T(8,128)(2,1)}, bf16[2,2,2,32,1280]{4,3,0,2,1:T(8,128)(2,1)}, u32[]{:S(2)}, u32[]{:S(2)}) collective-permute-start(bf16[2,2,2,32,1280]{4,3,0,2,1:T(8,128)(2,1)} %fusion.8), channel_id=1, source_target_pairs={{0,16},{1,17},{2,18},{3,19},{4,20},{5,21},{6,22},{7,23},{8,24},{9,... | collective-permute-start | bytes 1966088 | tf_op jit(solution)/shard_map/ppermute | solution.py:614
  211.3 17.1 %collective-permute-start.35 = (bf16[2,2,2,32,1280]{4,3,0,2,1:T(8,128)(2,1)}, bf16[2,2,2,32,1280]{4,3,0,2,1:T(8,128)(2,1)}, u32[]{:S(2)}, u32[]{:S(2)}) collective-permute-start(bf16[2,2,2,32,1280]{4,3,0,2,1:T(8,128)(2,1)} %fusion.9), channel_id=1, source_target_pairs={{0,8},{1,9},{2,10},{3,11},{4,12},{5,13},{6,14},{7,15},{8,0},{9,1},... | collective-permute-start | bytes 1966088 | tf_op jit(solution)/shard_map/ppermute | solution.py:614
  236.3 16.5 %collective-permute-start.40 = (bf16[2,2,32,768]{3,2,0,1:T(8,128)(2,1)}, bf16[2,2,32,768]{3,2,0,1:T(8,128)(2,1)}, u32[]{:S(2)}, u32[]{:S(2)}) collective-permute-start(bf16[2,2,32,768]{3,2,0,1:T(8,128)(2,1)} %fusion.14), channel_id=1, source_target_pairs={{0,2},{1,3},{2,0},{3,1},{4,6},{5,7},{6,4},{7,5},{8,10},{9,11},{10,... | collective-permute-start | bytes 589832 | tf_op jit(solution)/shard_map/ppermute | solution.py:614
  240.0 20.2 %collective-permute-start.39 = (bf16[2,2,32,1280]{3,2,0,1:T(8,128)(2,1)}, bf16[2,2,32,1280]{3,2,0,1:T(8,128)(2,1)}, u32[]{:S(2)}, u32[]{:S(2)}) collective-permute-start(bf16[2,2,32,1280]{3,2,0,1:T(8,128)(2,1)} %fusion.10), channel_id=1, source_target_pairs={{0,2},{1,3},{2,0},{3,1},{4,6},{5,7},{6,4},{7,5},{8,10},{9,11},{10,... | collective-permute-start | bytes 983048 | tf_op jit(solution)/shard_map/ppermute | solution.py:614
  242.4 18.9 %collective-permute-start.38 = (bf16[2,2,32,1280]{3,2,0,1:T(8,128)(2,1)}, bf16[2,2,32,1280]{3,2,0,1:T(8,128)(2,1)}, u32[]{:S(2)}, u32[]{:S(2)}) collective-permute-start(bf16[2,2,32,1280]{3,2,0,1:T(8,128)(2,1)} %fusion.11), channel_id=1, source_target_pairs={{0,2},{1,3},{2,0},{3,1},{4,6},{5,7},{6,4},{7,5},{8,10},{9,11},{10,... | collective-permute-start | bytes 983048 | tf_op jit(solution)/shard_map/ppermute | solution.py:614
  (115 other events, 752.8 us)

commit v4 on v3

--- a/solution.py
+++ b/solution.py
@@ -12,7 +12,7 @@
 AXES = ("dp", "blk")
 epsilon = 1e-06
 score_scale = 0.125
-cost_share = 0.3
+cost_share = 1.0
 VMEM_LIMIT = 16 << 20
 bf16 = jnp.bfloat16
 f32 = jnp.float32
@@ -194,7 +194,6 @@
         out_specs=[col, pl.BlockSpec((1, 2, rows), lambda i: (i, 0, 0))],
         out_shape=[sds((rows, width), bf16), sds((pairs, 2, rows), f32)],
         scratch_shapes=[pltpu.VMEM((keys, rows), f32)],
-        compiler_params=pltpu.CompilerParams(vmem_limit_bytes=VMEM_LIMIT),
         cost_estimate=cost(
             8 * pairs * rows * keys * LANES, 2 * rows * width * (2 + 2 * slots), 2 * pairs * rows * keys
         ),
@@ -266,7 +265,6 @@
         + [sds((rows, width), f32)] * 2
         + [sds((2, rows, width), bf16)] * (slots - 1),
         scratch_shapes=[pltpu.VMEM((keys, rows), f32)],
-        compiler_params=pltpu.CompilerParams(vmem_limit_bytes=VMEM_LIMIT),
         cost_estimate=cost(
             20 * pairs * rows * keys * LANES, 2 * rows * width * (7 + 4 * slots), 2 * pairs * rows * keys
         ),
@@ -494,7 +492,7 @@
 
 
 def grad_inputs_body(seqs, packed_ref, w_ref, x_ref, gain_ref, gmid_ref, *refs):
-    given, out_refs = refs[: 2 * seqs], refs[2 * seqs :]
+    first_refs, out_refs = refs[:seqs], refs[seqs:]
     grads = mm(packed_ref[...], w_ref[...], NT)
     inputs = x_ref[...].astype(f32)
     factor = lax.rsqrt(jnp.mean(inputs * inputs, axis=-1, keepdims=True) + epsilon)
@@ -504,17 +502,16 @@
     grads = grads.astype(bf16)
     length = out_refs[0].shape[1]
     for s in range(seqs):
-        out_refs[s][0] = given[s][...]
-        out_refs[s][1] = grads[s * length : (s + 1) * length]
-        out_refs[s][2] = given[seqs + s][...]
-
-
-def grad_inputs(seqs, packed, w_qkv, x, gain, grad_middle, out_blocks, first_blocks):
+        out_refs[s][0] = grads[s * length : (s + 1) * length]
+        out_refs[s][1] = first_refs[s][...]
+
+
+def grad_inputs(seqs, packed, w_qkv, x, gain, grad_middle, first_blocks):
     rows, width = x.shape
     return resident_call(
         functools.partial(grad_inputs_body, seqs),
-        (packed, w_qkv, x, gain, grad_middle, *out_blocks, *first_blocks),
-        [sds((3, rows // seqs, width), bf16)] * seqs,
+        (packed, w_qkv, x, gain, grad_middle, *first_blocks),
+        [sds((2, rows // seqs, width), bf16)] * seqs,
         "grad_inputs",
         6 * rows * width * width,
         scalars=0,
@@ -595,7 +592,6 @@
         in_specs=[scalar()] + specs,
         out_specs=[out_spec] * 2,
         out_shape=[sds((height // (2 * per), per, width), bf16)] * 2,
-        compiler_params=pltpu.CompilerParams(vmem_limit_bytes=VMEM_LIMIT),
         cost_estimate=cost(flops, 2 * (sum(a.size for a in args) + height * width)),
         name="outer",
     )(core[None], *args)
@@ -707,8 +703,8 @@
         middle, nffn = middle_norm(x, attended, w_out, gain_f)
         nffn_x = flip(nffn, low_e)
         hidden, gg, gu, hk, hs, ak, a_s, bk, bs = ffn_acts(edges, nffn, cot, w_gate, w_up, w_down)
-        hidden, gg, gu, hs, a_s, bs, nffn_x, cot_y = tie(
-            hidden, gg, gu, hs, a_s, bs, nffn_x, cot_y
+        hidden, gg, gu, hs, a_s, bs, nffn_x, cot_y, attended_y = tie(
+            hidden, gg, gu, hs, a_s, bs, nffn_x, cot_y, attended_y
         )
         h_y = flip(hs, high_e)
         a_x = flip(a_s, low_e)
@@ -716,25 +712,18 @@
             seqs, edges, hidden, gg, gu, w_gate, w_up, w_down, middle, cot, w_out, gain_f
         )
         gbs, bs, grad_att = tie(gbs, bs, grad_att)
+        out_parts = from_sequence(out_blocks)
         b_x = flip(bs, low_e)
         gb_y = flip(gbs, high_e)
         gq, gk, gv, other_kv = attend_back(
             q, grad_att, ks, vs, lse, kpos, qpos, qstart, cosine, sines
         )
-        gq, gk, gv, other_kv, h_y, a_x = tie(gq, gk, gv, other_kv, h_y, a_x)
+        gq, gk, gv, other_kv, h_y, a_x, out_parts = tie(
+            gq, gk, gv, other_kv, h_y, a_x, out_parts
+        )
         got_kv = [send(v, lambda i, g=g: shift_member(i, -g)) for g, v in enumerate(other_kv, 1)]
         per_down = ff // n
         per = width // n
-        dk, ds = outer(core, per_down, ([hk, h_y], [cot, cot_y]))
-        dk, ds, got_kv = tie(dk, ds, got_kv)
-        d_c = flip(ds, 0)
-        packed, first_blocks, (qxk, qxs, qyk, qys) = grad_pack(
-            seqs, edges, gq, gk, gv, got_kv, cosine, sines
-        )
-        packed, first_blocks, qxs, qys, d_c = tie(packed, first_blocks, qxs, qys, d_c)
-        q_x = flip(qxs, low_e)
-        q_y = flip(qys, high_e)
-        blocks = grad_inputs(seqs, packed, w_qkv, x, gain_a, grad_mid, out_blocks, first_blocks)
 
         class Rows:
             def __init__(self, keep, got, top, skip):
@@ -780,35 +769,50 @@
             return values
 
         ak2, as2 = outer(core, per, ([nffn, nffn_x], [ak, a_x]))
-        blocks, ak2, as2, b_x, gb_y, attended_y = tie(blocks, ak2, as2, b_x, gb_y, attended_y)
+        ak2, as2, got_kv = tie(ak2, as2, got_kv)
         a_c = flip(as2, 0)
+        packed, first_blocks, (qxk, qxs, qyk, qys) = grad_pack(
+            seqs, edges, gq, gk, gv, got_kv, cosine, sines
+        )
+        packed, first_blocks, qxs, qys, a_c, hk, h_y = tie(
+            packed, first_blocks, qxs, qys, a_c, hk, h_y
+        )
+        part_a = Rows(ak2, a_c, nbits - 1, low_e)
+        part_a.next()
+        q_x = flip(qxs, low_e)
+        q_y = flip(qys, high_e)
+        dk, ds = outer(core, per_down, ([hk, h_y], [cot, cot_y]))
+        blocks = grad_inputs(seqs, packed, w_qkv, x, gain_a, grad_mid, first_blocks)
+        blocks, dk, ds, bk, b_x, gb_y = tie(blocks, dk, ds, bk, b_x, gb_y)
+        d_c = flip(ds, 0)
+        moved = from_sequence(blocks)
+        bk2, bs2 = outer(core, per, ([nffn, nffn_x], [bk, b_x]))
+        bk2, bs2, d_c, q_x, q_y = tie(bk2, bs2, d_c, q_x, q_y)
+        b_c = flip(bs2, 0)
         down = Rows(dk, d_c, nbits - 2, -1)
         down.next()
-        moved = from_sequence(blocks)
-        bk2, bs2 = outer(core, per, ([nffn, nffn_x], [bk, b_x]))
-        bk2, bs2, a_c, q_x, q_y = tie(bk2, bs2, a_c, q_x, q_y)
-        b_c = flip(bs2, 0)
-        part_a = Rows(ak2, a_c, nbits - 1, low_e)
-        part_a.next()
         qyk2, qys2 = outer(
             core, per, ([normed, normed_y], [qyk, q_y]), ([attended, attended_y], [gbk, gb_y])
         )
-        qyk2, qys2, b_c, moved[1::2] = tie(qyk2, qys2, b_c, moved[1::2])
+        qyk2, qys2, b_c, moved[1::2] = settle((qyk2, qys2, b_c, moved[1::2]), part_a)
         qy_c = flip(qys2, 0)
         part_b = Rows(bk2, b_c, nbits - 1, low_e)
+        part_b.next()
+        part_a.next()
         qxk2, qxs2 = outer(core, per, ([normed, normed_x], [qxk, q_x]))
-        qxk2, qxs2, qy_c, moved = settle((qxk2, qxs2, qy_c, moved), down)
+        qxk2, qxs2, qy_c = settle((qxk2, qxs2, qy_c), part_a, down)
         qx_c = flip(qxs2, 0)
         part_y = Rows(qyk2, qy_c, nbits - 1, high_e)
+        part_y.next()
+        part_a.next()
+        down.next()
+        (qx_c,) = settle((qx_c,), part_a, part_b, down)
+        part_x = Rows(qxk2, qx_c, nbits - 1, low_e)
+        part_x.next()
         part_b.next()
         down.next()
-        part_y.next()
-        (qx_c,) = settle((qx_c,), part_a, down)
-        part_x = Rows(qxk2, qx_c, nbits - 1, low_e)
         part_a.next()
-        part_x.next()
-        down.next()
-        settle((), part_a, part_b, part_y, down)
+        (moved,) = settle((moved,), part_a, part_b, part_y, down)
         everything = (part_a, part_b, part_y, part_x, down)
         while True:
             busy = [part for part in everything if part.next()]
@@ -819,7 +823,8 @@
         a_done, b_done, qx_done, qy_done = (
             part.halves() for part in (part_a, part_b, part_x, part_y)
         )
-        output, grad_tokens, grad_first_values = place(moved, seq)
+        (output,) = place([part[None] for part in out_parts], seq)
+        grad_tokens, grad_first_values = place(moved, seq)
 
         acts = jnp.concatenate([a_done[0], a_done[1], b_done[0], b_done[1]], axis=1)
         grad_gate, grad_up = acts[:, :ff], acts[:, ff:]

time: 301 us -> 282 us (0.937)
  local copies, waits for them, and re-layouts: 50.4 us -> 35.4 us
  other arithmetic: 43.1 us -> 31.9 us
  starting transfers between devices: 53 us -> 62.9 us
  waiting for transfers between devices: 79.9 us -> 70.9 us
  Pallas kernels: 71.2 us -> 78.2 us
    unnamed x186 -> x124, local copies, waits for them, and re-layouts: 47.6 us -> 32.7 us
    convert_element_type x15, other arithmetic: 26.8 us -> 16.7 us  [go(): out = self.total([pick(v, 1 - b, axis) for v in self.terms]).astype(bf16)]
    ppermute x48 -> x51, starting transfers between devices: 53 us -> 62.9 us  [send(): return lax.ppermute(value, AXES, pairs)]
    ppermute x48 -> x51, waiting for transfers between devices: 79.9 us -> 70.9 us  [send(): return lax.ppermute(value, AXES, pairs)]
    pallas_call x5, Pallas kernels: 21.4 us -> 28.5 us  [outer(): pl.pallas_call(functools.partial(outer_body, [len(lefts) for lefts, _ in...]
  transfers between devices with their start and end apart: 48 -> 51, of which waited for: 21 -> 16; matrix products, arithmetic and copies ran while one was open for 11% -> 10% of each run, Pallas kernels for 23% -> 27%
where the time goes in v4:
time: 282 us; the launch traced here: 281 us
  Pallas kernels  78.2 us (28%)
  waiting for transfers between devices  70.9 us (25%)
  starting transfers between devices  62.9 us (22%)
  local copies, waits for them, and re-layouts  35.4 us (13%)
  other arithmetic  31.9 us (11%)
    ppermute x51, waiting for transfers between devices, send(): return lax.ppermute(value, AXES, pairs)  70.9 us
    ppermute x51, starting transfers between devices, send(): return lax.ppermute(value, AXES, pairs)  62.9 us
    unnamed x124, local copies, waits for them, and re-layouts  32.7 us
    pallas_call x5, Pallas kernels, outer(): pl.pallas_call(functools.partial(outer_body, [len(lefts) for lefts, _ in...  28.5 us
    pallas_call x7, Pallas kernels, resident_call(): pl.pallas_call(body, in_specs=[scalar()] * scalars + [RESIDENT] * (len(in...  21.3 us
    convert_element_type x15, other arithmetic, go(): out = self.total([pick(v, 1 - b, axis) for v in self.terms]).astype(bf16)  16.7 us
    pallas_call x1, Pallas kernels, attend_back(): pl.pallas_call(functools.partial(attend_back_body, slots), grid=(pairs,),...  12.2 us
    pallas_call x1, Pallas kernels, attend(): pl.pallas_call(functools.partial(attend_body, slots), grid=(pairs,), in_s...  11.8 us
  transfers between devices with their start and end apart: 51, of which 16 were waited for; matrix products, arithmetic and copies ran while one was open for 10% of the time, Pallas kernels for 27%

profile of v4, /device:TPU:0, one launch (start us, length us, event | category | flops | bytes accessed | tf_op | source)
XLA Modules:
  0.0 281.0 jit_solution(14227984527698797347)
XLA Ops:
  11.6 4.0 %collective-permute-done = bf16[136,1024]{1,0:T(8,128)(2,1)S(1)} collective-permute-done((bf16[136,1024]{1,0:T(8,128)(2,1)S(1)}, bf16[136,1024]{1,0:T(8,128)(2,1)S(1)}, u32[]{:S(2)}, u32[]{:S(2)}) %collective-permute-start) | collective-permute-done | bytes 278560 | tf_op jit(solution)/shard_map/ppermute | solution.py:610
  15.6 11.1 %collective-permute-done.1 = bf16[136,1024]{1,0:T(8,128)(2,1)S(1)} collective-permute-done((bf16[136,1024]{1,0:T(8,128)(2,1)S(1)}, bf16[136,1024]{1,0:T(8,128)(2,1)S(1)}, u32[]{:S(2)}, u32[]{:S(2)}) %collective-permute-start.1) | collective-permute-done | bytes 278560 | tf_op jit(solution)/shard_map/ppermute | solution.py:610
  38.1 7.5 %collective-permute-start.10 = (bf16[64,1024]{1,0:T(8,128)(2,1)}, bf16[64,1024]{1,0:T(8,128)(2,1)S(1)}, u32[]{:S(2)}, u32[]{:S(2)}) collective-permute-start(bf16[64,1024]{1,0:T(8,128)(2,1)} %get-tuple-element.317), channel_id=1, source_target_pairs={{0,6},{1,7},{2,0},{3,1},{4,2},{5,3},{6,4},{7,5},{8,14},{9,15},{10,... | collective-permute-start | bytes 393224 | tf_op jit(solution)/shard_map/ppermute | solution.py:610
  46.9 11.8 %attend.1 = (bf16[256,1024]{1,0:T(8,128)(2,1)}, f32[8,2,256]{2,1,0:T(2,128)}) custom-call(bf16[256,1024]{1,0:T(8,128)(2,1)} %copy-done.34, bf16[256,1024]{1,0:T(8,128)(2,1)} %copy-done.35, bf16[256,1024]{1,0:T(8,128)(2,1)} %collective-permute-done.3.refs_2_.refs_3_, bf16[256,1024]{1,0:T(8,128)(2,1)} %copy-done.20, ...), custom_call_target="tpu_custom_call" | custom-call | flops 1073741824 | bytes 3145728 | tf_op jit(solution)/shard_map/attend/pallas_call | solution.py:187
  72.3 7.1 %ffn_acts.1 = (bf16[256,2816]{1,0:T(8,128)(2,1)S(1)}, bf16[256,2816]{1,0:T(8,128)(2,1)S(1)}, bf16[256,2816]{1,0:T(8,128)(2,1)S(1)}, bf16[256,1408]{1,0:T(8,128)(...) custom-call(s32[2]{0:T(128)S(1)} %pad_add_fusion.2.edge_ref, ...), custom_call_target="tpu_custom_call" | custom-call | flops 4429185024 | bytes 27000840 | tf_op jit(solution)/shard_map/ffn_acts/pallas_call | solution.py:56
  81.2 3.6 %collective-permute-done.13.refs_5_ = bf16[256,1024]{1,0:T(8,128)(2,1)S(1)} collective-permute-done((bf16[256,1024]{1,0:T(8,128)(2,1)}, bf16[256,1024]{1,0:T(8,128)(2,1)S(1)}, u32[]{:S(2)}, u32[]{:S(2)}) %collective-permute-start.13) | collective-permute-done | bytes 524320 | tf_op jit(solution)/shard_map/ppermute | solution.py:610
  85.8 6.2 %ffn_back.1 = (bf16[64,1024]{1,0:T(8,128)(2,1)S(1)}, bf16[64,1024]{1,0:T(8,128)(2,1)S(1)}, bf16[64,1024]{1,0:T(8,128)(2,1)S(1)}, bf16[64,1024]{1,0:T(8,128)(2,1)...) custom-call(s32[2]{0:T(128)S(1)} %pad_add_fusion.2.edge_ref, ...), custom_call_target="tpu_custom_call" | custom-call | flops 4966055936 | bytes 27922440 | tf_op jit(solution)/shard_map/ffn_back/pallas_call | solution.py:56
  99.6 12.2 %attend_back.1 = (bf16[256,1024]{1,0:T(8,128)(2,1)}, f32[256,1024]{1,0:T(8,128)}, f32[256,1024]{1,0:T(8,128)}, bf16[2,256,1024]{2,1,0:T(8,128)(2,1)}) custom-call(bf16[256,1024]{1,0:T(8,128)(2,1)} %copy-done.34, bf16[256,1024]{1,0:T(8,128)(2,1)} %copy-done.36, bf16[256,1024]{1,0:T(8,128)(2,1)} %copy-done.35, ...), custom_call_target="tpu_custom_call" | custom-call | flops 2684354560 | bytes 7864320 | tf_op jit(solution)/shard_map/attend_back/pallas_call | solution.py:254
  113.8 5.9 %outer.5 = (bf16[16,32,1536]{2,1,0:T(8,128)(2,1)}, bf16[16,32,1536]{2,1,0:T(8,128)(2,1)}) custom-call(s32[1]{0:T(128)} %bitcast.26.core_ref, bf16[256,1024]{1,0:T(8,128)(2,1)} %copy-done.21, bf16[256,1024]{1,0:T(8,128)(2,1)} %copy-done.57, bf16[256,1536]{1,0:T(8,128)(2,1)} %copy-done.30, bf16[256,1536]{1,0:T(8,128)(2,1)} %collective-permute-done.15.refs_3_), custom_call_target="tpu_custom_call" | custom-call | flops 1610612736 | bytes 5767168 | tf_op jit(solution)/shard_map/outer/pallas_call | solution.py:589
  132.7 5.5 %outer.6 = (bf16[8,88,1024]{2,1,0:T(8,128)(2,1)}, bf16[8,88,1024]{2,1,0:T(8,128)(2,1)}) custom-call(s32[1]{0:T(128)} %bitcast.26.core_ref, bf16[256,1408]{1,0:T(8,128)(2,1)} %copy-done.31, bf16[256,1408]{1,0:T(8,128)(2,1)} %collective-permute-done.14.refs_1_, bf16[256,1024]{1,0:T(8,128)(2,1)} %copy-done.6, bf16[256,1024]{1,0:T(8,128)(2,1)} %copy-done.58), custom_call_target="tpu_custom_call" | custom-call | flops 1476395008 | bytes 5373952 | tf_op jit(solution)/shard_map/outer/pallas_call | solution.py:589
  147.6 5.4 %outer.7 = (bf16[16,32,1280]{2,1,0:T(8,128)(2,1)}, bf16[16,32,1280]{2,1,0:T(8,128)(2,1)}) custom-call(s32[1]{0:T(128)} %bitcast.26.core_ref, bf16[256,1024]{1,0:T(8,128)(2,1)} %copy-done.21, bf16[256,1024]{1,0:T(8,128)(2,1)} %copy-done.57, bf16[256,1280]{1,0:T(8,128)(2,1)} %copy-done.32, bf16[256,1280]{1,0:T(8,128)(2,1)} %collective-permute-done.21.refs_3_), custom_call_target="tpu_custom_call" | custom-call | flops 1342177280 | bytes 4980736 | tf_op jit(solution)/shard_map/outer/pallas_call | solution.py:589
  153.0 5.2 %collective-permute-done.24.refs_3_ = bf16[256,768]{1,0:T(8,128)(2,1)S(1)} collective-permute-done((bf16[256,768]{1,0:T(8,128)(2,1)}, bf16[256,768]{1,0:T(8,128)(2,1)S(1)}, u32[]{:S(2)}, u32[]{:S(2)}) %collective-permute-start.24) | collective-permute-done | bytes 393248 | tf_op jit(solution)/shard_map/ppermute | solution.py:610
  161.1 3.8 %collective-permute-start.27 = (bf16[2,64,1024]{2,1,0:T(8,128)(2,1)S(1)}, bf16[2,64,1024]{2,1,0:T(8,128)(2,1)S(1)}, u32[]{:S(2)}, u32[]{:S(2)}) collective-permute-start(bf16[2,64,1024]{2,1,0:T(8,128)(2,1)S(1)} %copy-done.47), channel_id=1, source_target_pairs={{0,6},{1,7},{2,0},{3,1},{4,2},{5,3},{6,4},{7,5},{8,14},{9,15},{10,... | collective-permute-start | bytes 786440 | tf_op jit(solution)/shard_map/ppermute | solution.py:610
  165.0 7.0 %outer.8 = (bf16[16,32,1280]{2,1,0:T(8,128)(2,1)}, bf16[16,32,1280]{2,1,0:T(8,128)(2,1)}) custom-call(s32[1]{0:T(128)} %bitcast.26.core_ref, bf16[256,1024]{1,0:T(8,128)(2,1)} %copy-done.19, bf16[256,1024]{1,0:T(8,128)(2,1)} %collective-permute-done.7.refs_1_, bf16[256,768]{1,0:T(8,128)(2,1)} %copy-done.38, ...), custom_call_target="tpu_custom_call" | custom-call | flops 1342177280 | bytes 6029312 | tf_op jit(solution)/shard_map/outer/pallas_call | solution.py:589
  172.0 5.3 %collective-permute-done.28.refs_3_ = bf16[2,64,1024]{2,1,0:T(8,128)(2,1)S(1)} collective-permute-done((bf16[2,64,1024]{2,1,0:T(8,128)(2,1)S(1)}, bf16[2,64,1024]{2,1,0:T(8,128)(2,1)S(1)}, u32[]{:S(2)}, u32[]{:S(2)}) %collective-permute-start.28) | collective-permute-done | bytes 262176 | tf_op jit(solution)/shard_map/ppermute | solution.py:610
  177.3 3.6 %collective-permute-done.29 = bf16[2,2,2,32,1536]{4,3,0,2,1:T(8,128)(2,1)} collective-permute-done((bf16[2,2,2,32,1536]{4,3,0,2,1:T(8,128)(2,1)}, bf16[2,2,2,32,1536]{4,3,0,2,1:T(8,128)(2,1)}, u32[]{:S(2)}, u32[]{:S(2)}) %collective-permute-start.29) | collective-permute-done | bytes 786464 | tf_op jit(solution)/shard_map/ppermute | solution.py:610
  192.7 4.7 %outer.9 = (bf16[16,32,768]{2,1,0:T(8,128)(2,1)}, bf16[16,32,768]{2,1,0:T(8,128)(2,1)}) custom-call(s32[1]{0:T(128)} %bitcast.26.core_ref, bf16[256,1024]{1,0:T(8,128)(2,1)} %copy-done.19, bf16[256,1024]{1,0:T(8,128)(2,1)} %collective-permute-done.6.refs_1_, bf16[256,768]{1,0:T(8,128)(2,1)} %copy-done.37, bf16[256,768]{1,0:T(8,128)(2,1)} %copy-done.59), custom_call_target="tpu_custom_call" | custom-call | flops 805306368 | bytes 3407872 | tf_op jit(solution)/shard_map/outer/pallas_call | solution.py:589
  197.4 5.0 %collective-permute-done.33 = bf16[2,2,88,1024]{3,2,1,0:T(8,128)(2,1)} collective-permute-done((bf16[2,2,88,1024]{3,2,1,0:T(8,128)(2,1)}, bf16[2,2,88,1024]{3,2,1,0:T(8,128)(2,1)}, u32[]{:S(2)}, u32[]{:S(2)}) %collective-permute-start.33) | collective-permute-done | bytes 720928 | tf_op jit(solution)/shard_map/ppermute | solution.py:610
  213.1 8.6 %collective-permute-done.36 = bf16[2,2,2,32,1280]{4,3,0,2,1:T(8,128)(2,1)S(1)} collective-permute-done((bf16[2,2,2,32,1280]{4,3,0,2,1:T(8,128)(2,1)S(1)}, bf16[2,2,2,32,1280]{4,3,0,2,1:T(8,128)(2,1)S(1)}, u32[]{:S(2)}, u32[]{:S(2)}) %collective-permute-start.36) | collective-permute-done | bytes 655392 | tf_op jit(solution)/shard_map/ppermute | solution.py:610
  232.3 6.8 %collective-permute-done.40 = bf16[2,2,2,32,1280]{4,3,0,2,1:T(8,128)(2,1)S(1)} collective-permute-done((bf16[2,2,2,32,1280]{4,3,0,2,1:T(8,128)(2,1)S(1)}, bf16[2,2,2,32,1280]{4,3,0,2,1:T(8,128)(2,1)S(1)}, u32[]{:S(2)}, u32[]{:S(2)}) %collective-permute-start.40) | collective-permute-done | bytes 655392 | tf_op jit(solution)/shard_map/ppermute | solution.py:610
  243.1 3.3 %collective-permute-start.43 = (bf16[2,32,1280]{2,1,0:T(8,128)(2,1)S(1)}, bf16[2,32,1280]{2,1,0:T(8,128)(2,1)S(1)}, u32[]{:S(2)}, u32[]{:S(2)}) collective-permute-start(bf16[2,32,1280]{2,1,0:T(8,128)(2,1)S(1)} %fusion.21), channel_id=1, source_target_pairs={{0,4},{1,5},{2,6},{3,7},{4,0},{5,1},{6,2},{7,3},{8,12},{9,13},{10,... | collective-permute-start | bytes 491528 | tf_op jit(solution)/shard_map/ppermute | solution.py:610
  246.6 7.0 %collective-permute-done.43 = bf16[2,32,1280]{2,1,0:T(8,128)(2,1)S(1)} collective-permute-done((bf16[2,32,1280]{2,1,0:T(8,128)(2,1)S(1)}, bf16[2,32,1280]{2,1,0:T(8,128)(2,1)S(1)}, u32[]{:S(2)}, u32[]{:S(2)}) %collective-permute-start.43) | collective-permute-done | bytes 163872 | tf_op jit(solution)/shard_map/ppermute | solution.py:610
  253.6 3.8 %collective-permute-done.45 = bf16[2,2,32,768]{3,2,0,1:T(8,128)(2,1)S(1)} collective-permute-done((bf16[2,2,32,768]{3,2,0,1:T(8,128)(2,1)S(1)}, bf16[2,2,32,768]{3,2,0,1:T(8,128)(2,1)S(1)}, u32[]{:S(2)}, u32[]{:S(2)}) %collective-permute-start.45) | collective-permute-done | bytes 196640 | tf_op jit(solution)/shard_map/ppermute | solution.py:610
  267.7 3.5 %collective-permute-done.47 = bf16[2,32,1280]{2,1,0:T(8,128)(2,1)S(1)} collective-permute-done((bf16[2,32,1280]{2,1,0:T(8,128)(2,1)S(1)}, bf16[2,32,1280]{2,1,0:T(8,128)(2,1)S(1)}, u32[]{:S(2)}, u32[]{:S(2)}) %collective-permute-start.47) | collective-permute-done | bytes 163872 | tf_op jit(solution)/shard_map/ppermute | solution.py:610
  (293 shorter events, 131.6 us)
Async XLA Ops:
  5.9 20.8 %collective-permute-start.1 = (bf16[136,1024]{1,0:T(8,128)(2,1)S(1)}, bf16[136,1024]{1,0:T(8,128)(2,1)S(1)}, u32[]{:S(2)}, u32[]{:S(2)}) collective-permute-start(bf16[136,1024]{1,0:T(8,128)(2,1)S(1)} %get-tuple-element.314), channel_id=1, source_target_pairs={{0,4},{1,5},{2,6},{3,7},{4,0},{5,1},{6,2},{7,3},{8,12},{9,13},{10,... | collective-permute-start | bytes 835592 | tf_op jit(solution)/shard_map/ppermute | solution.py:610
  8.5 18.2 %collective-permute-start.2 = (bf16[136,1024]{1,0:T(8,128)(2,1)S(1)}, bf16[136,1024]{1,0:T(8,128)(2,1)S(1)}, u32[]{:S(2)}, u32[]{:S(2)}) collective-permute-start(bf16[136,1024]{1,0:T(8,128)(2,1)S(1)} %get-tuple-element.313), channel_id=1, source_target_pairs={{0,6},{1,7},{2,0},{3,1},{4,2},{5,3},{6,4},{7,5},{8,14},{9,15},{10,... | collective-permute-start | bytes 835592 | tf_op jit(solution)/shard_map/ppermute | solution.py:610
  33.3 25.5 %collective-permute-start.6 = (bf16[256,1024]{1,0:T(8,128)(2,1)S(1)}, bf16[256,1024]{1,0:T(8,128)(2,1)}, u32[]{:S(2)}, u32[]{:S(2)}) collective-permute-start(bf16[256,1024]{1,0:T(8,128)(2,1)S(1)} %get-tuple-element.167.normed_ref.refs_0_), channel_id=1, source_target_pairs={{0,8},{1,9},{2,10},{3,11},{4,12},{5,13},{6,14},{7,15},{8,0},{9,1},... | collective-permute-start | bytes 1572872 | tf_op jit(solution)/shard_map/ppermute | solution.py:610
  34.8 24.0 %collective-permute-start.7 = (bf16[256,1024]{1,0:T(8,128)(2,1)S(1)}, bf16[256,1024]{1,0:T(8,128)(2,1)}, u32[]{:S(2)}, u32[]{:S(2)}) collective-permute-start(bf16[256,1024]{1,0:T(8,128)(2,1)S(1)} %get-tuple-element.167.normed_ref.refs_0_), channel_id=1, source_target_pairs={{0,16},{1,17},{2,18},{3,19},{4,20},{5,21},{6,22},{7,23},{8,24},{9,... | collective-permute-start | bytes 1572872 | tf_op jit(solution)/shard_map/ppermute | solution.py:610
  38.1 20.6 %collective-permute-start.10 = (bf16[64,1024]{1,0:T(8,128)(2,1)}, bf16[64,1024]{1,0:T(8,128)(2,1)S(1)}, u32[]{:S(2)}, u32[]{:S(2)}) collective-permute-start(bf16[64,1024]{1,0:T(8,128)(2,1)} %get-tuple-element.317), channel_id=1, source_target_pairs={{0,6},{1,7},{2,0},{3,1},{4,2},{5,3},{6,4},{7,5},{8,14},{9,15},{10,... | collective-permute-start | bytes 393224 | tf_op jit(solution)/shard_map/ppermute | solution.py:610
  59.7 21.4 %collective-permute-start.12 = (bf16[256,1024]{1,0:T(8,128)(2,1)S(1)}, bf16[256,1024]{1,0:T(8,128)(2,1)S(1)}, u32[]{:S(2)}, u32[]{:S(2)}) collective-permute-start(bf16[256,1024]{1,0:T(8,128)(2,1)S(1)} %constant_dynamic-update-slice_fusion.cot_ref.refs_2_), channel_id=1, source_target_pairs={{0,16},{1,17},{2,18},{3,19},{4,20},{5,21},{6,22},{7,23},{8,24},{9,... | collective-permute-start | bytes 1572872 | tf_op jit(solution)/shard_map/ppermute | solution.py:610
  60.3 24.5 %collective-permute-start.13 = (bf16[256,1024]{1,0:T(8,128)(2,1)}, bf16[256,1024]{1,0:T(8,128)(2,1)S(1)}, u32[]{:S(2)}, u32[]{:S(2)}) collective-permute-start(bf16[256,1024]{1,0:T(8,128)(2,1)} %get-tuple-element.172.att_ref.refs_4_), channel_id=1, source_target_pairs={{0,16},{1,17},{2,18},{3,19},{4,20},{5,21},{6,22},{7,23},{8,24},{9,... | collective-permute-start | bytes 1572872 | tf_op jit(solution)/shard_map/ppermute | solution.py:610
  63.8 17.4 %collective-permute-start.11 = (bf16[256,1024]{1,0:T(8,128)(2,1)S(1)}, bf16[256,1024]{1,0:T(8,128)(2,1)S(1)}, u32[]{:S(2)}, u32[]{:S(2)}) collective-permute-start(bf16[256,1024]{1,0:T(8,128)(2,1)S(1)} %get-tuple-element.173.nffn_ref.refs_0_), channel_id=1, source_target_pairs={{0,8},{1,9},{2,10},{3,11},{4,12},{5,13},{6,14},{7,15},{8,0},{9,1},... | collective-permute-start | bytes 1572872 | tf_op jit(solution)/shard_map/ppermute | solution.py:610
  84.8 29.0 %collective-permute-start.15 = (bf16[256,1536]{1,0:T(8,128)(2,1)}, bf16[256,1536]{1,0:T(8,128)(2,1)}, u32[]{:S(2)}, u32[]{:S(2)}) collective-permute-start(bf16[256,1536]{1,0:T(8,128)(2,1)} %get-tuple-element.198), channel_id=1, source_target_pairs={{0,8},{1,9},{2,10},{3,11},{4,12},{5,13},{6,14},{7,15},{8,0},{9,1},... | collective-permute-start | bytes 2359304 | tf_op jit(solution)/shard_map/ppermute | solution.py:610
  85.3 28.4 %collective-permute-start.14 = (bf16[256,1408]{1,0:T(8,128)(2,1)}, bf16[256,1408]{1,0:T(8,128)(2,1)}, u32[]{:S(2)}, u32[]{:S(2)}) collective-permute-start(bf16[256,1408]{1,0:T(8,128)(2,1)} %get-tuple-element.197), channel_id=1, source_target_pairs={{0,16},{1,17},{2,18},{3,19},{4,20},{5,21},{6,22},{7,23},{8,24},{9,... | collective-permute-start | bytes 2162696 | tf_op jit(solution)/shard_map/ppermute | solution.py:610
  94.6 17.1 %collective-permute-start.16 = (bf16[64,1024]{1,0:T(8,128)(2,1)S(1)}, bf16[64,1024]{1,0:T(8,128)(2,1)S(1)}, u32[]{:S(2)}, u32[]{:S(2)}) collective-permute-start(bf16[64,1024]{1,0:T(8,128)(2,1)S(1)} %get-tuple-element.200), channel_id=1, source_target_pairs={{0,6},{1,7},{2,0},{3,1},{4,2},{5,3},{6,4},{7,5},{8,14},{9,15},{10,... | collective-permute-start | bytes 393224 | tf_op jit(solution)/shard_map/ppermute | solution.py:610
  121.1 25.3 %collective-permute-start.21 = (bf16[256,1280]{1,0:T(8,128)(2,1)}, bf16[256,1280]{1,0:T(8,128)(2,1)}, u32[]{:S(2)}, u32[]{:S(2)}) collective-permute-start(bf16[256,1280]{1,0:T(8,128)(2,1)} %copy-done.33), channel_id=1, source_target_pairs={{0,8},{1,9},{2,10},{3,11},{4,12},{5,13},{6,14},{7,15},{8,0},{9,1},... | collective-permute-start | bytes 1966088 | tf_op jit(solution)/shard_map/ppermute | solution.py:610
  122.6 23.8 %collective-permute-start.22 = (bf16[256,512]{1,0:T(8,128)(2,1)}, bf16[256,512]{1,0:T(8,128)(2,1)}, u32[]{:S(2)}, u32[]{:S(2)}) collective-permute-start(bf16[256,512]{1,0:T(8,128)(2,1)} %get-tuple-element.244), channel_id=1, source_target_pairs={{0,16},{1,17},{2,18},{3,19},{4,20},{5,21},{6,22},{7,23},{8,24},{9,... | collective-permute-start | bytes 786440 | tf_op jit(solution)/shard_map/ppermute | solution.py:610
  158.4 22.5 %collective-permute-start.26 = (bf16[16,32,1280]{2,1,0:T(8,128)(2,1)}, bf16[16,32,1280]{2,1,0:T(8,128)(2,1)}, u32[]{:S(2)}, u32[]{:S(2)}) collective-permute-start(bf16[16,32,1280]{2,1,0:T(8,128)(2,1)} %get-tuple-element.261), channel_id=1, source_target_pairs={{0,1},{1,0},{2,3},{3,2},{4,5},{5,4},{6,7},{7,6},{8,9},{9,8},{10,11... | collective-permute-start | bytes 3932168 | tf_op jit(solution)/shard_map/ppermute | solution.py:610
  160.6 20.3 %collective-permute-start.29 = (bf16[2,2,2,32,1536]{4,3,0,2,1:T(8,128)(2,1)}, bf16[2,2,2,32,1536]{4,3,0,2,1:T(8,128)(2,1)}, u32[]{:S(2)}, u32[]{:S(2)}) collective-permute-start(bf16[2,2,2,32,1536]{4,3,0,2,1:T(8,128)(2,1)} %fusion.4), channel_id=1, source_target_pairs={{0,16},{1,17},{2,18},{3,19},{4,20},{5,21},{6,22},{7,23},{8,24},{9,... | collective-permute-start | bytes 2359304 | tf_op jit(solution)/shard_map/ppermute | solution.py:610
  180.9 22.4 %collective-permute-start.31 = (bf16[16,32,1280]{2,1,0:T(8,128)(2,1)}, bf16[16,32,1280]{2,1,0:T(8,128)(2,1)}, u32[]{:S(2)}, u32[]{:S(2)}) collective-permute-start(bf16[16,32,1280]{2,1,0:T(8,128)(2,1)} %get-tuple-element.275), channel_id=1, source_target_pairs={{0,1},{1,0},{2,3},{3,2},{4,5},{5,4},{6,7},{7,6},{8,9},{9,8},{10,11... | collective-permute-start | bytes 3932168 | tf_op jit(solution)/shard_map/ppermute | solution.py:610
  183.5 18.8 %collective-permute-start.33 = (bf16[2,2,88,1024]{3,2,1,0:T(8,128)(2,1)}, bf16[2,2,88,1024]{3,2,1,0:T(8,128)(2,1)}, u32[]{:S(2)}, u32[]{:S(2)}) collective-permute-start(bf16[2,2,88,1024]{3,2,1,0:T(8,128)(2,1)} %fusion.6), channel_id=1, source_target_pairs={{0,8},{1,9},{2,10},{3,11},{4,12},{5,13},{6,14},{7,15},{8,0},{9,1},... | collective-permute-start | bytes 2162696 | tf_op jit(solution)/shard_map/ppermute | solution.py:610
  186.2 17.0 %collective-permute-start.32 = (bf16[2,2,32,1536]{3,2,0,1:T(8,128)(2,1)S(1)}, bf16[2,2,32,1536]{3,2,0,1:T(8,128)(2,1)}, u32[]{:S(2)}, u32[]{:S(2)}) collective-permute-start(bf16[2,2,32,1536]{3,2,0,1:T(8,128)(2,1)S(1)} %fusion.5), channel_id=1, source_target_pairs={{0,2},{1,3},{2,0},{3,1},{4,6},{5,7},{6,4},{7,5},{8,10},{9,11},{10,... | collective-permute-start | bytes 1179656 | tf_op jit(solution)/shard_map/ppermute | solution.py:610
  190.0 41.7 %collective-permute-start.30 = (bf16[2,64,1024]{2,1,0:T(8,128)(2,1)S(1)}, bf16[2,64,1024]{2,1,0:T(8,128)(2,1)S(1)}, u32[]{:S(2)}, u32[]{:S(2)}) collective-permute-start(bf16[2,64,1024]{2,1,0:T(8,128)(2,1)S(1)} %copy-done.42), channel_id=1, source_target_pairs={{0,4},{1,5},{2,6},{3,7},{4,0},{5,1},{6,2},{7,3},{8,12},{9,13},{10,... | collective-permute-start | bytes 786440 | tf_op jit(solution)/shard_map/ppermute | solution.py:610
  203.3 19.1 %collective-permute-start.34 = (bf16[16,32,768]{2,1,0:T(8,128)(2,1)}, bf16[16,32,768]{2,1,0:T(8,128)(2,1)S(1)}, u32[]{:S(2)}, u32[]{:S(2)}) collective-permute-start(bf16[16,32,768]{2,1,0:T(8,128)(2,1)} %get-tuple-element.279), channel_id=1, source_target_pairs={{0,1},{1,0},{2,3},{3,2},{4,5},{5,4},{6,7},{7,6},{8,9},{9,8},{10,11... | collective-permute-start | bytes 2359304 | tf_op jit(solution)/shard_map/ppermute | solution.py:610
  204.5 17.2 %collective-permute-start.36 = (bf16[2,2,2,32,1280]{4,3,0,2,1:T(8,128)(2,1)S(1)}, bf16[2,2,2,32,1280]{4,3,0,2,1:T(8,128)(2,1)S(1)}, u32[]{:S(2)}, u32[]{:S(2)}) collective-permute-start(bf16[2,2,2,32,1280]{4,3,0,2,1:T(8,128)(2,1)S(1)} %fusion.8), channel_id=1, source_target_pairs={{0,16},{1,17},{2,18},{3,19},{4,20},{5,21},{6,22},{7,23},{8,24},{9,... | collective-permute-start | bytes 1966088 | tf_op jit(solution)/shard_map/ppermute | solution.py:610
  221.7 17.3 %collective-permute-start.40 = (bf16[2,2,2,32,1280]{4,3,0,2,1:T(8,128)(2,1)S(1)}, bf16[2,2,2,32,1280]{4,3,0,2,1:T(8,128)(2,1)S(1)}, u32[]{:S(2)}, u32[]{:S(2)}) collective-permute-start(bf16[2,2,2,32,1280]{4,3,0,2,1:T(8,128)(2,1)S(1)} %fusion.9), channel_id=1, source_target_pairs={{0,8},{1,9},{2,10},{3,11},{4,12},{5,13},{6,14},{7,15},{8,0},{9,1},... | collective-permute-start | bytes 1966088 | tf_op jit(solution)/shard_map/ppermute | solution.py:610
  223.5 16.7 %collective-permute-start.41 = (bf16[88,1024]{1,0:T(8,128)(2,1)S(1)}, bf16[88,1024]{1,0:T(8,128)(2,1)S(1)}, u32[]{:S(2)}, u32[]{:S(2)}) collective-permute-start(bf16[88,1024]{1,0:T(8,128)(2,1)S(1)} %fusion.17), channel_id=1, source_target_pairs={{0,4},{1,5},{2,6},{3,7},{4,0},{5,1},{6,2},{7,3},{8,12},{9,13},{10,... | collective-permute-start | bytes 540680 | tf_op jit(solution)/shard_map/ppermute | solution.py:610
  241.2 16.2 %collective-permute-start.44 = (bf16[2,2,32,1280]{3,2,0,1:T(8,128)(2,1)S(1)}, bf16[2,2,32,1280]{3,2,0,1:T(8,128)(2,1)S(1)}, u32[]{:S(2)}, u32[]{:S(2)}) collective-permute-start(bf16[2,2,32,1280]{3,2,0,1:T(8,128)(2,1)S(1)} %fusion.10), channel_id=1, source_target_pairs={{0,2},{1,3},{2,0},{3,1},{4,6},{5,7},{6,4},{7,5},{8,10},{9,11},{10,... | collective-permute-start | bytes 983048 | tf_op jit(solution)/shard_map/ppermute | solution.py:610
  (87 other events, 654.6 us)

commit v5 on v4

--- a/solution.py
+++ b/solution.py
@@ -12,7 +12,7 @@
 AXES = ("dp", "blk")
 epsilon = 1e-06
 score_scale = 0.125
-cost_share = 1.0
+cost_share = 3.0
 VMEM_LIMIT = 16 << 20
 bf16 = jnp.bfloat16
 f32 = jnp.float32
@@ -783,7 +783,7 @@
         q_y = flip(qys, high_e)
         dk, ds = outer(core, per_down, ([hk, h_y], [cot, cot_y]))
         blocks = grad_inputs(seqs, packed, w_qkv, x, gain_a, grad_mid, first_blocks)
-        blocks, dk, ds, bk, b_x, gb_y = tie(blocks, dk, ds, bk, b_x, gb_y)
+        blocks, dk, ds, bk, b_x, gb_y = settle((blocks, dk, ds, bk, b_x, gb_y), part_a)
         d_c = flip(ds, 0)
         moved = from_sequence(blocks)
         bk2, bs2 = outer(core, per, ([nffn, nffn_x], [bk, b_x]))
@@ -794,7 +794,7 @@
         qyk2, qys2 = outer(
             core, per, ([normed, normed_y], [qyk, q_y]), ([attended, attended_y], [gbk, gb_y])
         )
-        qyk2, qys2, b_c, moved[1::2] = settle((qyk2, qys2, b_c, moved[1::2]), part_a)
+        qyk2, qys2, b_c, moved[1::2] = tie(qyk2, qys2, b_c, moved[1::2])
         qy_c = flip(qys2, 0)
         part_b = Rows(bk2, b_c, nbits - 1, low_e)
         part_b.next()

time: 282 us -> 278 us (0.986)
  local copies, waits for them, and re-layouts: 35.4 us -> 27.7 us
  waiting for transfers between devices: 70.9 us -> 78.5 us
  starting transfers between devices: 62.9 us -> 59.1 us
    ppermute x51, waiting for transfers between devices: 70.9 us -> 78.5 us  [send(): return lax.ppermute(value, AXES, pairs)]
    unnamed x124, local copies, waits for them, and re-layouts: 32.7 us -> 25.7 us
    ppermute x51, starting transfers between devices: 62.9 us -> 59.1 us  [send(): return lax.ppermute(value, AXES, pairs)]
  transfers between devices with their start and end apart: 51 -> 51, of which waited for: 16 -> 18; matrix products, arithmetic and copies ran while one was open for 10% -> 10% of each run, Pallas kernels for 27% -> 28%
where the time goes in v5:
time: 278 us; the launch traced here: 277 us
  waiting for transfers between devices  78.5 us (28%)
  Pallas kernels  77.9 us (28%)
  starting transfers between devices  59.1 us (21%)
  other arithmetic  32.3 us (12%)
  local copies, waits for them, and re-layouts  27.7 us (10%)
    ppermute x51, waiting for transfers between devices, send(): return lax.ppermute(value, AXES, pairs)  78.5 us
    ppermute x51, starting transfers between devices, send(): return lax.ppermute(value, AXES, pairs)  59.1 us
    pallas_call x5, Pallas kernels, outer(): pl.pallas_call(functools.partial(outer_body, [len(lefts) for lefts, _ in...  28.3 us
    unnamed x124, local copies, waits for them, and re-layouts  25.7 us
    pallas_call x7, Pallas kernels, resident_call(): pl.pallas_call(body, in_specs=[scalar()] * scalars + [RESIDENT] * (len(in...  21.2 us
    convert_element_type x15, other arithmetic, go(): out = self.total([pick(v, 1 - b, axis) for v in self.terms]).astype(bf16)  17.2 us
    pallas_call x1, Pallas kernels, attend_back(): pl.pallas_call(functools.partial(attend_back_body, slots), grid=(pairs,),...  12.2 us
    pallas_call x1, Pallas kernels, attend(): pl.pallas_call(functools.partial(attend_body, slots), grid=(pairs,), in_s...  11.7 us
  transfers between devices with their start and end apart: 51, of which 18 were waited for; matrix products, arithmetic and copies ran while one was open for 10% of the time, Pallas kernels for 28%

profile of v5, /device:TPU:0, one launch (start us, length us, event | category | flops | bytes accessed | tf_op | source)
XLA Modules:
  0.0 277.1 jit_solution(1210979525881357251)
XLA Ops:
  2.8 3.1 %collective-permute-start = (bf16[136,1024]{1,0:T(8,128)(2,1)S(1)}, bf16[136,1024]{1,0:T(8,128)(2,1)S(1)}, u32[]{:S(2)}, u32[]{:S(2)}) collective-permute-start(bf16[136,1024]{1,0:T(8,128)(2,1)S(1)} %get-tuple-element.315), channel_id=1, source_target_pairs={{0,2},{1,3},{2,4},{3,5},{4,6},{5,7},{6,0},{7,1},{8,10},{9,11},{10,... | collective-permute-start | bytes 835592 | tf_op jit(solution)/shard_map/ppermute | solution.py:610
  11.7 3.9 %collective-permute-done = bf16[136,1024]{1,0:T(8,128)(2,1)S(1)} collective-permute-done((bf16[136,1024]{1,0:T(8,128)(2,1)S(1)}, bf16[136,1024]{1,0:T(8,128)(2,1)S(1)}, u32[]{:S(2)}, u32[]{:S(2)}) %collective-permute-start) | collective-permute-done | bytes 278560 | tf_op jit(solution)/shard_map/ppermute | solution.py:610
  15.6 11.1 %collective-permute-done.1 = bf16[136,1024]{1,0:T(8,128)(2,1)S(1)} collective-permute-done((bf16[136,1024]{1,0:T(8,128)(2,1)S(1)}, bf16[136,1024]{1,0:T(8,128)(2,1)S(1)}, u32[]{:S(2)}, u32[]{:S(2)}) %collective-permute-start.1) | collective-permute-done | bytes 278560 | tf_op jit(solution)/shard_map/ppermute | solution.py:610
  27.4 2.8 %copy-done = bf16[1024,3072]{1,0:T(8,128)(2,1)S(1)} copy-done((bf16[1024,3072]{1,0:T(8,128)(2,1)S(1)}, bf16[1024,3072]{1,0:T(8,128)(2,1)}, u32[]{:S(2)}) %copy-start) | copy-done | bytes 6291480
  39.3 7.5 %collective-permute-start.10 = (bf16[64,1024]{1,0:T(8,128)(2,1)S(1)}, bf16[64,1024]{1,0:T(8,128)(2,1)S(1)}, u32[]{:S(2)}, u32[]{:S(2)}) collective-permute-start(bf16[64,1024]{1,0:T(8,128)(2,1)S(1)} %get-tuple-element.317), channel_id=1, source_target_pairs={{0,6},{1,7},{2,0},{3,1},{4,2},{5,3},{6,4},{7,5},{8,14},{9,15},{10,... | collective-permute-start | bytes 393224 | tf_op jit(solution)/shard_map/ppermute | solution.py:610
  48.0 11.7 %attend.1 = (bf16[256,1024]{1,0:T(8,128)(2,1)}, f32[8,2,256]{2,1,0:T(2,128)}) custom-call(bf16[256,1024]{1,0:T(8,128)(2,1)} %copy-done.38, bf16[256,1024]{1,0:T(8,128)(2,1)} %copy-done.30, bf16[256,1024]{1,0:T(8,128)(2,1)} %collective-permute-done.3.refs_2_.refs_3_, bf16[256,1024]{1,0:T(8,128)(2,1)} %copy-done.12, ...), custom_call_target="tpu_custom_call" | custom-call | flops 3221225472 | bytes 9437184 | tf_op jit(solution)/shard_map/attend/pallas_call | solution.py:187
  73.9 7.1 %ffn_acts.1 = (bf16[256,2816]{1,0:T(8,128)(2,1)S(1)}, bf16[256,2816]{1,0:T(8,128)(2,1)S(1)}, bf16[256,2816]{1,0:T(8,128)(2,1)S(1)}, bf16[256,1408]{1,0:T(8,128)(...) custom-call(s32[2]{0:T(128)S(1)} %pad_add_fusion.2.edge_ref, ...), custom_call_target="tpu_custom_call" | custom-call | flops 13287555072 | bytes 81002520 | tf_op jit(solution)/shard_map/ffn_acts/pallas_call | solution.py:56
  85.1 6.9 %ffn_back.1 = (bf16[64,1024]{1,0:T(8,128)(2,1)S(1)}, bf16[64,1024]{1,0:T(8,128)(2,1)}, bf16[64,1024]{1,0:T(8,128)(2,1)}, bf16[64,1024]{1,0:T(8,128)(2,1)S(1)}, f...) custom-call(s32[2]{0:T(128)S(1)} %pad_add_fusion.2.edge_ref, ...), custom_call_target="tpu_custom_call" | custom-call | flops 14898167808 | bytes 83767320 | tf_op jit(solution)/shard_map/ffn_back/pallas_call | solution.py:56
  94.5 3.3 %collective-permute-start.16 = (bf16[64,1024]{1,0:T(8,128)(2,1)}, bf16[64,1024]{1,0:T(8,128)(2,1)S(1)}, u32[]{:S(2)}, u32[]{:S(2)}) collective-permute-start(bf16[64,1024]{1,0:T(8,128)(2,1)} %get-tuple-element.200), channel_id=1, source_target_pairs={{0,6},{1,7},{2,0},{3,1},{4,2},{5,3},{6,4},{7,5},{8,14},{9,15},{10,... | collective-permute-start | bytes 393224 | tf_op jit(solution)/shard_map/ppermute | solution.py:610
  100.0 12.2 %attend_back.1 = (bf16[256,1024]{1,0:T(8,128)(2,1)}, f32[256,1024]{1,0:T(8,128)}, f32[256,1024]{1,0:T(8,128)}, bf16[2,256,1024]{2,1,0:T(8,128)(2,1)}) custom-call(bf16[256,1024]{1,0:T(8,128)(2,1)} %copy-done.38, bf16[256,1024]{1,0:T(8,128)(2,1)} %copy-done.45, bf16[256,1024]{1,0:T(8,128)(2,1)} %copy-done.30, ...), custom_call_target="tpu_custom_call" | custom-call | flops 8053063680 | bytes 23592960 | tf_op jit(solution)/shard_map/attend_back/pallas_call | solution.py:254
  116.3 6.0 %outer.5 = (bf16[16,32,1536]{2,1,0:T(8,128)(2,1)}, bf16[16,32,1536]{2,1,0:T(8,128)(2,1)}) custom-call(s32[1]{0:T(128)} %bitcast.26.core_ref, bf16[256,1024]{1,0:T(8,128)(2,1)} %copy-done.29, bf16[256,1024]{1,0:T(8,128)(2,1)} %copy-done.58, bf16[256,1536]{1,0:T(8,128)(2,1)} %copy-done.43, bf16[256,1536]{1,0:T(8,128)(2,1)} %collective-permute-done.15.refs_3_), custom_call_target="tpu_custom_call" | custom-call | flops 4831838208 | bytes 17301504 | tf_op jit(solution)/shard_map/outer/pallas_call | solution.py:589
  135.9 5.3 %outer.6 = (bf16[8,88,1024]{2,1,0:T(8,128)(2,1)}, bf16[8,88,1024]{2,1,0:T(8,128)(2,1)}) custom-call(s32[1]{0:T(128)} %bitcast.26.core_ref, bf16[256,1408]{1,0:T(8,128)(2,1)} %copy-done.42, bf16[256,1408]{1,0:T(8,128)(2,1)} %copy-done.55, bf16[256,1024]{1,0:T(8,128)(2,1)} %copy-done.19, bf16[256,1024]{1,0:T(8,128)(2,1)} %copy-done.59), custom_call_target="tpu_custom_call" | custom-call | flops 4429185024 | bytes 16121856 | tf_op jit(solution)/shard_map/outer/pallas_call | solution.py:589
  141.2 8.2 %collective-permute-done.23 = bf16[2,2,2,32,1536]{4,3,0,2,1:T(8,128)(2,1)} collective-permute-done((bf16[2,2,2,32,1536]{4,3,0,2,1:T(8,128)(2,1)S(1)}, bf16[2,2,2,32,1536]{4,3,0,2,1:T(8,128)(2,1)}, u32[]{:S(2)}, u32[]{:S(2)}) %collective-permute-start.23) | collective-permute-done | bytes 786464 | tf_op jit(solution)/shard_map/ppermute | solution.py:610
  150.9 5.4 %outer.7 = (bf16[16,32,1280]{2,1,0:T(8,128)(2,1)}, bf16[16,32,1280]{2,1,0:T(8,128)(2,1)}) custom-call(s32[1]{0:T(128)} %bitcast.26.core_ref, bf16[256,1024]{1,0:T(8,128)(2,1)} %copy-done.29, bf16[256,1024]{1,0:T(8,128)(2,1)} %copy-done.58, bf16[256,1280]{1,0:T(8,128)(2,1)} %copy-done.41, bf16[256,1280]{1,0:T(8,128)(2,1)} %collective-permute-done.21.refs_3_), custom_call_target="tpu_custom_call" | custom-call | flops 4026531840 | bytes 14942208 | tf_op jit(solution)/shard_map/outer/pallas_call | solution.py:589
  156.3 4.7 %collective-permute-done.25.refs_3_ = bf16[256,768]{1,0:T(8,128)(2,1)} collective-permute-done((bf16[256,768]{1,0:T(8,128)(2,1)S(1)}, bf16[256,768]{1,0:T(8,128)(2,1)}, u32[]{:S(2)}, u32[]{:S(2)}) %collective-permute-start.25) | collective-permute-done | bytes 393248 | tf_op jit(solution)/shard_map/ppermute | solution.py:610
  161.3 3.6 %collective-permute-start.28 = (bf16[2,64,1024]{2,1,0:T(8,128)(2,1)S(1)}, bf16[2,64,1024]{2,1,0:T(8,128)(2,1)S(1)}, u32[]{:S(2)}, u32[]{:S(2)}) collective-permute-start(bf16[2,64,1024]{2,1,0:T(8,128)(2,1)S(1)} %get-tuple-element.264), channel_id=1, source_target_pairs={{0,6},{1,7},{2,0},{3,1},{4,2},{5,3},{6,4},{7,5},{8,14},{9,15},{10,... | collective-permute-start | bytes 786440 | tf_op jit(solution)/shard_map/ppermute | solution.py:610
  164.9 7.0 %outer.8 = (bf16[16,32,1280]{2,1,0:T(8,128)(2,1)}, bf16[16,32,1280]{2,1,0:T(8,128)(2,1)}) custom-call(s32[1]{0:T(128)} %bitcast.26.core_ref, bf16[256,1024]{1,0:T(8,128)(2,1)} %copy-done.11, bf16[256,1024]{1,0:T(8,128)(2,1)} %collective-permute-done.7.refs_1_, bf16[256,768]{1,0:T(8,128)(2,1)} %copy-done.32, ...), custom_call_target="tpu_custom_call" | custom-call | flops 4026531840 | bytes 18087936 | tf_op jit(solution)/shard_map/outer/pallas_call | solution.py:589
  171.9 5.5 %collective-permute-done.29.refs_3_ = bf16[2,64,1024]{2,1,0:T(8,128)(2,1)S(1)} collective-permute-done((bf16[2,64,1024]{2,1,0:T(8,128)(2,1)S(1)}, bf16[2,64,1024]{2,1,0:T(8,128)(2,1)S(1)}, u32[]{:S(2)}, u32[]{:S(2)}) %collective-permute-start.29) | collective-permute-done | bytes 262176 | tf_op jit(solution)/shard_map/ppermute | solution.py:610
  187.7 4.7 %outer.9 = (bf16[16,32,768]{2,1,0:T(8,128)(2,1)}, bf16[16,32,768]{2,1,0:T(8,128)(2,1)}) custom-call(s32[1]{0:T(128)} %bitcast.26.core_ref, bf16[256,1024]{1,0:T(8,128)(2,1)} %copy-done.11, bf16[256,1024]{1,0:T(8,128)(2,1)} %copy-done.56, bf16[256,768]{1,0:T(8,128)(2,1)} %copy-done.31, bf16[256,768]{1,0:T(8,128)(2,1)} %collective-permute-done.25.refs_3_), custom_call_target="tpu_custom_call" | custom-call | flops 2415919104 | bytes 10223616 | tf_op jit(solution)/shard_map/outer/pallas_call | solution.py:589
  192.4 7.6 %collective-permute-done.32 = bf16[2,2,32,1536]{3,2,0,1:T(8,128)(2,1)} collective-permute-done((bf16[2,2,32,1536]{3,2,0,1:T(8,128)(2,1)}, bf16[2,2,32,1536]{3,2,0,1:T(8,128)(2,1)}, u32[]{:S(2)}, u32[]{:S(2)}) %collective-permute-start.32) | collective-permute-done | bytes 393248 | tf_op jit(solution)/shard_map/ppermute | solution.py:610
  209.4 9.2 %collective-permute-done.36 = bf16[2,2,2,32,1280]{4,3,0,2,1:T(8,128)(2,1)S(1)} collective-permute-done((bf16[2,2,2,32,1280]{4,3,0,2,1:T(8,128)(2,1)S(1)}, bf16[2,2,2,32,1280]{4,3,0,2,1:T(8,128)(2,1)S(1)}, u32[]{:S(2)}, u32[]{:S(2)}) %collective-permute-start.36) | collective-permute-done | bytes 655392 | tf_op jit(solution)/shard_map/ppermute | solution.py:610
  228.6 7.4 %collective-permute-done.40 = bf16[2,2,2,32,1280]{4,3,0,2,1:T(8,128)(2,1)S(1)} collective-permute-done((bf16[2,2,2,32,1280]{4,3,0,2,1:T(8,128)(2,1)S(1)}, bf16[2,2,2,32,1280]{4,3,0,2,1:T(8,128)(2,1)S(1)}, u32[]{:S(2)}, u32[]{:S(2)}) %collective-permute-start.40) | collective-permute-done | bytes 655392 | tf_op jit(solution)/shard_map/ppermute | solution.py:610
  242.5 7.9 %collective-permute-done.43 = bf16[2,32,1280]{2,1,0:T(8,128)(2,1)S(1)} collective-permute-done((bf16[2,32,1280]{2,1,0:T(8,128)(2,1)S(1)}, bf16[2,32,1280]{2,1,0:T(8,128)(2,1)S(1)}, u32[]{:S(2)}, u32[]{:S(2)}) %collective-permute-start.43) | collective-permute-done | bytes 163872 | tf_op jit(solution)/shard_map/ppermute | solution.py:610
  250.4 4.0 %collective-permute-done.45 = bf16[2,2,32,768]{3,2,0,1:T(8,128)(2,1)S(1)} collective-permute-done((bf16[2,2,32,768]{3,2,0,1:T(8,128)(2,1)S(1)}, bf16[2,2,32,768]{3,2,0,1:T(8,128)(2,1)S(1)}, u32[]{:S(2)}, u32[]{:S(2)}) %collective-permute-start.45) | collective-permute-done | bytes 196640 | tf_op jit(solution)/shard_map/ppermute | solution.py:610
  (293 shorter events, 119.5 us)
Async XLA Ops:
  5.9 20.8 %collective-permute-start.1 = (bf16[136,1024]{1,0:T(8,128)(2,1)S(1)}, bf16[136,1024]{1,0:T(8,128)(2,1)S(1)}, u32[]{:S(2)}, u32[]{:S(2)}) collective-permute-start(bf16[136,1024]{1,0:T(8,128)(2,1)S(1)} %get-tuple-element.314), channel_id=1, source_target_pairs={{0,4},{1,5},{2,6},{3,7},{4,0},{5,1},{6,2},{7,3},{8,12},{9,13},{10,... | collective-permute-start | bytes 835592 | tf_op jit(solution)/shard_map/ppermute | solution.py:610
  8.5 18.2 %collective-permute-start.2 = (bf16[136,1024]{1,0:T(8,128)(2,1)S(1)}, bf16[136,1024]{1,0:T(8,128)(2,1)S(1)}, u32[]{:S(2)}, u32[]{:S(2)}) collective-permute-start(bf16[136,1024]{1,0:T(8,128)(2,1)S(1)} %get-tuple-element.313), channel_id=1, source_target_pairs={{0,6},{1,7},{2,0},{3,1},{4,2},{5,3},{6,4},{7,5},{8,14},{9,15},{10,... | collective-permute-start | bytes 835592 | tf_op jit(solution)/shard_map/ppermute | solution.py:610
  32.6 27.1 %collective-permute-start.6 = (bf16[256,1024]{1,0:T(8,128)(2,1)S(1)}, bf16[256,1024]{1,0:T(8,128)(2,1)S(1)}, u32[]{:S(2)}, u32[]{:S(2)}) collective-permute-start(bf16[256,1024]{1,0:T(8,128)(2,1)S(1)} %get-tuple-element.167.normed_ref.refs_0_), channel_id=1, source_target_pairs={{0,8},{1,9},{2,10},{3,11},{4,12},{5,13},{6,14},{7,15},{8,0},{9,1},... | collective-permute-start | bytes 1572872 | tf_op jit(solution)/shard_map/ppermute | solution.py:610
  34.1 25.6 %collective-permute-start.7 = (bf16[256,1024]{1,0:T(8,128)(2,1)S(1)}, bf16[256,1024]{1,0:T(8,128)(2,1)}, u32[]{:S(2)}, u32[]{:S(2)}) collective-permute-start(bf16[256,1024]{1,0:T(8,128)(2,1)S(1)} %get-tuple-element.167.normed_ref.refs_0_), channel_id=1, source_target_pairs={{0,16},{1,17},{2,18},{3,19},{4,20},{5,21},{6,22},{7,23},{8,24},{9,... | collective-permute-start | bytes 1572872 | tf_op jit(solution)/shard_map/ppermute | solution.py:610
  39.3 20.4 %collective-permute-start.10 = (bf16[64,1024]{1,0:T(8,128)(2,1)S(1)}, bf16[64,1024]{1,0:T(8,128)(2,1)S(1)}, u32[]{:S(2)}, u32[]{:S(2)}) collective-permute-start(bf16[64,1024]{1,0:T(8,128)(2,1)S(1)} %get-tuple-element.317), channel_id=1, source_target_pairs={{0,6},{1,7},{2,0},{3,1},{4,2},{5,3},{6,4},{7,5},{8,14},{9,15},{10,... | collective-permute-start | bytes 393224 | tf_op jit(solution)/shard_map/ppermute | solution.py:610
  59.8 22.9 %collective-permute-start.12 = (bf16[256,1024]{1,0:T(8,128)(2,1)S(1)}, bf16[256,1024]{1,0:T(8,128)(2,1)S(1)}, u32[]{:S(2)}, u32[]{:S(2)}) collective-permute-start(bf16[256,1024]{1,0:T(8,128)(2,1)S(1)} %constant_dynamic-update-slice_fusion.cot_ref.refs_2_), channel_id=1, source_target_pairs={{0,16},{1,17},{2,18},{3,19},{4,20},{5,21},{6,22},{7,23},{8,24},{9,... | collective-permute-start | bytes 1572872 | tf_op jit(solution)/shard_map/ppermute | solution.py:610
  60.4 24.1 %collective-permute-start.13 = (bf16[256,1024]{1,0:T(8,128)(2,1)}, bf16[256,1024]{1,0:T(8,128)(2,1)S(1)}, u32[]{:S(2)}, u32[]{:S(2)}) collective-permute-start(bf16[256,1024]{1,0:T(8,128)(2,1)} %get-tuple-element.172.att_ref.refs_4_), channel_id=1, source_target_pairs={{0,16},{1,17},{2,18},{3,19},{4,20},{5,21},{6,22},{7,23},{8,24},{9,... | collective-permute-start | bytes 1572872 | tf_op jit(solution)/shard_map/ppermute | solution.py:610
  65.4 17.4 %collective-permute-start.11 = (bf16[256,1024]{1,0:T(8,128)(2,1)S(1)}, bf16[256,1024]{1,0:T(8,128)(2,1)S(1)}, u32[]{:S(2)}, u32[]{:S(2)}) collective-permute-start(bf16[256,1024]{1,0:T(8,128)(2,1)S(1)} %get-tuple-element.173.nffn_ref.refs_0_), channel_id=1, source_target_pairs={{0,8},{1,9},{2,10},{3,11},{4,12},{5,13},{6,14},{7,15},{8,0},{9,1},... | collective-permute-start | bytes 1572872 | tf_op jit(solution)/shard_map/ppermute | solution.py:610
  84.5 30.8 %collective-permute-start.15 = (bf16[256,1536]{1,0:T(8,128)(2,1)}, bf16[256,1536]{1,0:T(8,128)(2,1)}, u32[]{:S(2)}, u32[]{:S(2)}) collective-permute-start(bf16[256,1536]{1,0:T(8,128)(2,1)} %get-tuple-element.198), channel_id=1, source_target_pairs={{0,8},{1,9},{2,10},{3,11},{4,12},{5,13},{6,14},{7,15},{8,0},{9,1},... | collective-permute-start | bytes 2359304 | tf_op jit(solution)/shard_map/ppermute | solution.py:610
  94.5 17.7 %collective-permute-start.16 = (bf16[64,1024]{1,0:T(8,128)(2,1)}, bf16[64,1024]{1,0:T(8,128)(2,1)S(1)}, u32[]{:S(2)}, u32[]{:S(2)}) collective-permute-start(bf16[64,1024]{1,0:T(8,128)(2,1)} %get-tuple-element.200), channel_id=1, source_target_pairs={{0,6},{1,7},{2,0},{3,1},{4,2},{5,3},{6,4},{7,5},{8,14},{9,15},{10,... | collective-permute-start | bytes 393224 | tf_op jit(solution)/shard_map/ppermute | solution.py:610
  99.5 15.9 %collective-permute-start.14 = (bf16[256,1408]{1,0:T(8,128)(2,1)}, bf16[256,1408]{1,0:T(8,128)(2,1)S(1)}, u32[]{:S(2)}, u32[]{:S(2)}) collective-permute-start(bf16[256,1408]{1,0:T(8,128)(2,1)} %get-tuple-element.197), channel_id=1, source_target_pairs={{0,16},{1,17},{2,18},{3,19},{4,20},{5,21},{6,22},{7,23},{8,24},{9,... | collective-permute-start | bytes 2162696 | tf_op jit(solution)/shard_map/ppermute | solution.py:610
  122.3 18.9 %collective-permute-start.21 = (bf16[256,1280]{1,0:T(8,128)(2,1)}, bf16[256,1280]{1,0:T(8,128)(2,1)}, u32[]{:S(2)}, u32[]{:S(2)}) collective-permute-start(bf16[256,1280]{1,0:T(8,128)(2,1)} %copy-done.27), channel_id=1, source_target_pairs={{0,8},{1,9},{2,10},{3,11},{4,12},{5,13},{6,14},{7,15},{8,0},{9,1},... | collective-permute-start | bytes 1966088 | tf_op jit(solution)/shard_map/ppermute | solution.py:610
  123.8 17.3 %collective-permute-start.22 = (bf16[256,512]{1,0:T(8,128)(2,1)}, bf16[256,512]{1,0:T(8,128)(2,1)}, u32[]{:S(2)}, u32[]{:S(2)}) collective-permute-start(bf16[256,512]{1,0:T(8,128)(2,1)} %copy-done.37), channel_id=1, source_target_pairs={{0,16},{1,17},{2,18},{3,19},{4,20},{5,21},{6,22},{7,23},{8,24},{9,... | collective-permute-start | bytes 786440 | tf_op jit(solution)/shard_map/ppermute | solution.py:610
  129.4 20.0 %collective-permute-start.23 = (bf16[2,2,2,32,1536]{4,3,0,2,1:T(8,128)(2,1)S(1)}, bf16[2,2,2,32,1536]{4,3,0,2,1:T(8,128)(2,1)}, u32[]{:S(2)}, u32[]{:S(2)}) collective-permute-start(bf16[2,2,2,32,1536]{4,3,0,2,1:T(8,128)(2,1)S(1)} %fusion.4), channel_id=1, source_target_pairs={{0,16},{1,17},{2,18},{3,19},{4,20},{5,21},{6,22},{7,23},{8,24},{9,... | collective-permute-start | bytes 2359304 | tf_op jit(solution)/shard_map/ppermute | solution.py:610
  161.3 16.1 %collective-permute-start.27 = (bf16[16,32,1280]{2,1,0:T(8,128)(2,1)}, bf16[16,32,1280]{2,1,0:T(8,128)(2,1)}, u32[]{:S(2)}, u32[]{:S(2)}) collective-permute-start(bf16[16,32,1280]{2,1,0:T(8,128)(2,1)} %get-tuple-element.263), channel_id=1, source_target_pairs={{0,1},{1,0},{2,3},{3,2},{4,5},{5,4},{6,7},{7,6},{8,9},{9,8},{10,11... | collective-permute-start | bytes 3932168 | tf_op jit(solution)/shard_map/ppermute | solution.py:610
  177.4 22.6 %collective-permute-start.31 = (bf16[16,32,1280]{2,1,0:T(8,128)(2,1)}, bf16[16,32,1280]{2,1,0:T(8,128)(2,1)}, u32[]{:S(2)}, u32[]{:S(2)}) collective-permute-start(bf16[16,32,1280]{2,1,0:T(8,128)(2,1)} %get-tuple-element.275), channel_id=1, source_target_pairs={{0,1},{1,0},{2,3},{3,2},{4,5},{5,4},{6,7},{7,6},{8,9},{9,8},{10,11... | collective-permute-start | bytes 3932168 | tf_op jit(solution)/shard_map/ppermute | solution.py:610
  180.0 20.0 %collective-permute-start.33 = (bf16[2,2,88,1024]{3,2,1,0:T(8,128)(2,1)}, bf16[2,2,88,1024]{3,2,1,0:T(8,128)(2,1)}, u32[]{:S(2)}, u32[]{:S(2)}) collective-permute-start(bf16[2,2,88,1024]{3,2,1,0:T(8,128)(2,1)} %fusion.6), channel_id=1, source_target_pairs={{0,8},{1,9},{2,10},{3,11},{4,12},{5,13},{6,14},{7,15},{8,0},{9,1},... | collective-permute-start | bytes 2162696 | tf_op jit(solution)/shard_map/ppermute | solution.py:610
  183.5 16.5 %collective-permute-start.32 = (bf16[2,2,32,1536]{3,2,0,1:T(8,128)(2,1)}, bf16[2,2,32,1536]{3,2,0,1:T(8,128)(2,1)}, u32[]{:S(2)}, u32[]{:S(2)}) collective-permute-start(bf16[2,2,32,1536]{3,2,0,1:T(8,128)(2,1)} %fusion.5), channel_id=1, source_target_pairs={{0,2},{1,3},{2,0},{3,1},{4,6},{5,7},{6,4},{7,5},{8,10},{9,11},{10,... | collective-permute-start | bytes 1179656 | tf_op jit(solution)/shard_map/ppermute | solution.py:610
  187.2 40.3 %collective-permute-start.30 = (bf16[2,64,1024]{2,1,0:T(8,128)(2,1)S(1)}, bf16[2,64,1024]{2,1,0:T(8,128)(2,1)S(1)}, u32[]{:S(2)}, u32[]{:S(2)}) collective-permute-start(bf16[2,64,1024]{2,1,0:T(8,128)(2,1)S(1)} %get-tuple-element.267), channel_id=1, source_target_pairs={{0,4},{1,5},{2,6},{3,7},{4,0},{5,1},{6,2},{7,3},{8,12},{9,13},{10,... | collective-permute-start | bytes 786440 | tf_op jit(solution)/shard_map/ppermute | solution.py:610
  200.0 19.2 %collective-permute-start.34 = (bf16[16,32,768]{2,1,0:T(8,128)(2,1)}, bf16[16,32,768]{2,1,0:T(8,128)(2,1)S(1)}, u32[]{:S(2)}, u32[]{:S(2)}) collective-permute-start(bf16[16,32,768]{2,1,0:T(8,128)(2,1)} %get-tuple-element.279), channel_id=1, source_target_pairs={{0,1},{1,0},{2,3},{3,2},{4,5},{5,4},{6,7},{7,6},{8,9},{9,8},{10,11... | collective-permute-start | bytes 2359304 | tf_op jit(solution)/shard_map/ppermute | solution.py:610
  201.5 17.2 %collective-permute-start.36 = (bf16[2,2,2,32,1280]{4,3,0,2,1:T(8,128)(2,1)S(1)}, bf16[2,2,2,32,1280]{4,3,0,2,1:T(8,128)(2,1)S(1)}, u32[]{:S(2)}, u32[]{:S(2)}) collective-permute-start(bf16[2,2,2,32,1280]{4,3,0,2,1:T(8,128)(2,1)S(1)} %fusion.8), channel_id=1, source_target_pairs={{0,16},{1,17},{2,18},{3,19},{4,20},{5,21},{6,22},{7,23},{8,24},{9,... | collective-permute-start | bytes 1966088 | tf_op jit(solution)/shard_map/ppermute | solution.py:610
  218.7 17.3 %collective-permute-start.40 = (bf16[2,2,2,32,1280]{4,3,0,2,1:T(8,128)(2,1)S(1)}, bf16[2,2,2,32,1280]{4,3,0,2,1:T(8,128)(2,1)S(1)}, u32[]{:S(2)}, u32[]{:S(2)}) collective-permute-start(bf16[2,2,2,32,1280]{4,3,0,2,1:T(8,128)(2,1)S(1)} %fusion.9), channel_id=1, source_target_pairs={{0,8},{1,9},{2,10},{3,11},{4,12},{5,13},{6,14},{7,15},{8,0},{9,1},... | collective-permute-start | bytes 1966088 | tf_op jit(solution)/shard_map/ppermute | solution.py:610
  220.3 16.7 %collective-permute-start.41 = (bf16[88,1024]{1,0:T(8,128)(2,1)S(1)}, bf16[88,1024]{1,0:T(8,128)(2,1)S(1)}, u32[]{:S(2)}, u32[]{:S(2)}) collective-permute-start(bf16[88,1024]{1,0:T(8,128)(2,1)S(1)} %fusion.17), channel_id=1, source_target_pairs={{0,4},{1,5},{2,6},{3,7},{4,0},{5,1},{6,2},{7,3},{8,12},{9,13},{10,... | collective-permute-start | bytes 540680 | tf_op jit(solution)/shard_map/ppermute | solution.py:610
  238.2 16.2 %collective-permute-start.44 = (bf16[2,2,32,1280]{3,2,0,1:T(8,128)(2,1)S(1)}, bf16[2,2,32,1280]{3,2,0,1:T(8,128)(2,1)S(1)}, u32[]{:S(2)}, u32[]{:S(2)}) collective-permute-start(bf16[2,2,32,1280]{3,2,0,1:T(8,128)(2,1)S(1)} %fusion.10), channel_id=1, source_target_pairs={{0,2},{1,3},{2,0},{3,1},{4,6},{5,7},{6,4},{7,5},{8,10},{9,11},{10,... | collective-permute-start | bytes 983048 | tf_op jit(solution)/shard_map/ppermute | solution.py:610
  (87 other events, 683.7 us)

commit v6 on v5

--- a/solution.py
+++ b/solution.py
@@ -12,7 +12,7 @@
 AXES = ("dp", "blk")
 epsilon = 1e-06
 score_scale = 0.125
-cost_share = 3.0
+cost_share = 2.0
 VMEM_LIMIT = 16 << 20
 bf16 = jnp.bfloat16
 f32 = jnp.float32

time: 278 us -> 282 us (1.014)
  starting transfers between devices: 59.1 us -> 62.7 us
    ppermute x51, starting transfers between devices: 59.1 us -> 62.7 us  [send(): return lax.ppermute(value, AXES, pairs)]
    unnamed x124 -> x126, local copies, waits for them, and re-layouts: 25.7 us -> 24.9 us
  transfers between devices with their start and end apart: 51 -> 51, of which waited for: 18 -> 19; matrix products, arithmetic and copies ran while one was open for 10% -> 9% of each run, Pallas kernels for 28% -> 27%
where the time goes in v6:
time: 282 us; the launch traced here: 281 us
  waiting for transfers between devices  78.7 us (28%)
  Pallas kernels  77.9 us (28%)
  starting transfers between devices  62.7 us (22%)
  other arithmetic  32.9 us (12%)
  local copies, waits for them, and re-layouts  26.9 us (10%)
    ppermute x51, waiting for transfers between devices, send(): return lax.ppermute(value, AXES, pairs)  78.7 us
    ppermute x51, starting transfers between devices, send(): return lax.ppermute(value, AXES, pairs)  62.7 us
    pallas_call x5, Pallas kernels, outer(): pl.pallas_call(functools.partial(outer_body, [len(lefts) for lefts, _ in...  28.4 us
    unnamed x126, local copies, waits for them, and re-layouts  24.9 us
    pallas_call x7, Pallas kernels, resident_call(): pl.pallas_call(body, in_specs=[scalar()] * scalars + [RESIDENT] * (len(in...  21.2 us
    convert_element_type x15, other arithmetic, go(): out = self.total([pick(v, 1 - b, axis) for v in self.terms]).astype(bf16)  17.6 us
    pallas_call x1, Pallas kernels, attend_back(): pl.pallas_call(functools.partial(attend_back_body, slots), grid=(pairs,),...  12.2 us
    pallas_call x1, Pallas kernels, attend(): pl.pallas_call(functools.partial(attend_body, slots), grid=(pairs,), in_s...  11.6 us
  transfers between devices with their start and end apart: 51, of which 19 were waited for; matrix products, arithmetic and copies ran while one was open for 9% of the time, Pallas kernels for 27%

profile of v6, /device:TPU:0, one launch (start us, length us, event | category | flops | bytes accessed | tf_op | source)
XLA Modules:
  0.0 280.7 jit_solution(12306948929401958890)
XLA Ops:
  2.8 3.1 %collective-permute-start = (bf16[136,1024]{1,0:T(8,128)(2,1)S(1)}, bf16[136,1024]{1,0:T(8,128)(2,1)S(1)}, u32[]{:S(2)}, u32[]{:S(2)}) collective-permute-start(bf16[136,1024]{1,0:T(8,128)(2,1)S(1)} %get-tuple-element.315), channel_id=1, source_target_pairs={{0,2},{1,3},{2,4},{3,5},{4,6},{5,7},{6,0},{7,1},{8,10},{9,11},{10,... | collective-permute-start | bytes 835592 | tf_op jit(solution)/shard_map/ppermute | solution.py:610
  11.7 3.9 %collective-permute-done = bf16[136,1024]{1,0:T(8,128)(2,1)S(1)} collective-permute-done((bf16[136,1024]{1,0:T(8,128)(2,1)S(1)}, bf16[136,1024]{1,0:T(8,128)(2,1)S(1)}, u32[]{:S(2)}, u32[]{:S(2)}) %collective-permute-start) | collective-permute-done | bytes 278560 | tf_op jit(solution)/shard_map/ppermute | solution.py:610
  15.6 11.1 %collective-permute-done.1 = bf16[136,1024]{1,0:T(8,128)(2,1)S(1)} collective-permute-done((bf16[136,1024]{1,0:T(8,128)(2,1)S(1)}, bf16[136,1024]{1,0:T(8,128)(2,1)S(1)}, u32[]{:S(2)}, u32[]{:S(2)}) %collective-permute-start.1) | collective-permute-done | bytes 278560 | tf_op jit(solution)/shard_map/ppermute | solution.py:610
  39.3 7.5 %collective-permute-start.10 = (bf16[64,1024]{1,0:T(8,128)(2,1)S(1)}, bf16[64,1024]{1,0:T(8,128)(2,1)S(1)}, u32[]{:S(2)}, u32[]{:S(2)}) collective-permute-start(bf16[64,1024]{1,0:T(8,128)(2,1)S(1)} %get-tuple-element.317), channel_id=1, source_target_pairs={{0,6},{1,7},{2,0},{3,1},{4,2},{5,3},{6,4},{7,5},{8,14},{9,15},{10,... | collective-permute-start | bytes 393224 | tf_op jit(solution)/shard_map/ppermute | solution.py:610
  48.1 11.6 %attend.1 = (bf16[256,1024]{1,0:T(8,128)(2,1)}, f32[8,2,256]{2,1,0:T(2,128)}) custom-call(bf16[256,1024]{1,0:T(8,128)(2,1)} %copy-done.40, bf16[256,1024]{1,0:T(8,128)(2,1)} %copy-done.31, bf16[256,1024]{1,0:T(8,128)(2,1)} %collective-permute-done.3.refs_2_.refs_3_, bf16[256,1024]{1,0:T(8,128)(2,1)} %copy-done.12, ...), custom_call_target="tpu_custom_call" | custom-call | flops 2147483648 | bytes 6291456 | tf_op jit(solution)/shard_map/attend/pallas_call | solution.py:187
  74.0 7.1 %ffn_acts.1 = (bf16[256,2816]{1,0:T(8,128)(2,1)S(1)}, bf16[256,2816]{1,0:T(8,128)(2,1)S(1)}, bf16[256,2816]{1,0:T(8,128)(2,1)S(1)}, bf16[256,1408]{1,0:T(8,128)(...) custom-call(s32[2]{0:T(128)S(1)} %pad_add_fusion.2.edge_ref, ...), custom_call_target="tpu_custom_call" | custom-call | flops 8858370048 | bytes 54001680 | tf_op jit(solution)/shard_map/ffn_acts/pallas_call | solution.py:56
  85.6 6.9 %ffn_back.1 = (bf16[64,1024]{1,0:T(8,128)(2,1)S(1)}, bf16[64,1024]{1,0:T(8,128)(2,1)}, bf16[64,1024]{1,0:T(8,128)(2,1)}, bf16[64,1024]{1,0:T(8,128)(2,1)S(1)}, f...) custom-call(s32[2]{0:T(128)S(1)} %pad_add_fusion.2.edge_ref, ...), custom_call_target="tpu_custom_call" | custom-call | flops 9932111872 | bytes 55844880 | tf_op jit(solution)/shard_map/ffn_back/pallas_call | solution.py:56
  95.1 3.3 %collective-permute-start.16 = (bf16[64,1024]{1,0:T(8,128)(2,1)}, bf16[64,1024]{1,0:T(8,128)(2,1)S(1)}, u32[]{:S(2)}, u32[]{:S(2)}) collective-permute-start(bf16[64,1024]{1,0:T(8,128)(2,1)} %get-tuple-element.200), channel_id=1, source_target_pairs={{0,6},{1,7},{2,0},{3,1},{4,2},{5,3},{6,4},{7,5},{8,14},{9,15},{10,... | collective-permute-start | bytes 393224 | tf_op jit(solution)/shard_map/ppermute | solution.py:610
  100.1 12.2 %attend_back.1 = (bf16[256,1024]{1,0:T(8,128)(2,1)}, f32[256,1024]{1,0:T(8,128)}, f32[256,1024]{1,0:T(8,128)}, bf16[2,256,1024]{2,1,0:T(8,128)(2,1)}) custom-call(bf16[256,1024]{1,0:T(8,128)(2,1)} %copy-done.40, bf16[256,1024]{1,0:T(8,128)(2,1)} %copy-done.47, bf16[256,1024]{1,0:T(8,128)(2,1)} %copy-done.31, ...), custom_call_target="tpu_custom_call" | custom-call | flops 5368709120 | bytes 15728640 | tf_op jit(solution)/shard_map/attend_back/pallas_call | solution.py:254
  114.3 5.9 %outer.5 = (bf16[16,32,1536]{2,1,0:T(8,128)(2,1)}, bf16[16,32,1536]{2,1,0:T(8,128)(2,1)}) custom-call(s32[1]{0:T(128)} %bitcast.26.core_ref, bf16[256,1024]{1,0:T(8,128)(2,1)} %copy-done.30, bf16[256,1024]{1,0:T(8,128)(2,1)} %copy-done.58, bf16[256,1536]{1,0:T(8,128)(2,1)} %copy-done.45, bf16[256,1536]{1,0:T(8,128)(2,1)} %collective-permute-done.15.refs_3_), custom_call_target="tpu_custom_call" | custom-call | flops 3221225472 | bytes 11534336 | tf_op jit(solution)/shard_map/outer/pallas_call | solution.py:589
  124.2 2.8 fusion.4
  135.4 5.4 %outer.6 = (bf16[8,88,1024]{2,1,0:T(8,128)(2,1)}, bf16[8,88,1024]{2,1,0:T(8,128)(2,1)}) custom-call(s32[1]{0:T(128)} %bitcast.26.core_ref, bf16[256,1408]{1,0:T(8,128)(2,1)} %copy-done.44, bf16[256,1408]{1,0:T(8,128)(2,1)} %collective-permute-done.14.refs_1_, bf16[256,1024]{1,0:T(8,128)(2,1)} %copy-done.19, bf16[256,1024]{1,0:T(8,128)(2,1)} %copy-done.59), custom_call_target="tpu_custom_call" | custom-call | flops 2952790016 | bytes 10747904 | tf_op jit(solution)/shard_map/outer/pallas_call | solution.py:589
  140.8 11.6 %collective-permute-done.22.refs_7_ = bf16[256,512]{1,0:T(8,128)(2,1)} collective-permute-done((bf16[256,512]{1,0:T(8,128)(2,1)S(1)}, bf16[256,512]{1,0:T(8,128)(2,1)}, u32[]{:S(2)}, u32[]{:S(2)}) %collective-permute-start.22) | collective-permute-done | bytes 262176 | tf_op jit(solution)/shard_map/ppermute | solution.py:610
  155.6 5.4 %outer.7 = (bf16[16,32,1280]{2,1,0:T(8,128)(2,1)}, bf16[16,32,1280]{2,1,0:T(8,128)(2,1)}) custom-call(s32[1]{0:T(128)} %bitcast.26.core_ref, bf16[256,1024]{1,0:T(8,128)(2,1)} %copy-done.30, bf16[256,1024]{1,0:T(8,128)(2,1)} %copy-done.58, bf16[256,1280]{1,0:T(8,128)(2,1)} %copy-done.43, bf16[256,1280]{1,0:T(8,128)(2,1)} %copy-done.55), custom_call_target="tpu_custom_call" | custom-call | flops 2684354560 | bytes 9961472 | tf_op jit(solution)/shard_map/outer/pallas_call | solution.py:589
  161.0 3.0 %collective-permute-done.25.refs_3_ = bf16[256,768]{1,0:T(8,128)(2,1)S(1)} collective-permute-done((bf16[256,768]{1,0:T(8,128)(2,1)S(1)}, bf16[256,768]{1,0:T(8,128)(2,1)S(1)}, u32[]{:S(2)}, u32[]{:S(2)}) %collective-permute-start.25) | collective-permute-done | bytes 393248 | tf_op jit(solution)/shard_map/ppermute | solution.py:610
  165.4 3.9 %collective-permute-start.28 = (bf16[2,64,1024]{2,1,0:T(8,128)(2,1)S(1)}, bf16[2,64,1024]{2,1,0:T(8,128)(2,1)S(1)}, u32[]{:S(2)}, u32[]{:S(2)}) collective-permute-start(bf16[2,64,1024]{2,1,0:T(8,128)(2,1)S(1)} %get-tuple-element.264), channel_id=1, source_target_pairs={{0,6},{1,7},{2,0},{3,1},{4,2},{5,3},{6,4},{7,5},{8,14},{9,15},{10,... | collective-permute-start | bytes 786440 | tf_op jit(solution)/shard_map/ppermute | solution.py:610
  169.2 7.0 %outer.8 = (bf16[16,32,1280]{2,1,0:T(8,128)(2,1)}, bf16[16,32,1280]{2,1,0:T(8,128)(2,1)}) custom-call(s32[1]{0:T(128)} %bitcast.26.core_ref, bf16[256,1024]{1,0:T(8,128)(2,1)} %copy-done.11, bf16[256,1024]{1,0:T(8,128)(2,1)} %collective-permute-done.7.refs_1_, bf16[256,768]{1,0:T(8,128)(2,1)} %copy-done.33, ...), custom_call_target="tpu_custom_call" | custom-call | flops 2684354560 | bytes 12058624 | tf_op jit(solution)/shard_map/outer/pallas_call | solution.py:589
  176.3 5.5 %collective-permute-done.29.refs_3_ = bf16[2,64,1024]{2,1,0:T(8,128)(2,1)S(1)} collective-permute-done((bf16[2,64,1024]{2,1,0:T(8,128)(2,1)S(1)}, bf16[2,64,1024]{2,1,0:T(8,128)(2,1)S(1)}, u32[]{:S(2)}, u32[]{:S(2)}) %collective-permute-start.29) | collective-permute-done | bytes 262176 | tf_op jit(solution)/shard_map/ppermute | solution.py:610
  191.0 4.7 %outer.9 = (bf16[16,32,768]{2,1,0:T(8,128)(2,1)}, bf16[16,32,768]{2,1,0:T(8,128)(2,1)}) custom-call(s32[1]{0:T(128)} %bitcast.26.core_ref, bf16[256,1024]{1,0:T(8,128)(2,1)} %copy-done.11, bf16[256,1024]{1,0:T(8,128)(2,1)} %copy-done.56, bf16[256,768]{1,0:T(8,128)(2,1)} %copy-done.32, bf16[256,768]{1,0:T(8,128)(2,1)} %copy-done.60), custom_call_target="tpu_custom_call" | custom-call | flops 1610612736 | bytes 6815744 | tf_op jit(solution)/shard_map/outer/pallas_call | solution.py:589
  195.6 6.9 %collective-permute-done.32 = bf16[2,2,32,1536]{3,2,0,1:T(8,128)(2,1)} collective-permute-done((bf16[2,2,32,1536]{3,2,0,1:T(8,128)(2,1)S(1)}, bf16[2,2,32,1536]{3,2,0,1:T(8,128)(2,1)}, u32[]{:S(2)}, u32[]{:S(2)}) %collective-permute-start.32) | collective-permute-done | bytes 393248 | tf_op jit(solution)/shard_map/ppermute | solution.py:610
  213.1 8.8 %collective-permute-done.36 = bf16[2,2,2,32,1280]{4,3,0,2,1:T(8,128)(2,1)S(1)} collective-permute-done((bf16[2,2,2,32,1280]{4,3,0,2,1:T(8,128)(2,1)S(1)}, bf16[2,2,2,32,1280]{4,3,0,2,1:T(8,128)(2,1)S(1)}, u32[]{:S(2)}, u32[]{:S(2)}) %collective-permute-start.36) | collective-permute-done | bytes 655392 | tf_op jit(solution)/shard_map/ppermute | solution.py:610
  232.2 7.0 %collective-permute-done.40 = bf16[2,2,2,32,1280]{4,3,0,2,1:T(8,128)(2,1)S(1)} collective-permute-done((bf16[2,2,2,32,1280]{4,3,0,2,1:T(8,128)(2,1)S(1)}, bf16[2,2,2,32,1280]{4,3,0,2,1:T(8,128)(2,1)S(1)}, u32[]{:S(2)}, u32[]{:S(2)}) %collective-permute-start.40) | collective-permute-done | bytes 655392 | tf_op jit(solution)/shard_map/ppermute | solution.py:610
  245.6 9.2 %collective-permute-done.43 = bf16[2,32,1280]{2,1,0:T(8,128)(2,1)S(1)} collective-permute-done((bf16[2,32,1280]{2,1,0:T(8,128)(2,1)S(1)}, bf16[2,32,1280]{2,1,0:T(8,128)(2,1)S(1)}, u32[]{:S(2)}, u32[]{:S(2)}) %collective-permute-start.43) | collective-permute-done | bytes 163872 | tf_op jit(solution)/shard_map/ppermute | solution.py:610
  254.8 2.8 %collective-permute-done.45 = bf16[2,2,32,768]{3,2,0,1:T(8,128)(2,1)S(1)} collective-permute-done((bf16[2,2,32,768]{3,2,0,1:T(8,128)(2,1)S(1)}, bf16[2,2,32,768]{3,2,0,1:T(8,128)(2,1)S(1)}, u32[]{:S(2)}, u32[]{:S(2)}) %collective-permute-start.45) | collective-permute-done | bytes 196640 | tf_op jit(solution)/shard_map/ppermute | solution.py:610
  (295 shorter events, 122.4 us)
Async XLA Ops:
  5.9 20.8 %collective-permute-start.1 = (bf16[136,1024]{1,0:T(8,128)(2,1)S(1)}, bf16[136,1024]{1,0:T(8,128)(2,1)S(1)}, u32[]{:S(2)}, u32[]{:S(2)}) collective-permute-start(bf16[136,1024]{1,0:T(8,128)(2,1)S(1)} %get-tuple-element.314), channel_id=1, source_target_pairs={{0,4},{1,5},{2,6},{3,7},{4,0},{5,1},{6,2},{7,3},{8,12},{9,13},{10,... | collective-permute-start | bytes 835592 | tf_op jit(solution)/shard_map/ppermute | solution.py:610
  8.5 18.2 %collective-permute-start.2 = (bf16[136,1024]{1,0:T(8,128)(2,1)S(1)}, bf16[136,1024]{1,0:T(8,128)(2,1)S(1)}, u32[]{:S(2)}, u32[]{:S(2)}) collective-permute-start(bf16[136,1024]{1,0:T(8,128)(2,1)S(1)} %get-tuple-element.313), channel_id=1, source_target_pairs={{0,6},{1,7},{2,0},{3,1},{4,2},{5,3},{6,4},{7,5},{8,14},{9,15},{10,... | collective-permute-start | bytes 835592 | tf_op jit(solution)/shard_map/ppermute | solution.py:610
  32.6 27.1 %collective-permute-start.6 = (bf16[256,1024]{1,0:T(8,128)(2,1)S(1)}, bf16[256,1024]{1,0:T(8,128)(2,1)S(1)}, u32[]{:S(2)}, u32[]{:S(2)}) collective-permute-start(bf16[256,1024]{1,0:T(8,128)(2,1)S(1)} %get-tuple-element.167.normed_ref.refs_0_), channel_id=1, source_target_pairs={{0,8},{1,9},{2,10},{3,11},{4,12},{5,13},{6,14},{7,15},{8,0},{9,1},... | collective-permute-start | bytes 1572872 | tf_op jit(solution)/shard_map/ppermute | solution.py:610
  34.1 25.7 %collective-permute-start.7 = (bf16[256,1024]{1,0:T(8,128)(2,1)S(1)}, bf16[256,1024]{1,0:T(8,128)(2,1)}, u32[]{:S(2)}, u32[]{:S(2)}) collective-permute-start(bf16[256,1024]{1,0:T(8,128)(2,1)S(1)} %get-tuple-element.167.normed_ref.refs_0_), channel_id=1, source_target_pairs={{0,16},{1,17},{2,18},{3,19},{4,20},{5,21},{6,22},{7,23},{8,24},{9,... | collective-permute-start | bytes 1572872 | tf_op jit(solution)/shard_map/ppermute | solution.py:610
  39.3 20.4 %collective-permute-start.10 = (bf16[64,1024]{1,0:T(8,128)(2,1)S(1)}, bf16[64,1024]{1,0:T(8,128)(2,1)S(1)}, u32[]{:S(2)}, u32[]{:S(2)}) collective-permute-start(bf16[64,1024]{1,0:T(8,128)(2,1)S(1)} %get-tuple-element.317), channel_id=1, source_target_pairs={{0,6},{1,7},{2,0},{3,1},{4,2},{5,3},{6,4},{7,5},{8,14},{9,15},{10,... | collective-permute-start | bytes 393224 | tf_op jit(solution)/shard_map/ppermute | solution.py:610
  59.9 22.9 %collective-permute-start.12 = (bf16[256,1024]{1,0:T(8,128)(2,1)S(1)}, bf16[256,1024]{1,0:T(8,128)(2,1)S(1)}, u32[]{:S(2)}, u32[]{:S(2)}) collective-permute-start(bf16[256,1024]{1,0:T(8,128)(2,1)S(1)} %constant_dynamic-update-slice_fusion.cot_ref.refs_2_), channel_id=1, source_target_pairs={{0,16},{1,17},{2,18},{3,19},{4,20},{5,21},{6,22},{7,23},{8,24},{9,... | collective-permute-start | bytes 1572872 | tf_op jit(solution)/shard_map/ppermute | solution.py:610
  60.4 24.1 %collective-permute-start.13 = (bf16[256,1024]{1,0:T(8,128)(2,1)}, bf16[256,1024]{1,0:T(8,128)(2,1)S(1)}, u32[]{:S(2)}, u32[]{:S(2)}) collective-permute-start(bf16[256,1024]{1,0:T(8,128)(2,1)} %get-tuple-element.172.att_ref.refs_4_), channel_id=1, source_target_pairs={{0,16},{1,17},{2,18},{3,19},{4,20},{5,21},{6,22},{7,23},{8,24},{9,... | collective-permute-start | bytes 1572872 | tf_op jit(solution)/shard_map/ppermute | solution.py:610
  65.5 17.4 %collective-permute-start.11 = (bf16[256,1024]{1,0:T(8,128)(2,1)S(1)}, bf16[256,1024]{1,0:T(8,128)(2,1)S(1)}, u32[]{:S(2)}, u32[]{:S(2)}) collective-permute-start(bf16[256,1024]{1,0:T(8,128)(2,1)S(1)} %get-tuple-element.173.nffn_ref.refs_0_), channel_id=1, source_target_pairs={{0,8},{1,9},{2,10},{3,11},{4,12},{5,13},{6,14},{7,15},{8,0},{9,1},... | collective-permute-start | bytes 1572872 | tf_op jit(solution)/shard_map/ppermute | solution.py:610
  84.6 29.7 %collective-permute-start.15 = (bf16[256,1536]{1,0:T(8,128)(2,1)}, bf16[256,1536]{1,0:T(8,128)(2,1)}, u32[]{:S(2)}, u32[]{:S(2)}) collective-permute-start(bf16[256,1536]{1,0:T(8,128)(2,1)} %get-tuple-element.198), channel_id=1, source_target_pairs={{0,8},{1,9},{2,10},{3,11},{4,12},{5,13},{6,14},{7,15},{8,0},{9,1},... | collective-permute-start | bytes 2359304 | tf_op jit(solution)/shard_map/ppermute | solution.py:610
  85.1 29.2 %collective-permute-start.14 = (bf16[256,1408]{1,0:T(8,128)(2,1)}, bf16[256,1408]{1,0:T(8,128)(2,1)}, u32[]{:S(2)}, u32[]{:S(2)}) collective-permute-start(bf16[256,1408]{1,0:T(8,128)(2,1)} %get-tuple-element.197), channel_id=1, source_target_pairs={{0,16},{1,17},{2,18},{3,19},{4,20},{5,21},{6,22},{7,23},{8,24},{9,... | collective-permute-start | bytes 2162696 | tf_op jit(solution)/shard_map/ppermute | solution.py:610
  95.1 17.2 %collective-permute-start.16 = (bf16[64,1024]{1,0:T(8,128)(2,1)}, bf16[64,1024]{1,0:T(8,128)(2,1)S(1)}, u32[]{:S(2)}, u32[]{:S(2)}) collective-permute-start(bf16[64,1024]{1,0:T(8,128)(2,1)} %get-tuple-element.200), channel_id=1, source_target_pairs={{0,6},{1,7},{2,0},{3,1},{4,2},{5,3},{6,4},{7,5},{8,14},{9,15},{10,... | collective-permute-start | bytes 393224 | tf_op jit(solution)/shard_map/ppermute | solution.py:610
  127.0 25.4 %collective-permute-start.23 = (bf16[2,2,2,32,1536]{4,3,0,2,1:T(8,128)(2,1)}, bf16[2,2,2,32,1536]{4,3,0,2,1:T(8,128)(2,1)}, u32[]{:S(2)}, u32[]{:S(2)}) collective-permute-start(bf16[2,2,2,32,1536]{4,3,0,2,1:T(8,128)(2,1)} %fusion.4), channel_id=1, source_target_pairs={{0,16},{1,17},{2,18},{3,19},{4,20},{5,21},{6,22},{7,23},{8,24},{9,... | collective-permute-start | bytes 2359304 | tf_op jit(solution)/shard_map/ppermute | solution.py:610
  128.5 23.9 %collective-permute-start.21 = (bf16[256,1280]{1,0:T(8,128)(2,1)S(1)}, bf16[256,1280]{1,0:T(8,128)(2,1)S(1)}, u32[]{:S(2)}, u32[]{:S(2)}) collective-permute-start(bf16[256,1280]{1,0:T(8,128)(2,1)S(1)} %copy-done.28), channel_id=1, source_target_pairs={{0,8},{1,9},{2,10},{3,11},{4,12},{5,13},{6,14},{7,15},{8,0},{9,1},... | collective-permute-start | bytes 1966088 | tf_op jit(solution)/shard_map/ppermute | solution.py:610
  130.0 22.4 %collective-permute-start.22 = (bf16[256,512]{1,0:T(8,128)(2,1)S(1)}, bf16[256,512]{1,0:T(8,128)(2,1)}, u32[]{:S(2)}, u32[]{:S(2)}) collective-permute-start(bf16[256,512]{1,0:T(8,128)(2,1)S(1)} %copy-done.39), channel_id=1, source_target_pairs={{0,16},{1,17},{2,18},{3,19},{4,20},{5,21},{6,22},{7,23},{8,24},{9,... | collective-permute-start | bytes 786440 | tf_op jit(solution)/shard_map/ppermute | solution.py:610
  165.4 16.4 %collective-permute-start.27 = (bf16[16,32,1280]{2,1,0:T(8,128)(2,1)}, bf16[16,32,1280]{2,1,0:T(8,128)(2,1)}, u32[]{:S(2)}, u32[]{:S(2)}) collective-permute-start(bf16[16,32,1280]{2,1,0:T(8,128)(2,1)} %get-tuple-element.263), channel_id=1, source_target_pairs={{0,1},{1,0},{2,3},{3,2},{4,5},{5,4},{6,7},{7,6},{8,9},{9,8},{10,11... | collective-permute-start | bytes 3932168 | tf_op jit(solution)/shard_map/ppermute | solution.py:610
  181.8 21.4 %collective-permute-start.31 = (bf16[16,32,1280]{2,1,0:T(8,128)(2,1)}, bf16[16,32,1280]{2,1,0:T(8,128)(2,1)}, u32[]{:S(2)}, u32[]{:S(2)}) collective-permute-start(bf16[16,32,1280]{2,1,0:T(8,128)(2,1)} %get-tuple-element.275), channel_id=1, source_target_pairs={{0,1},{1,0},{2,3},{3,2},{4,5},{5,4},{6,7},{7,6},{8,9},{9,8},{10,11... | collective-permute-start | bytes 3932168 | tf_op jit(solution)/shard_map/ppermute | solution.py:610
  184.4 18.8 %collective-permute-start.33 = (bf16[2,2,88,1024]{3,2,1,0:T(8,128)(2,1)}, bf16[2,2,88,1024]{3,2,1,0:T(8,128)(2,1)}, u32[]{:S(2)}, u32[]{:S(2)}) collective-permute-start(bf16[2,2,88,1024]{3,2,1,0:T(8,128)(2,1)} %fusion.6), channel_id=1, source_target_pairs={{0,8},{1,9},{2,10},{3,11},{4,12},{5,13},{6,14},{7,15},{8,0},{9,1},... | collective-permute-start | bytes 2162696 | tf_op jit(solution)/shard_map/ppermute | solution.py:610
  186.7 15.9 %collective-permute-start.32 = (bf16[2,2,32,1536]{3,2,0,1:T(8,128)(2,1)S(1)}, bf16[2,2,32,1536]{3,2,0,1:T(8,128)(2,1)}, u32[]{:S(2)}, u32[]{:S(2)}) collective-permute-start(bf16[2,2,32,1536]{3,2,0,1:T(8,128)(2,1)S(1)} %fusion.5), channel_id=1, source_target_pairs={{0,2},{1,3},{2,0},{3,1},{4,6},{5,7},{6,4},{7,5},{8,10},{9,11},{10,... | collective-permute-start | bytes 1179656 | tf_op jit(solution)/shard_map/ppermute | solution.py:610
  190.5 40.2 %collective-permute-start.30 = (bf16[2,64,1024]{2,1,0:T(8,128)(2,1)S(1)}, bf16[2,64,1024]{2,1,0:T(8,128)(2,1)S(1)}, u32[]{:S(2)}, u32[]{:S(2)}) collective-permute-start(bf16[2,64,1024]{2,1,0:T(8,128)(2,1)S(1)} %get-tuple-element.267), channel_id=1, source_target_pairs={{0,4},{1,5},{2,6},{3,7},{4,0},{5,1},{6,2},{7,3},{8,12},{9,13},{10,... | collective-permute-start | bytes 786440 | tf_op jit(solution)/shard_map/ppermute | solution.py:610
  203.2 19.6 %collective-permute-start.34 = (bf16[16,32,768]{2,1,0:T(8,128)(2,1)}, bf16[16,32,768]{2,1,0:T(8,128)(2,1)S(1)}, u32[]{:S(2)}, u32[]{:S(2)}) collective-permute-start(bf16[16,32,768]{2,1,0:T(8,128)(2,1)} %get-tuple-element.279), channel_id=1, source_target_pairs={{0,1},{1,0},{2,3},{3,2},{4,5},{5,4},{6,7},{7,6},{8,9},{9,8},{10,11... | collective-permute-start | bytes 2359304 | tf_op jit(solution)/shard_map/ppermute | solution.py:610
  204.7 17.2 %collective-permute-start.36 = (bf16[2,2,2,32,1280]{4,3,0,2,1:T(8,128)(2,1)S(1)}, bf16[2,2,2,32,1280]{4,3,0,2,1:T(8,128)(2,1)S(1)}, u32[]{:S(2)}, u32[]{:S(2)}) collective-permute-start(bf16[2,2,2,32,1280]{4,3,0,2,1:T(8,128)(2,1)S(1)} %fusion.8), channel_id=1, source_target_pairs={{0,16},{1,17},{2,18},{3,19},{4,20},{5,21},{6,22},{7,23},{8,24},{9,... | collective-permute-start | bytes 1966088 | tf_op jit(solution)/shard_map/ppermute | solution.py:610
  221.9 17.3 %collective-permute-start.40 = (bf16[2,2,2,32,1280]{4,3,0,2,1:T(8,128)(2,1)S(1)}, bf16[2,2,2,32,1280]{4,3,0,2,1:T(8,128)(2,1)S(1)}, u32[]{:S(2)}, u32[]{:S(2)}) collective-permute-start(bf16[2,2,2,32,1280]{4,3,0,2,1:T(8,128)(2,1)S(1)} %fusion.9), channel_id=1, source_target_pairs={{0,8},{1,9},{2,10},{3,11},{4,12},{5,13},{6,14},{7,15},{8,0},{9,1},... | collective-permute-start | bytes 1966088 | tf_op jit(solution)/shard_map/ppermute | solution.py:610
  223.9 16.3 %collective-permute-start.41 = (bf16[88,1024]{1,0:T(8,128)(2,1)S(1)}, bf16[88,1024]{1,0:T(8,128)(2,1)S(1)}, u32[]{:S(2)}, u32[]{:S(2)}) collective-permute-start(bf16[88,1024]{1,0:T(8,128)(2,1)S(1)} %fusion.17), channel_id=1, source_target_pairs={{0,4},{1,5},{2,6},{3,7},{4,0},{5,1},{6,2},{7,3},{8,12},{9,13},{10,... | collective-permute-start | bytes 540680 | tf_op jit(solution)/shard_map/ppermute | solution.py:610
  241.4 16.3 %collective-permute-start.44 = (bf16[2,2,32,1280]{3,2,0,1:T(8,128)(2,1)S(1)}, bf16[2,2,32,1280]{3,2,0,1:T(8,128)(2,1)S(1)}, u32[]{:S(2)}, u32[]{:S(2)}) collective-permute-start(bf16[2,2,32,1280]{3,2,0,1:T(8,128)(2,1)S(1)} %fusion.10), channel_id=1, source_target_pairs={{0,2},{1,3},{2,0},{3,1},{4,6},{5,7},{6,4},{7,5},{8,10},{9,11},{10,... | collective-permute-start | bytes 983048 | tf_op jit(solution)/shard_map/ppermute | solution.py:610
  (88 other events, 703.2 us)
